TPU v7x, 32 devices: a whole 2x2x4 slice. The times are simulated.
32 devices in a mesh: gx: 4 (over z), gy: 2 (over x), gz: 4 (over y, core).
Axes of the slice: x: 2, y: 2, z: 4, core: 2. Of those that a mesh axis runs over, the one named last changes fastest.
Arguments:
- density_start: float32 [64, 32, 512], P('gx', 'gy', 'gz'), may hold values from 0.7 to 1.3
- velocity_start: float32 [3, 64, 32, 512], P(None, 'gx', 'gy', 'gz'), may hold values from -0.75 to 0.75
- temp_start: float32 [64, 32, 512], P('gx', 'gy', 'gz'), may hold values from -6 to 6
- block_level: int32 [4, 2, 32], P('gx', 'gy', 'gz'), may hold values from 0 to 1
- solid_source: float32 [32, 32, 512], P('gx', 'gy', 'gz'), may hold values from -6 to 6
- ambient: float32 [32, 32, 512], P('gx', 'gy', 'gz'), may hold values from 0.5 to 2
- conduct: float32 [32, 32, 512], P('gx', 'gy', 'gz'), may hold values from 1 to 10
- pair_cell: int32 [32768], P(('gx', 'gy', 'gz')), may hold values from 0 to 32767
- pair_dest: int32 [32768, 1], P(('gx', 'gy', 'gz')), may hold values from 0 to 7; in each aligned block of 1024 rows (0 to 1023, 1024 to 2047, ...) at most 256 rows name the same one
- pair_solid: int32 [32768], P(('gx', 'gy', 'gz')), may hold values from 0 to 16383
- pair_coef: float32 [32768], P(('gx', 'gy', 'gz')), may hold values from 0.5 to 2
Outputs:
- fluid_temp: float32 [64, 32, 512], P('gx', 'gy', 'gz')
- fluid_vel: float32 [3, 64, 32, 512], P(None, 'gx', 'gy', 'gz')
- solid_temp: float32 [32, 32, 512], P('gx', 'gy', 'gz')
- wall_flux: float32 [64, 32, 512], P('gx', 'gy', 'gz')
Inputs may be any that keep to these rules, and one draw needn't show every extreme that they name: `pair_dest`: among the 1024 pairs listed on one device, at most 256 name the same solid device, and some solid device is named exactly 256 times.
All inputs are finite; a program needn't handle non-finite values.
Results may differ from a plain program's by a relative error of at most 0.0001.
Values sent between devices are 32-bit elements; how exact they have to be, the bound alone decides.
A program may use at most 64 MiB of HBM per device.

v0:
```python
import jax
import jax.numpy as jnp
from jax import lax
from jax.sharding import PartitionSpec as P

BLK = 16
ITERS = 2


velocity_set = (
    (0, 0, 0),
    (1, 0, 0),
    (-1, 0, 0),
    (0, 1, 0),
    (0, -1, 0),
    (0, 0, 1),
    (0, 0, -1),
    (1, 1, 0),
    (-1, -1, 0),
    (1, -1, 0),
    (-1, 1, 0),
    (1, 0, 1),
    (-1, 0, -1),
    (1, 0, -1),
    (-1, 0, 1),
    (0, 1, 1),
    (0, -1, -1),
    (0, 1, -1),
    (0, -1, 1),
)
weight_flow = (1.0 / 3.0,) + (1.0 / 18.0,) * 6 + (1.0 / 36.0,) * 12
weight_heat = (0.25,) + (0.125,) * 6
stacked_set = velocity_set + velocity_set[:7]


def with_halo(cells, sides, width, closed):
    for axis, dim in sides:
        count = lax.axis_size(axis)
        ends = count if closed else count - 1
        head = lax.slice_in_dim(cells, 0, width, axis=dim)
        tail = lax.slice_in_dim(cells, cells.shape[dim] - width, cells.shape[dim], axis=dim)
        cells = jnp.concatenate(
            [
                lax.ppermute(tail, axis, [(i, (i + 1) % count) for i in range(ends)]),
                cells,
                lax.ppermute(head, axis, [((i + 1) % count, i) for i in range(ends)]),
            ],
            axis=dim,
        )
    return cells


def projection(which, speed):
    along = jnp.zeros_like(speed[0])
    for dimen in range(3):
        sign = velocity_set[which][dimen]
        if sign == 1:
            along = along + speed[dimen]
        elif sign == -1:
            along = along - speed[dimen]
    return along


def moments(flow):
    density = flow[0]
    for which in range(1, 19):
        density = density + flow[which]
    speed = []
    for dimen in range(3):
        total = jnp.zeros_like(density)
        for which in range(19):
            sign = velocity_set[which][dimen]
            if sign == 1:
                total = total + flow[which]
            elif sign == -1:
                total = total - flow[which]
        speed.append(total / density)
    return (density, speed)


def flow_balance(density, speed):
    square = speed[0] * speed[0] + speed[1] * speed[1] + speed[2] * speed[2]
    rows_out = []
    for which in range(19):
        along = projection(which, speed)
        rows_out.append(
            weight_flow[which] * density * (1.0 + 3.0 * along + 4.5 * along * along - 1.5 * square)
        )
    return jnp.stack(rows_out)


def heat_balance(temper, speed):
    rows_out = []
    for which in range(7):
        along = projection(which, speed)
        rows_out.append(weight_heat[which] * temper * (1.0 + 4.0 * along))
    return jnp.stack(rows_out)


def relax(flow, heat, fine, every):
    density, speed = moments(flow)
    temper = jnp.sum(heat, axis=0)
    rate_flow = jnp.where(fine, 1.0 / 1.3, 1.0 / 0.9)
    rate_heat = jnp.where(fine, 1.0 / 1.1, 1.0 / 0.8)
    new_flow = flow - rate_flow * (flow - flow_balance(density, speed))
    new_heat = heat - rate_heat * (heat - heat_balance(temper, speed))
    if not every:
        new_flow = jnp.where(fine, new_flow, flow)
        new_heat = jnp.where(fine, new_heat, heat)
    return (new_flow, new_heat)


def stream_padded(padded, size_x, size_y, size_z):
    rows_out = []
    for which in range(26):
        off_x, off_y, off_z = stacked_set[which]
        rows_out.append(
            padded[
                which,
                1 - off_x : 1 - off_x + size_x,
                1 - off_y : 1 - off_y + size_y,
                1 - off_z : 1 - off_z + size_z,
            ]
        )
    return jnp.stack(rows_out)


def neighbours(padded):
    return (
        padded[2:, 1:-1, 1:-1],
        padded[:-2, 1:-1, 1:-1],
        padded[1:-1, 2:, 1:-1],
        padded[1:-1, :-2, 1:-1],
        padded[1:-1, 1:-1, 2:],
        padded[1:-1, 1:-1, :-2],
    )


def apply_operator(field, diagonal, weights):
    padded = with_halo(field, (("gx", 0), ("gy", 1), ("gz", 2)), 1, False)
    total = diagonal * field
    for weight, other in zip(weights, neighbours(padded)):
        total = total + weight * (field - other)
    return total


def paired_sums(residual, image):
    return lax.psum((jnp.sum(residual * residual), jnp.sum(residual * image)), ("gx", "gy", "gz"))


def per_device(
    density_start,
    velocity_start,
    temp_start,
    block_level,
    solid_source,
    ambient,
    conduct,
    pair_cell,
    pair_dest,
    pair_solid,
    pair_coef,
):
    size_x, size_y, size_z = density_start.shape
    blocks_x, blocks_y, blocks_z = block_level.shape
    fine = jnp.broadcast_to(
        (block_level == 1)[:, None, :, None, :, None], (blocks_x, BLK, blocks_y, BLK, blocks_z, BLK)
    ).reshape(size_x, size_y, size_z)
    speed0 = [velocity_start[0], velocity_start[1], velocity_start[2]]
    flow = flow_balance(density_start, speed0)
    heat = heat_balance(temp_start, speed0)
    for substep in range(2):
        flow, heat = relax(flow, heat, fine, substep == 0)
        stacked = jnp.concatenate([flow, heat], axis=0)
        padded = with_halo(stacked, (("gx", 1), ("gy", 2), ("gz", 3)), 1, True)
        moved = stream_padded(padded, size_x, size_y, size_z)
        flow = moved[:19]
        heat = moved[19:]
    density, speed = moments(flow)
    fluid_temp = jnp.sum(heat, axis=0)
    fluid_vel = jnp.stack(speed)
    groups = lax.axis_size(("gy", "gz"))
    pair_count = pair_cell.shape[0]
    capacity = 2 * pair_count // groups
    dest = pair_dest[:, 0]
    onehot = (dest[:, None] == jnp.arange(groups, dtype=jnp.int32)[None, :]).astype(jnp.int32)
    rank = jnp.sum((jnp.cumsum(onehot, axis=0) - onehot) * onehot, axis=1)
    slot = dest * capacity + rank
    temp_at = fluid_temp.reshape(-1)[pair_cell]
    payload = jnp.stack([temp_at, pair_coef, pair_solid.astype(temp_at.dtype)])
    outgoing = jnp.zeros((3, groups * capacity), temp_at.dtype).at[:, slot].set(payload)
    arrived = lax.all_to_all(
        outgoing.reshape(3, groups, capacity), ("gy", "gz"), split_axis=1, concat_axis=1, tiled=True
    )
    got_temp = arrived[0].reshape(-1)
    got_coef = arrived[1].reshape(-1)
    got_cell = arrived[2].reshape(-1).astype(jnp.int32)
    solid_shape = solid_source.shape
    solid_cells = solid_source.size
    zeros_solid = jnp.zeros((solid_cells,), solid_source.dtype)
    gain = zeros_solid.at[got_cell].add(got_coef).reshape(solid_shape)
    inflow = zeros_solid.at[got_cell].add(got_coef * got_temp).reshape(solid_shape)
    load = solid_source + inflow
    conduct_pad = with_halo(conduct, (("gx", 0), ("gy", 1), ("gz", 2)), 1, False)
    weights = [2.0 * conduct * other / (conduct + other) for other in neighbours(conduct_pad)]
    diagonal = ambient + gain
    solid_temp = jnp.zeros_like(load)
    residual = load
    image = apply_operator(residual, diagonal, weights)
    norm_now, product = paired_sums(residual, image)
    alpha = norm_now / product
    direction, along = (residual, image)
    for step in range(ITERS):
        solid_temp = solid_temp + alpha * direction
        residual = residual - alpha * along
        if step + 1 < ITERS:
            image = apply_operator(residual, diagonal, weights)
            norm_next, product = paired_sums(residual, image)
            ratio = norm_next / norm_now
            alpha = norm_next / (product - ratio * norm_next / alpha)
            direction = residual + ratio * direction
            along = image + ratio * along
            norm_now = norm_next
    wall_slots = solid_temp.reshape(-1)[got_cell].reshape(groups, capacity)
    returned = lax.all_to_all(wall_slots, ("gy", "gz"), split_axis=0, concat_axis=0, tiled=True)
    wall_at = returned.reshape(-1)[slot]
    flux = pair_coef * (wall_at - temp_at)
    wall_flux = jnp.zeros((size_x * size_y * size_z,), fluid_temp.dtype).at[pair_cell].add(flux)
    return (fluid_temp, fluid_vel, solid_temp, wall_flux.reshape(size_x, size_y, size_z))


def solution(mesh):
    return jax.shard_map(
        per_device,
        mesh=mesh,
        in_specs=(
            P("gx", "gy", "gz"),
            P(None, "gx", "gy", "gz"),
            P("gx", "gy", "gz"),
            P("gx", "gy", "gz"),
            P("gx", "gy", "gz"),
            P("gx", "gy", "gz"),
            P("gx", "gy", "gz"),
            P(("gx", "gy", "gz")),
            P(("gx", "gy", "gz"), None),
            P(("gx", "gy", "gz")),
            P(("gx", "gy", "gz")),
        ),
        out_specs=(
            P("gx", "gy", "gz"),
            P(None, "gx", "gy", "gz"),
            P("gx", "gy", "gz"),
            P("gx", "gy", "gz"),
        ),
        check_vma=False,
    )
```

profile of v0, /device:TPU:0, one launch (start us, length us, event | category | flops | bytes accessed | tf_op | source)
XLA Modules:
  0.0 403.1 jit_solution(2088430860659298116)
XLA Ops:
  0.7 2.9 constant_dynamic-update-slice_fusion.51
  8.9 1.4 copy-done.16
  17.8 1.5 copy-done.18
  19.2 1.5 multiply_subtract_fusion.1
  22.4 5.1 %collective-permute-start.1 = (f32[26,1,16,128]{3,2,1,0:T(8,128)}, f32[26,1,16,128]{3,2,1,0:T(8,128)}, u32[]{:S(2)}, u32[]{:S(2)}) collective-permute-start(f32[26,1,16,128]{3,2,1,0:T(8,128)} %get-tuple-element.104), channel_id=1, source_target_pairs={{8,0},{16,8},{24,16},{0,24},{9,1},{17,9},{25,17},{1,25},{10,2},{18... | collective-permute-start | bytes 638984 | tf_op jit(solution)/shard_map/ppermute | solution.py:46
  28.8 1.9 collective-permute-start.14
  32.6 2.3 reduce-window.6
  35.4 2.4 collective-permute-done
  37.8 1.4 pad_maximum_fusion.10
  39.3 1.6 collective-permute-start.3
  42.1 7.1 %collective-permute-done.3 = f32[26,18,1,128]{3,0,2,1:T(8,128)S(1)} collective-permute-done((f32[26,18,1,128]{3,0,2,1:T(8,128)S(1)}, f32[26,18,1,128]{3,0,2,1:T(8,128)S(1)}, u32[]{:S(2)}, u32[]{:S(2)}) %collective-permute-start.3) | collective-permute-done | bytes 239648 | tf_op jit(solution)/shard_map/ppermute | solution.py:46
  49.5 4.0 collective-permute-done.2
  53.7 3.3 pad_maximum_fusion
  57.1 6.0 %fusion.281 = (f32[26,18,18,1]{3,2,1,0:T(8,128)}, f32[26,18,18,1]{3,2,1,0:T(8,128)}) fusion(f32[26,18,18,128]{3,2,1,0:T(8,128)S(1)} %pad_maximum_fusion), kind=kLoop, calls=%fused_computation.665 | loop fusion | bytes 134784 | tf_op jit(solution)/shard_map/slice | solution.py:41
  63.1 5.2 %copy.69 = f32[26,18,18,1]{0,2,3,1:T(8,128)} copy(f32[26,18,18,1]{3,2,1,0:T(8,128)} %get-tuple-element.94) | data formatting | bytes 67392 | tf_op jit(solution)/shard_map/slice | solution.py:40
  68.3 5.2 %copy.67 = f32[26,18,18,1]{0,2,3,1:T(8,128)} copy(f32[26,18,18,1]{3,2,1,0:T(8,128)} %get-tuple-element.93) | data formatting | bytes 67392 | tf_op jit(solution)/shard_map/slice | solution.py:41
  74.6 5.3 %copy.70 = f32[26,18,18,1]{3,2,1,0:T(8,128)} copy(f32[26,18,18,1]{0,2,3,1:T(8,128)} %collective-permute-done.5) | data formatting | bytes 67392 | tf_op jit(solution)/shard_map/ppermute | solution.py:46
  79.9 5.3 %copy.68 = f32[26,18,18,1]{3,2,1,0:T(8,128)} copy(f32[26,18,18,1]{0,2,3,1:T(8,128)} %collective-permute-done.4) | data formatting | bytes 67392 | tf_op jit(solution)/shard_map/ppermute | solution.py:44
  85.2 2.7 constant_dynamic-update-slice_fusion.103
  89.1 1.7 copy-done.2
  94.9 4.0 collective-permute-start.7
  99.4 4.9 %collective-permute-done.7 = f32[26,1,16,128]{3,2,1,0:T(8,128)S(1)} collective-permute-done((f32[26,1,16,128]{3,2,1,0:T(8,128)S(1)}, f32[26,1,16,128]{3,2,1,0:T(8,128)S(1)}, u32[]{:S(2)}, u32[]{:S(2)}) %collective-permute-start.7) | collective-permute-done | bytes 213024 | tf_op jit(solution)/shard_map/ppermute | solution.py:46
  104.4 5.3 %collective-permute-done.6 = f32[26,1,16,128]{3,2,1,0:T(8,128)S(1)} collective-permute-done((f32[26,1,16,128]{3,2,1,0:T(8,128)S(1)}, f32[26,1,16,128]{3,2,1,0:T(8,128)S(1)}, u32[]{:S(2)}, u32[]{:S(2)}) %collective-permute-start.6) | collective-permute-done | bytes 213024 | tf_op jit(solution)/shard_map/ppermute | solution.py:44
  110.0 1.6 collective-permute-start.9
  113.4 6.5 %collective-permute-done.9 = f32[26,18,1,128]{3,0,2,1:T(8,128)S(1)} collective-permute-done((f32[26,18,1,128]{3,0,2,1:T(8,128)S(1)}, f32[26,18,1,128]{3,0,2,1:T(8,128)S(1)}, u32[]{:S(2)}, u32[]{:S(2)}) %collective-permute-start.9) | collective-permute-done | bytes 239648 | tf_op jit(solution)/shard_map/ppermute | solution.py:46
  120.2 5.2 %collective-permute-done.8 = f32[26,18,1,128]{3,0,2,1:T(8,128)S(1)} collective-permute-done((f32[26,18,1,128]{3,0,2,1:T(8,128)S(1)}, f32[26,18,1,128]{3,0,2,1:T(8,128)S(1)}, u32[]{:S(2)}, u32[]{:S(2)}) %collective-permute-start.8) | collective-permute-done | bytes 239648 | tf_op jit(solution)/shard_map/ppermute | solution.py:44
  125.7 2.4 pad_maximum_fusion.1
  128.1 6.0 %fusion.280 = (f32[26,18,18,1]{3,2,1,0:T(8,128)}, f32[26,18,18,1]{3,2,1,0:T(8,128)}) fusion(f32[26,18,18,128]{3,2,1,0:T(8,128)S(1)} %pad_maximum_fusion.1), kind=kLoop, calls=%fused_computation.664 | loop fusion | bytes 134784 | tf_op jit(solution)/shard_map/slice | solution.py:41
  134.2 5.2 %copy.79 = f32[26,18,18,1]{0,2,3,1:T(8,128)} copy(f32[26,18,18,1]{3,2,1,0:T(8,128)} %get-tuple-element.92) | data formatting | bytes 67392 | tf_op jit(solution)/shard_map/slice | solution.py:40
  139.4 5.2 %copy.77 = f32[26,18,18,1]{0,2,3,1:T(8,128)} copy(f32[26,18,18,1]{3,2,1,0:T(8,128)} %get-tuple-element.91) | data formatting | bytes 67392 | tf_op jit(solution)/shard_map/slice | solution.py:41
  145.0 5.3 %copy.80 = f32[26,18,18,1]{3,2,1,0:T(8,128)} copy(f32[26,18,18,1]{0,2,3,1:T(8,128)} %collective-permute-done.11) | data formatting | bytes 67392 | tf_op jit(solution)/shard_map/ppermute | solution.py:46
  150.4 5.3 %copy.78 = f32[26,18,18,1]{3,2,1,0:T(8,128)} copy(f32[26,18,18,1]{0,2,3,1:T(8,128)} %collective-permute-done.10) | data formatting | bytes 67392 | tf_op jit(solution)/shard_map/ppermute | solution.py:44
  155.7 1.3 maximum_add_fusion
  157.0 10.6 %gather_fusion = f32[1024]{0:T(1024)} fusion(f32[32768]{0:T(1024)S(1)} %bitcast.411, s32[1024]{0:T(1024)} %get-tuple-element.150), kind=kCustom, calls=%fused_computation | custom fusion | bytes 12288 | tf_op jit(solution)/shard_map/gather | solution.py:189
  167.7 1.3 maximum_bitcast_fusion
  169.0 1.7 copy.81
  170.7 4.5 %scatter_custom_fusion = f32[3,2048]{0,1:T(8,128)} fusion(s32[1024]{0:T(1024)} %bitcast.428, f32[1024,3]{1,0:T(8,128)} %copy.81, f32[]{:T(128)} %constant.27.clone.1), kind=kCustom, calls=%fused_computation.13 | custom fusion | bytes 25088 | tf_op jit(solution)/shard_map/scatter | solution.py:191
  175.2 2.2 copy.82
  177.4 3.4 all-to-all-start
  180.9 1.4 fusion.285
  182.3 4.5 %collective-permute-start.18 = (f32[10,1,128]{2,1,0:T(1,128)}, f32[10,1,128]{2,1,0:T(1,128)}, u32[]{:S(2)}, u32[]{:S(2)}) collective-permute-start(f32[10,1,128]{2,1,0:T(1,128)} %get-tuple-element.137), channel_id=1, source_target_pairs={{0,4},{1,5},{2,6},{3,7},{8,12},{9,13},{10,14},{11,15},{16,20},{17,... | collective-permute-start | bytes 15368 | tf_op jit(solution)/shard_map/ppermute | solution.py:44
  188.1 12.1 %scatter_custom_fusion.1 = f32[16384]{0:T(1024)S(1)} fusion(s32[2048]{0:T(1024)S(1)} %bitcast.420, f32[2048]{0:T(1024)S(1)} %mul.1595, f32[]{:T(128)} %constant.27.clone.1), kind=kCustom, calls=%fused_computation.644 | custom fusion | flops 2048 | bytes 65540 | tf_op jit(solution)/shard_map/scatter-add | solution.py:202
  202.5 4.6 %collective-permute-start.15 = (f32[1,16,128]{2,1,0:T(8,128)S(1)}, f32[1,16,128]{2,1,0:T(8,128)S(1)}, u32[]{:S(2)}, u32[]{:S(2)}) collective-permute-start(f32[1,16,128]{2,1,0:T(8,128)S(1)} %get-tuple-element.144), channel_id=1, source_target_pairs={{0,8},{8,16},{16,24},{1,9},{9,17},{17,25},{2,10},{10,18},{18,26},{... | collective-permute-start | bytes 24584 | tf_op jit(solution)/shard_map/ppermute | solution.py:44
  209.8 6.2 %collective-permute-start.19 = (f32[10,1,128]{2,1,0:T(1,128)S(1)}, f32[10,1,128]{2,1,0:T(1,128)S(1)}, u32[]{:S(2)}, u32[]{:S(2)}) collective-permute-start(f32[10,1,128]{2,1,0:T(1,128)S(1)} %get-tuple-element.138), channel_id=1, source_target_pairs={{0,4},{1,5},{2,6},{3,7},{8,12},{9,13},{10,14},{11,15},{16,20},{17,... | collective-permute-start | bytes 15368 | tf_op jit(solution)/shard_map/ppermute | solution.py:44
  216.8 1.4 collective-permute-start.20
  218.2 3.7 collective-permute-start.22
  222.7 3.3 collective-permute-start.23
  227.3 1.4 pad_maximum_fusion.47
  228.7 12.9 %scatter_custom_fusion.2 = f32[16384]{0:T(1024)} fusion(s32[2048]{0:T(1024)} %bitcast.421, f32[2048]{0:T(1024)} %bitcast.424, f32[]{:T(128)} %constant.27.clone.1), kind=kCustom, calls=%fused_computation.642 | custom fusion | flops 2048 | bytes 66048 | tf_op jit(solution)/shard_map/scatter-add | solution.py:201
  241.6 2.8 multiply_reduce_fusion.1
  244.4 42.4 %all-reduce.1 = (f32[]{:T(128)}, f32[]{:T(128)}) all-reduce(f32[]{:T(128)} %get-tuple-element.9, f32[]{:T(128)} %get-tuple-element.8), channel_id=1, replica_groups=mesh['gx'=4,'gy'=2,'gz'=4] {'gx','gy','gz'}, use_global_device_ids=true, to_apply=%region_6.7 | all-reduce | flops 2 | bytes 16 | tf_op jit(solution)/shard_map/psum | solution.py:148
  288.1 1.5 multiply_reduce_fusion
  290.9 4.5 %collective-permute-start.25 = (f32[1,16,128]{2,1,0:T(8,128)S(1)}, f32[1,16,128]{2,1,0:T(8,128)S(1)}, u32[]{:S(2)}, u32[]{:S(2)}) collective-permute-start(f32[1,16,128]{2,1,0:T(8,128)S(1)} %get-tuple-element.140), channel_id=1, source_target_pairs={{0,8},{8,16},{16,24},{1,9},{9,17},{17,25},{2,10},{10,18},{18,26},{... | collective-permute-start | bytes 24584 | tf_op jit(solution)/shard_map/ppermute | solution.py:44
  295.4 3.3 subtract_divide_fusion.1
  298.8 1.4 collective-permute-start.26
  300.2 4.5 %collective-permute-start.27 = (f32[10,1,128]{2,1,0:T(1,128)S(1)}, f32[10,1,128]{2,1,0:T(1,128)S(1)}, u32[]{:S(2)}, u32[]{:S(2)}) collective-permute-start(f32[10,1,128]{2,1,0:T(1,128)S(1)} %get-tuple-element.134), channel_id=1, source_target_pairs={{0,4},{1,5},{2,6},{3,7},{8,12},{9,13},{10,14},{11,15},{16,20},{17,... | collective-permute-start | bytes 15368 | tf_op jit(solution)/shard_map/ppermute | solution.py:44
  308.9 4.6 %collective-permute-done.28 = f32[10,18,1]{2,1,0:T(8,128)S(1)} collective-permute-done((f32[10,18,1]{2,1,0:T(8,128)S(1)}, f32[10,18,1]{2,1,0:T(8,128)S(1)}, u32[]{:S(2)}, u32[]{:S(2)}) %collective-permute-start.28) | collective-permute-done | bytes 752 | tf_op jit(solution)/shard_map/ppermute | solution.py:46
  313.5 1.5 fusion.215
  315.0 41.7 %all-reduce = (f32[]{:T(128)}, f32[]{:T(128)}) all-reduce(f32[]{:T(128)} %get-tuple-element.14, f32[]{:T(128)} %fusion.215), channel_id=1, replica_groups=mesh['gx'=4,'gy'=2,'gz'=4] {'gx','gy','gz'}, use_global_device_ids=true, to_apply=%region_11.12 | all-reduce | flops 2 | bytes 16 | tf_op jit(solution)/shard_map/psum | solution.py:148
  361.4 20.4 %gather_fusion.1 = f32[2048]{0:T(1024)} fusion(f32[16384]{0:T(1024)S(1)} %bitcast.410, s32[2048]{0:T(1024)S(1)} %broadcast_clamp_fusion), kind=kCustom, calls=%fused_computation.1 | custom fusion | bytes 24576 | tf_op jit(solution)/shard_map/gather | solution.py:224
  381.8 3.7 all-to-all-start.1
  386.4 3.9 all-to-all-done.1
  390.2 6.1 %gather_fusion.2 = f32[1024]{0:T(1024)S(1)} fusion(f32[2048]{0:T(1024)S(1)} %bitcast.409, s32[1024]{0:T(1024)S(1)} %copy-done.43), kind=kCustom, calls=%fused_computation.2 | custom fusion | bytes 12288 | tf_op jit(solution)/shard_map/gather | solution.py:226
  396.4 6.7 %scatter_custom_fusion.3 = f32[32768]{0:T(1024)} fusion(s32[1024]{0:T(1024)} %get-tuple-element.149, f32[1024]{0:T(1024)S(1)} %subtract_multiply_fusion.1, f32[]{:T(128)} %constant.27.clone.1), kind=kCustom, calls=%fused_computation.619 | custom fusion | flops 1024 | bytes 131584 | tf_op jit(solution)/shard_map/scatter-add | solution.py:228
  (282 shorter events, 44.6 us)
Async XLA Ops:
  5.9 5.1 %copy-start.52 = (s32[1,1,8]{2,1,0:T(1,128)S(1)}, s32[1,1,8]{2,1,0:T(1,128)}, u32[]{:S(2)}) copy-start(s32[1,1,8]{2,1,0:T(1,128)} %param.14) | copy-start | bytes 100
  11.2 9.5 %copy-start.46 = (pred[128]{0:T(512)(128)(4,1)}, pred[128]{0:T(512)(128)(4,1)S(1)}, u32[]{:S(2)}) copy-start(pred[128]{0:T(512)(128)(4,1)S(1)} %broadcast_in_dim.61) | copy-start | bytes 388
  11.2 8.0 %copy-start.22 = (f32[7,16,16,128]{3,2,1,0:T(8,128)S(1)}, f32[7,16,16,128]{3,2,1,0:T(8,128)}, u32[]{:S(2)}) copy-start(f32[7,16,16,128]{3,2,1,0:T(8,128)} %copy-done.21) | copy-start | bytes 2752516
  11.2 9.5 %copy-start.48 = (f32[128]{0:T(128)}, f32[128]{0:T(128)S(1)}, u32[]{:S(2)}) copy-start(f32[128]{0:T(128)S(1)} %get-tuple-element.152) | copy-start | bytes 1540
  11.2 9.5 %copy-start.50 = (f32[128]{0:T(128)}, f32[128]{0:T(128)S(1)}, u32[]{:S(2)}) copy-start(f32[128]{0:T(128)S(1)} %get-tuple-element.151) | copy-start | bytes 1540
  15.9 4.8 %copy-start.17 = (f32[19,16,16,128]{3,2,1,0:T(8,128)S(1)}, f32[19,16,16,128]{3,2,1,0:T(8,128)}, u32[]{:S(2)}) copy-start(f32[19,16,16,128]{3,2,1,0:T(8,128)} %copy-done.16) | copy-start | bytes 7471108
  21.6 11.1 %copy-start.34 = (s32[1024,1]{0,1:T(1,128)S(1)}, s32[1024,1]{0,1:T(1,128)}, u32[]{:S(2)}) copy-start(s32[1024,1]{0,1:T(1,128)} %param.19) | copy-start | bytes 12292
  22.4 13.1 %collective-permute-start.1 = (f32[26,1,16,128]{3,2,1,0:T(8,128)}, f32[26,1,16,128]{3,2,1,0:T(8,128)}, u32[]{:S(2)}, u32[]{:S(2)}) collective-permute-start(f32[26,1,16,128]{3,2,1,0:T(8,128)} %get-tuple-element.104), channel_id=1, source_target_pairs={{8,0},{16,8},{24,16},{0,24},{9,1},{17,9},{25,17},{1,25},{10,2},{18... | collective-permute-start | bytes 638984 | tf_op jit(solution)/shard_map/ppermute | solution.py:46
  27.4 10.4 %collective-permute-start = (f32[26,1,16,128]{3,2,1,0:T(8,128)}, f32[26,1,16,128]{3,2,1,0:T(8,128)}, u32[]{:S(2)}, u32[]{:S(2)}) collective-permute-start(f32[26,1,16,128]{3,2,1,0:T(8,128)} %get-tuple-element.103), channel_id=1, source_target_pairs={{0,8},{8,16},{16,24},{24,0},{1,9},{9,17},{17,25},{25,1},{2,10},{10... | collective-permute-start | bytes 638984 | tf_op jit(solution)/shard_map/ppermute | solution.py:44
  28.8 84.6 %collective-permute-start.14 = (f32[1,16,128]{2,1,0:T(8,128)}, f32[1,16,128]{2,1,0:T(8,128)S(1)}, u32[]{:S(2)}, u32[]{:S(2)}) collective-permute-start(f32[1,16,128]{2,1,0:T(8,128)} %get-tuple-element.143), channel_id=1, source_target_pairs={{0,8},{8,16},{16,24},{1,9},{9,17},{17,25},{2,10},{10,18},{18,26},{... | collective-permute-start | bytes 24584 | tf_op jit(solution)/shard_map/ppermute | solution.py:44
  30.7 114.4 %collective-permute-start.12 = (f32[1,16,128]{2,1,0:T(8,128)}, f32[1,16,128]{2,1,0:T(8,128)S(1)}, u32[]{:S(2)}, u32[]{:S(2)}) collective-permute-start(f32[1,16,128]{2,1,0:T(8,128)} %get-tuple-element.142), channel_id=1, source_target_pairs={{8,0},{16,8},{24,16},{9,1},{17,9},{25,17},{10,2},{18,10},{26,18},{... | collective-permute-start | bytes 24584 | tf_op jit(solution)/shard_map/ppermute | solution.py:46
  39.3 9.9 %collective-permute-start.3 = (f32[26,18,1,128]{3,0,2,1:T(8,128)S(1)}, f32[26,18,1,128]{3,0,2,1:T(8,128)S(1)}, u32[]{:S(2)}, u32[]{:S(2)}) collective-permute-start(f32[26,18,1,128]{3,0,2,1:T(8,128)S(1)} %copy.63), channel_id=1, source_target_pairs={{4,0},{0,4},{5,1},{1,5},{6,2},{2,6},{7,3},{3,7},{12,8},{8,12},{13,... | collective-permute-start | bytes 718856 | tf_op jit(solution)/shard_map/ppermute | solution.py:46
  40.9 12.6 %collective-permute-start.2 = (f32[26,18,1,128]{3,0,2,1:T(8,128)S(1)}, f32[26,18,1,128]{3,0,2,1:T(8,128)S(1)}, u32[]{:S(2)}, u32[]{:S(2)}) collective-permute-start(f32[26,18,1,128]{3,0,2,1:T(8,128)S(1)} %copy.61), channel_id=1, source_target_pairs={{0,4},{4,0},{1,5},{5,1},{2,6},{6,2},{3,7},{7,3},{8,12},{12,8},{9,1... | collective-permute-start | bytes 718856 | tf_op jit(solution)/shard_map/ppermute | solution.py:44
  49.5 7.6 %copy-start.11 = (f32[26,18,1,128]{3,2,1,0:T(1,128)}, f32[26,18,1,128]{3,2,1,0:T(1,128)S(1)}, u32[]{:S(2)}) copy-start(f32[26,18,1,128]{3,2,1,0:T(1,128)S(1)} %copy.64) | copy-start | bytes 718852
  68.3 6.3 %collective-permute-start.5 = (f32[26,18,18,1]{0,2,3,1:T(8,128)}, f32[26,18,18,1]{0,2,3,1:T(8,128)}, u32[]{:S(2)}, u32[]{:S(2)}) collective-permute-start(f32[26,18,18,1]{0,2,3,1:T(8,128)} %copy.69), channel_id=1, source_target_pairs={{1,0},{2,1},{3,2},{0,3},{5,4},{6,5},{7,6},{4,7},{9,8},{10,9},{11,1... | collective-permute-start | bytes 101096 | tf_op jit(solution)/shard_map/ppermute | solution.py:46
  73.4 6.4 %collective-permute-start.4 = (f32[26,18,18,1]{0,2,3,1:T(8,128)}, f32[26,18,18,1]{0,2,3,1:T(8,128)}, u32[]{:S(2)}, u32[]{:S(2)}) collective-permute-start(f32[26,18,18,1]{0,2,3,1:T(8,128)} %copy.67), channel_id=1, source_target_pairs={{0,1},{1,2},{2,3},{3,0},{4,5},{5,6},{6,7},{7,4},{8,9},{9,10},{10,1... | collective-permute-start | bytes 101096 | tf_op jit(solution)/shard_map/ppermute | solution.py:44
  94.9 9.5 %collective-permute-start.7 = (f32[26,1,16,128]{3,2,1,0:T(8,128)S(1)}, f32[26,1,16,128]{3,2,1,0:T(8,128)S(1)}, u32[]{:S(2)}, u32[]{:S(2)}) collective-permute-start(f32[26,1,16,128]{3,2,1,0:T(8,128)S(1)} %get-tuple-element.102), channel_id=1, source_target_pairs={{8,0},{16,8},{24,16},{0,24},{9,1},{17,9},{25,17},{1,25},{10,2},{18... | collective-permute-start | bytes 638984 | tf_op jit(solution)/shard_map/ppermute | solution.py:46
  98.8 10.8 %collective-permute-start.6 = (f32[26,1,16,128]{3,2,1,0:T(8,128)S(1)}, f32[26,1,16,128]{3,2,1,0:T(8,128)S(1)}, u32[]{:S(2)}, u32[]{:S(2)}) collective-permute-start(f32[26,1,16,128]{3,2,1,0:T(8,128)S(1)} %get-tuple-element.101), channel_id=1, source_target_pairs={{0,8},{8,16},{16,24},{24,0},{1,9},{9,17},{17,25},{25,1},{2,10},{10... | collective-permute-start | bytes 638984 | tf_op jit(solution)/shard_map/ppermute | solution.py:44
  99.4 12.8 %copy-start.41 = (s32[1024,1]{0,1:T(1,128)S(1)}, s32[1024,1]{0,1:T(1,128)}, u32[]{:S(2)}) copy-start(s32[1024,1]{0,1:T(1,128)} %compare_select_fusion.1) | copy-start | bytes 12292
  99.4 13.4 %copy-start.45 = (s32[1024]{0:T(1024)S(1)}, s32[1024]{0:T(1024)}, u32[]{:S(2)}) copy-start(s32[1024]{0:T(1024)} %param.20) | copy-start | bytes 12292
  99.4 14.0 %copy-start.25 = (f32[8,16,128]{2,1,0:T(8,128)S(1)}, f32[8,16,128]{2,1,0:T(8,128)}, u32[]{:S(2)}) copy-start(f32[8,16,128]{2,1,0:T(8,128)} %param.17) | copy-start | bytes 196612
  104.4 21.3 %copy-start.7 = (f32[26,1,16,128]{3,2,1,0:T(8,128)}, f32[26,1,16,128]{3,2,1,0:T(8,128)S(1)}, u32[]{:S(2)}) copy-start(f32[26,1,16,128]{3,2,1,0:T(8,128)S(1)} %collective-permute-done.7) | copy-start | bytes 638980
  109.6 16.1 %copy-start.8 = (f32[26,1,16,128]{3,2,1,0:T(8,128)}, f32[26,1,16,128]{3,2,1,0:T(8,128)S(1)}, u32[]{:S(2)}) copy-start(f32[26,1,16,128]{3,2,1,0:T(8,128)S(1)} %collective-permute-done.6) | copy-start | bytes 638980
  110.0 9.9 %collective-permute-start.9 = (f32[26,18,1,128]{3,0,2,1:T(8,128)S(1)}, f32[26,18,1,128]{3,0,2,1:T(8,128)S(1)}, u32[]{:S(2)}, u32[]{:S(2)}) collective-permute-start(f32[26,18,1,128]{3,0,2,1:T(8,128)S(1)} %copy.73), channel_id=1, source_target_pairs={{4,0},{0,4},{5,1},{1,5},{6,2},{2,6},{7,3},{3,7},{12,8},{8,12},{13,... | collective-permute-start | bytes 718856 | tf_op jit(solution)/shard_map/ppermute | solution.py:46
  111.6 13.8 %collective-permute-start.8 = (f32[26,18,1,128]{3,0,2,1:T(8,128)S(1)}, f32[26,18,1,128]{3,0,2,1:T(8,128)S(1)}, u32[]{:S(2)}, u32[]{:S(2)}) collective-permute-start(f32[26,18,1,128]{3,0,2,1:T(8,128)S(1)} %copy.71), channel_id=1, source_target_pairs={{0,4},{4,0},{1,5},{5,1},{2,6},{6,2},{3,7},{7,3},{8,12},{12,8},{9,1... | collective-permute-start | bytes 718856 | tf_op jit(solution)/shard_map/ppermute | solution.py:44
  120.2 7.9 %copy-start.9 = (f32[26,18,1,128]{3,2,1,0:T(1,128)}, f32[26,18,1,128]{3,2,1,0:T(1,128)S(1)}, u32[]{:S(2)}) copy-start(f32[26,18,1,128]{3,2,1,0:T(1,128)S(1)} %copy.74) | copy-start | bytes 718852
  139.4 5.7 %collective-permute-start.11 = (f32[26,18,18,1]{0,2,3,1:T(8,128)}, f32[26,18,18,1]{0,2,3,1:T(8,128)}, u32[]{:S(2)}, u32[]{:S(2)}) collective-permute-start(f32[26,18,18,1]{0,2,3,1:T(8,128)} %copy.79), channel_id=1, source_target_pairs={{1,0},{2,1},{3,2},{0,3},{5,4},{6,5},{7,6},{4,7},{9,8},{10,9},{11,1... | collective-permute-start | bytes 101096 | tf_op jit(solution)/shard_map/ppermute | solution.py:46
  144.5 5.9 %collective-permute-start.10 = (f32[26,18,18,1]{0,2,3,1:T(8,128)}, f32[26,18,18,1]{0,2,3,1:T(8,128)}, u32[]{:S(2)}, u32[]{:S(2)}) collective-permute-start(f32[26,18,18,1]{0,2,3,1:T(8,128)} %copy.77), channel_id=1, source_target_pairs={{0,1},{1,2},{2,3},{3,0},{4,5},{5,6},{6,7},{7,4},{8,9},{9,10},{10,1... | collective-permute-start | bytes 101096 | tf_op jit(solution)/shard_map/ppermute | solution.py:44
  145.0 5.3 %copy-start.23 = (f32[10,16,128]{2,1,0:T(8,128)}, f32[10,16,128]{2,1,0:T(8,128)S(1)}, u32[]{:S(2)}) copy-start(f32[10,16,128]{2,1,0:T(8,128)S(1)} %constant_dynamic-update-slice_fusion.104) | copy-start | bytes 245764
  157.0 18.2 %copy-start.1 = (f32[1,16,16,128]{3,2,1,0:T(8,128)}, f32[1,16,16,128]{3,2,1,0:T(8,128)S(1)}, u32[]{:S(2)}) copy-start(f32[1,16,16,128]{3,2,1,0:T(8,128)S(1)} %maximum_add_fusion) | copy-start | bytes 393220
  177.4 10.6 %all-to-all-start = ((f32[3,8,256]{2,0,1:T(4,128)}), f32[3,8,256]{2,0,1:T(4,128)S(1)}, u32[]{:S(2)}, u32[]{:S(2)}) async-start(f32[3,8,256]{2,0,1:T(4,128)} %copy.82), calls=%async_computation | async-start | bytes 65536 | tf_op jit(solution)/shard_map/all_to_all | solution.py:192
  182.3 24.9 %collective-permute-start.18 = (f32[10,1,128]{2,1,0:T(1,128)}, f32[10,1,128]{2,1,0:T(1,128)}, u32[]{:S(2)}, u32[]{:S(2)}) collective-permute-start(f32[10,1,128]{2,1,0:T(1,128)} %get-tuple-element.137), channel_id=1, source_target_pairs={{0,4},{1,5},{2,6},{3,7},{8,12},{9,13},{10,14},{11,15},{16,20},{17,... | collective-permute-start | bytes 15368 | tf_op jit(solution)/shard_map/ppermute | solution.py:44
  186.8 20.4 %collective-permute-start.16 = (f32[10,1,128]{2,1,0:T(1,128)}, f32[10,1,128]{2,1,0:T(1,128)}, u32[]{:S(2)}, u32[]{:S(2)}) collective-permute-start(f32[10,1,128]{2,1,0:T(1,128)} %get-tuple-element.136), channel_id=1, source_target_pairs={{4,0},{5,1},{6,2},{7,3},{12,8},{13,9},{14,10},{15,11},{20,16},{21,... | collective-permute-start | bytes 15368 | tf_op jit(solution)/shard_map/ppermute | solution.py:46
  188.1 12.2 %copy-start.38 = (f32[1,8,256]{2,0,1:T(1,128)}, f32[1,8,256]{2,0,1:T(1,128)S(1)}, u32[]{:S(2)}) copy-start(f32[1,8,256]{2,0,1:T(1,128)S(1)} %get-tuple-element.147) | copy-start | bytes 24580
  188.1 12.2 %copy-start.36 = (s32[2048,1]{0,1:T(1,128)}, s32[2048,1]{0,1:T(1,128)S(1)}, u32[]{:S(2)}) copy-start(s32[2048,1]{0,1:T(1,128)S(1)} %compare_select_fusion) | copy-start | bytes 24580
  201.2 6.9 %collective-permute-start.13 = (f32[1,16,128]{2,1,0:T(8,128)S(1)}, f32[1,16,128]{2,1,0:T(8,128)S(1)}, u32[]{:S(2)}, u32[]{:S(2)}) collective-permute-start(f32[1,16,128]{2,1,0:T(8,128)S(1)} %get-tuple-element.145), channel_id=1, source_target_pairs={{8,0},{16,8},{24,16},{9,1},{17,9},{25,17},{10,2},{18,10},{26,18},{... | collective-permute-start | bytes 24584 | tf_op jit(solution)/shard_map/ppermute | solution.py:46
  202.5 6.0 %collective-permute-start.15 = (f32[1,16,128]{2,1,0:T(8,128)S(1)}, f32[1,16,128]{2,1,0:T(8,128)S(1)}, u32[]{:S(2)}, u32[]{:S(2)}) collective-permute-start(f32[1,16,128]{2,1,0:T(8,128)S(1)} %get-tuple-element.144), channel_id=1, source_target_pairs={{0,8},{8,16},{16,24},{1,9},{9,17},{17,25},{2,10},{10,18},{18,26},{... | collective-permute-start | bytes 24584 | tf_op jit(solution)/shard_map/ppermute | solution.py:44
  208.1 14.6 %copy-start.32 = (f32[1,16,128]{2,1,0:T(8,128)}, f32[1,16,128]{2,1,0:T(8,128)S(1)}, u32[]{:S(2)}) copy-start(f32[1,16,128]{2,1,0:T(8,128)S(1)} %collective-permute-done.13) | copy-start | bytes 24580
  208.5 14.2 %copy-start.33 = (f32[1,16,128]{2,1,0:T(8,128)}, f32[1,16,128]{2,1,0:T(8,128)S(1)}, u32[]{:S(2)}) copy-start(f32[1,16,128]{2,1,0:T(8,128)S(1)} %collective-permute-done.15) | copy-start | bytes 24580
  208.5 13.4 %collective-permute-start.17 = (f32[10,1,128]{2,1,0:T(1,128)S(1)}, f32[10,1,128]{2,1,0:T(1,128)S(1)}, u32[]{:S(2)}, u32[]{:S(2)}) collective-permute-start(f32[10,1,128]{2,1,0:T(1,128)S(1)} %get-tuple-element.139), channel_id=1, source_target_pairs={{4,0},{5,1},{6,2},{7,3},{12,8},{13,9},{14,10},{15,11},{20,16},{21,... | collective-permute-start | bytes 15368 | tf_op jit(solution)/shard_map/ppermute | solution.py:46
  209.8 12.1 %collective-permute-start.19 = (f32[10,1,128]{2,1,0:T(1,128)S(1)}, f32[10,1,128]{2,1,0:T(1,128)S(1)}, u32[]{:S(2)}, u32[]{:S(2)}) collective-permute-start(f32[10,1,128]{2,1,0:T(1,128)S(1)} %get-tuple-element.138), channel_id=1, source_target_pairs={{0,4},{1,5},{2,6},{3,7},{8,12},{9,13},{10,14},{11,15},{16,20},{17,... | collective-permute-start | bytes 15368 | tf_op jit(solution)/shard_map/ppermute | solution.py:44
  216.8 24.8 %copy-start.26 = (f32[8,16,128]{2,1,0:T(8,128)S(1)}, f32[8,16,128]{2,1,0:T(8,128)}, u32[]{:S(2)}) copy-start(f32[8,16,128]{2,1,0:T(8,128)} %param.17) | copy-start | bytes 196612
  216.8 24.8 %collective-permute-start.20 = (f32[10,18,1]{2,1,0:T(8,128)}, f32[10,18,1]{2,1,0:T(8,128)}, u32[]{:S(2)}, u32[]{:S(2)}) collective-permute-start(f32[10,18,1]{2,1,0:T(8,128)} %get-tuple-element.131), channel_id=1, source_target_pairs={{1,0},{2,1},{3,2},{5,4},{6,5},{7,6},{9,8},{10,9},{11,10},{13,12},{... | collective-permute-start | bytes 2168 | tf_op jit(solution)/shard_map/ppermute | solution.py:46
  218.2 23.4 %collective-permute-start.22 = (f32[10,18,1]{2,1,0:T(8,128)}, f32[10,18,1]{2,1,0:T(8,128)}, u32[]{:S(2)}, u32[]{:S(2)}) collective-permute-start(f32[10,18,1]{2,1,0:T(8,128)} %get-tuple-element.130), channel_id=1, source_target_pairs={{0,1},{1,2},{2,3},{4,5},{5,6},{6,7},{8,9},{9,10},{10,11},{12,13},{... | collective-permute-start | bytes 2168 | tf_op jit(solution)/shard_map/ppermute | solution.py:44
  222.7 18.9 %collective-permute-start.23 = (f32[10,18,1]{2,1,0:T(8,128)}, f32[10,18,1]{2,1,0:T(8,128)}, u32[]{:S(2)}, u32[]{:S(2)}) collective-permute-start(f32[10,18,1]{2,1,0:T(8,128)} %get-tuple-element.133), channel_id=1, source_target_pairs={{0,1},{1,2},{2,3},{4,5},{5,6},{6,7},{8,9},{9,10},{10,11},{12,13},{... | collective-permute-start | bytes 2168 | tf_op jit(solution)/shard_map/ppermute | solution.py:44
  226.0 15.6 %collective-permute-start.21 = (f32[10,18,1]{2,1,0:T(8,128)}, f32[10,18,1]{2,1,0:T(8,128)}, u32[]{:S(2)}, u32[]{:S(2)}) collective-permute-start(f32[10,18,1]{2,1,0:T(8,128)} %get-tuple-element.132), channel_id=1, source_target_pairs={{1,0},{2,1},{3,2},{5,4},{6,5},{7,6},{9,8},{10,9},{11,10},{13,12},{... | collective-permute-start | bytes 2168 | tf_op jit(solution)/shard_map/ppermute | solution.py:46
  289.6 9.2 %collective-permute-start.24 = (f32[1,16,128]{2,1,0:T(8,128)S(1)}, f32[1,16,128]{2,1,0:T(8,128)S(1)}, u32[]{:S(2)}, u32[]{:S(2)}) collective-permute-start(f32[1,16,128]{2,1,0:T(8,128)S(1)} %get-tuple-element.141), channel_id=1, source_target_pairs={{8,0},{16,8},{24,16},{9,1},{17,9},{25,17},{10,2},{18,10},{26,18},{... | collective-permute-start | bytes 24584 | tf_op jit(solution)/shard_map/ppermute | solution.py:46
  290.9 7.9 %collective-permute-start.25 = (f32[1,16,128]{2,1,0:T(8,128)S(1)}, f32[1,16,128]{2,1,0:T(8,128)S(1)}, u32[]{:S(2)}, u32[]{:S(2)}) collective-permute-start(f32[1,16,128]{2,1,0:T(8,128)S(1)} %get-tuple-element.140), channel_id=1, source_target_pairs={{0,8},{8,16},{16,24},{1,9},{9,17},{17,25},{2,10},{10,18},{18,26},{... | collective-permute-start | bytes 24584 | tf_op jit(solution)/shard_map/ppermute | solution.py:44
  298.7 10.1 %copy-start.37 = (s32[2048,1]{0,1:T(1,128)S(1)}, s32[2048,1]{0,1:T(1,128)}, u32[]{:S(2)}) copy-start(s32[2048,1]{0,1:T(1,128)} %copy-done.36) | copy-start | bytes 24580
  298.7 14.8 %copy-start.24 = (f32[10,16,128]{2,1,0:T(8,128)S(1)}, f32[10,16,128]{2,1,0:T(8,128)}, u32[]{:S(2)}) copy-start(f32[10,16,128]{2,1,0:T(8,128)} %copy-done.23) | copy-start | bytes 245764
  298.7 14.8 %copy-start.27 = (f32[8,16,128]{2,1,0:T(8,128)S(1)}, f32[8,16,128]{2,1,0:T(8,128)}, u32[]{:S(2)}) copy-start(f32[8,16,128]{2,1,0:T(8,128)} %param.17) | copy-start | bytes 196612
  298.7 14.8 %copy-start.29 = (f32[8,16,128]{2,1,0:T(8,128)S(1)}, f32[8,16,128]{2,1,0:T(8,128)}, u32[]{:S(2)}) copy-start(f32[8,16,128]{2,1,0:T(8,128)} %get-tuple-element.17) | copy-start | bytes 196612
  298.7 14.8 %copy-start.30 = (f32[8,16,128]{2,1,0:T(8,128)S(1)}, f32[8,16,128]{2,1,0:T(8,128)}, u32[]{:S(2)}) copy-start(f32[8,16,128]{2,1,0:T(8,128)} %get-tuple-element.18) | copy-start | bytes 196612
  298.8 14.8 %copy-start.31 = (f32[8,16,128]{2,1,0:T(8,128)S(1)}, f32[8,16,128]{2,1,0:T(8,128)}, u32[]{:S(2)}) copy-start(f32[8,16,128]{2,1,0:T(8,128)} %get-tuple-element.19) | copy-start | bytes 196612
  298.8 6.1 %collective-permute-start.26 = (f32[10,1,128]{2,1,0:T(1,128)S(1)}, f32[10,1,128]{2,1,0:T(1,128)S(1)}, u32[]{:S(2)}, u32[]{:S(2)}) collective-permute-start(f32[10,1,128]{2,1,0:T(1,128)S(1)} %get-tuple-element.135), channel_id=1, source_target_pairs={{4,0},{5,1},{6,2},{7,3},{12,8},{13,9},{14,10},{15,11},{20,16},{21,... | collective-permute-start | bytes 15368 | tf_op jit(solution)/shard_map/ppermute | solution.py:46
  300.2 5.9 %collective-permute-start.27 = (f32[10,1,128]{2,1,0:T(1,128)S(1)}, f32[10,1,128]{2,1,0:T(1,128)S(1)}, u32[]{:S(2)}, u32[]{:S(2)}) collective-permute-start(f32[10,1,128]{2,1,0:T(1,128)S(1)} %get-tuple-element.134), channel_id=1, source_target_pairs={{0,4},{1,5},{2,6},{3,7},{8,12},{9,13},{10,14},{11,15},{16,20},{17,... | collective-permute-start | bytes 15368 | tf_op jit(solution)/shard_map/ppermute | solution.py:44
  306.2 2.6 collective-permute-start.29
  307.5 6.0 %collective-permute-start.28 = (f32[10,18,1]{2,1,0:T(8,128)S(1)}, f32[10,18,1]{2,1,0:T(8,128)S(1)}, u32[]{:S(2)}, u32[]{:S(2)}) collective-permute-start(f32[10,18,1]{2,1,0:T(8,128)S(1)} %get-tuple-element.128), channel_id=1, source_target_pairs={{1,0},{2,1},{3,2},{5,4},{6,5},{7,6},{9,8},{10,9},{11,10},{13,12},{... | collective-permute-start | bytes 2168 | tf_op jit(solution)/shard_map/ppermute | solution.py:46
  361.3 20.5 %copy-start = (f32[8,16,128]{2,1,0:T(8,128)}, f32[8,16,128]{2,1,0:T(8,128)S(1)}, u32[]{:S(2)}) copy-start(f32[8,16,128]{2,1,0:T(8,128)S(1)} %multiply_add_fusion) | copy-start | bytes 196612
  361.4 24.2 %copy-start.28 = (f32[1,16,16,128]{3,2,1,0:T(8,128)S(1)}, f32[1,16,16,128]{3,2,1,0:T(8,128)}, u32[]{:S(2)}) copy-start(f32[1,16,16,128]{3,2,1,0:T(8,128)} %get-tuple-element.20) | copy-start | bytes 393220
  361.4 28.9 %copy-start.43 = (s32[1024]{0:T(1024)S(1)}, s32[1024]{0:T(1024)}, u32[]{:S(2)}) copy-start(s32[1024]{0:T(1024)} %broadcast_clamp_fusion.1) | copy-start | bytes 12292
  381.8 8.4 %all-to-all-start.1 = ((f32[8,1,256]{2,1,0:T(1,128)}), f32[8,1,256]{2,1,0:T(1,128)S(1)}, u32[]{:S(2)}, u32[]{:S(2)}) async-start(f32[8,1,256]{2,1,0:T(1,128)} %bitcast.75), calls=%async_computation.1 | async-start | bytes 16384 | tf_op jit(solution)/shard_map/all_to_all | solution.py:225
  385.6 10.8 %copy-start.35 = (f32[1024]{0:T(1024)S(1)}, f32[1024]{0:T(1024)}, u32[]{:S(2)}) copy-start(f32[1024]{0:T(1024)} %gather_fusion) | copy-start | bytes 12292
  385.6 10.8 %copy-start.42 = (f32[1024]{0:T(1024)S(1)}, f32[1024]{0:T(1024)}, u32[]{:S(2)}) copy-start(f32[1024]{0:T(1024)} %param.21) | copy-start | bytes 12292
  (21 other events, 49.1 us)
where the time goes:
time: 405 us; the launch traced here: 403 us
  local copies, waits for them, and re-layouts  121 us (30%)
  blocking collectives  84.1 us (21%)
  other arithmetic  76.8 us (19%)
  starting transfers between devices  68 us (17%)
  waiting for transfers between devices  45.5 us (11%)
  between operations  8.04 us (2%)
    psum x2, blocking collectives, paired_sums(): lax.psum((jnp.sum(residual * residual), jnp.sum(residual * image)), ('gx'...  84.1 us
    ppermute x15, starting transfers between devices, with_halo(): lax.ppermute(tail, axis, [(i, (i + 1) % count) for i in range(ends)])  36.9 us
    ppermute x15, starting transfers between devices, with_halo(): lax.ppermute(head, axis, [((i + 1) % count, i) for i in range(ends)])  24 us
    slice x9, local copies, waits for them, and re-layouts, with_halo(): lax.slice_in_dim(cells, cells.shape[dim] - width, cells.shape[dim], axis=...  23.2 us
    ppermute x15, waiting for transfers between devices, with_halo(): lax.ppermute(head, axis, [((i + 1) % count, i) for i in range(ends)])  23.2 us
    gather x1, local copies, waits for them, and re-layouts, per_device(): wall_slots = solid_temp.reshape(-1)[got_cell].reshape(groups, capacity)  20.4 us
    ppermute x15, waiting for transfers between devices, with_halo(): lax.ppermute(tail, axis, [(i, (i + 1) % count) for i in range(ends)])  18.4 us
    unnamed x143, local copies, waits for them, and re-layouts  15.1 us
  transfers between devices with their start and end apart: 32, of which 11 were waited for; matrix products, arithmetic and copies ran while one was open for 26% of the time, Pallas kernels for 0%

commit v1 on v0

v1 whole, which is shorter than its diff:
```python
import functools

import jax
import jax.numpy as jnp
from jax import lax
from jax.experimental import pallas as pl
from jax.experimental.pallas import tpu as pltpu
from jax.sharding import PartitionSpec as P

BLK = 16
ITERS = 2


velocity_set = (
    (0, 0, 0),
    (1, 0, 0),
    (-1, 0, 0),
    (0, 1, 0),
    (0, -1, 0),
    (0, 0, 1),
    (0, 0, -1),
    (1, 1, 0),
    (-1, -1, 0),
    (1, -1, 0),
    (-1, 1, 0),
    (1, 0, 1),
    (-1, 0, -1),
    (1, 0, -1),
    (-1, 0, 1),
    (0, 1, 1),
    (0, -1, -1),
    (0, 1, -1),
    (0, -1, 1),
)
weight_flow = (1.0 / 3.0,) + (1.0 / 18.0,) * 6 + (1.0 / 36.0,) * 12
weight_heat = (0.25,) + (0.125,) * 6
stacked_set = velocity_set + velocity_set[:7]


def with_halo(cells, sides, width, closed):
    for axis, dim in sides:
        count = lax.axis_size(axis)
        ends = count if closed else count - 1
        head = lax.slice_in_dim(cells, 0, width, axis=dim)
        tail = lax.slice_in_dim(cells, cells.shape[dim] - width, cells.shape[dim], axis=dim)
        cells = jnp.concatenate(
            [
                lax.ppermute(tail, axis, [(i, (i + 1) % count) for i in range(ends)]),
                cells,
                lax.ppermute(head, axis, [((i + 1) % count, i) for i in range(ends)]),
            ],
            axis=dim,
        )
    return cells

AXES = ("gx", "gy", "gz")
HALO = 2
VMEM = pltpu.VMEM


def ring_halo(cells, axis, dim, total):
    count = lax.axis_size(axis)
    size = cells.shape[dim]
    head = lax.slice_in_dim(cells, 0, HALO, axis=dim)
    tail = lax.slice_in_dim(cells, size - HALO, size, axis=dim)
    after = lax.ppermute(head, axis, [((i + 1) % count, i) for i in range(count)])
    before = lax.ppermute(tail, axis, [(i, (i + 1) % count) for i in range(count)])
    gap = list(cells.shape)
    gap[dim] = total - size - 2 * HALO
    return jnp.concatenate([cells, after, jnp.ones(gap, cells.dtype), before], axis=dim)


def along_of(which, speed):
    along = None
    for dimen in range(3):
        sign = velocity_set[which][dimen]
        if sign == 1:
            along = speed[dimen] if along is None else along + speed[dimen]
        elif sign == -1:
            along = -speed[dimen] if along is None else along - speed[dimen]
    return along


def equilibrium(density, speed):
    square = 1.0 - 1.5 * (speed[0] * speed[0] + speed[1] * speed[1] + speed[2] * speed[2])
    weighted = {w: w * density for w in set(weight_flow)}
    rows_out = [weighted[weight_flow[0]] * square]
    for which in range(1, 19, 2):
        along = along_of(which, speed)
        rho = weighted[weight_flow[which]]
        even = rho * (square + 4.5 * along * along)
        odd = rho * (3.0 * along)
        rows_out += [even + odd, even - odd]
    return rows_out


def heat_equilibrium(temper, speed):
    rows_out = [weight_heat[0] * temper]
    for which in range(1, 7, 2):
        even = weight_heat[which] * temper
        odd = even * (4.0 * along_of(which, speed))
        rows_out += [even + odd, even - odd]
    return rows_out


def flow_moments(flow):
    density = flow[0]
    for which in range(1, 19):
        density = density + flow[which]
    inverse = 1.0 / density
    speed = []
    for dimen in range(3):
        total = None
        for which in range(19):
            sign = velocity_set[which][dimen]
            if sign == 1:
                total = flow[which] if total is None else total + flow[which]
            elif sign == -1:
                total = total - flow[which]
        speed.append(total * inverse)
    return density, speed


def collide(flow, heat, rate_flow, rate_heat):
    density, speed = flow_moments(flow)
    temper = functools.reduce(lambda a, b: a + b, heat)
    flow = [f - rate_flow * (f - e) for f, e in zip(flow, equilibrium(density, speed))]
    heat = [g - rate_heat * (g - e) for g, e in zip(heat, heat_equilibrium(temper, speed))]
    return flow, heat


def stream_plane(store, plane, values):
    height, width = values[0].shape
    for which, value in enumerate(values):
        off_x, off_y, off_z = stacked_set[which]
        if off_y:
            value = pltpu.roll(value, off_y % height, 0)
        if off_z:
            value = pltpu.roll(value, off_z % width, 1)
        store[which, plane + off_x + 1] = value


def fluid_kernel(fields, temp_out, vel_out, first, second):
    planes = fields.shape[1]
    size_x, size_y, size_z = temp_out.shape

    def one(plane, carry):
        density = fields[0, plane]
        speed = [fields[1, plane], fields[2, plane], fields[3, plane]]
        fine = fields[5, plane] == 1.0
        flow, heat = collide(
            equilibrium(density, speed),
            heat_equilibrium(fields[4, plane], speed),
            jnp.where(fine, 1.0 / 1.3, 1.0 / 0.9),
            jnp.where(fine, 1.0 / 1.1, 1.0 / 0.8),
        )
        stream_plane(first, plane, flow + heat)
        return carry

    def two(plane, carry):
        fine = fields[5, plane] == 1.0
        values = [first[which, plane + 1] for which in range(26)]
        flow, heat = collide(
            values[:19], values[19:], jnp.where(fine, 1.0 / 1.3, 0.0), jnp.where(fine, 1.0 / 1.1, 0.0)
        )
        stream_plane(second, plane, flow + heat)
        return carry

    def three(row, carry):
        plane = row + HALO + 1
        values = [second[which, plane, :size_y, :size_z] for which in range(26)]
        density, speed = flow_moments(values[:19])
        temp_out[row] = functools.reduce(lambda a, b: a + b, values[19:])
        for dimen in range(3):
            vel_out[dimen, row] = speed[dimen]
        return carry

    lax.fori_loop(0, planes, one, 0)
    lax.fori_loop(1, planes - 1, two, 0)
    lax.fori_loop(0, size_x, three, 0)


def run_fluid(fields, shape):
    planes, height, width = fields.shape[1:]
    whole = pl.BlockSpec(memory_space=VMEM)
    return pl.pallas_call(
        fluid_kernel,
        out_shape=(jax.ShapeDtypeStruct(shape, jnp.float32), jax.ShapeDtypeStruct((3,) + shape, jnp.float32)),
        in_specs=[whole],
        out_specs=(whole, whole),
        scratch_shapes=[VMEM((26, planes + 2, height, width), jnp.float32)] * 2,
        compiler_params=pltpu.CompilerParams(vmem_limit_bytes=52 * 1024 * 1024),
        name="fluid",
    )(fields)


def thirds(value):
    high = value.astype(jnp.bfloat16)
    rest = value - high.astype(jnp.float32)
    middle = rest.astype(jnp.bfloat16)
    low = (rest - middle.astype(jnp.float32)).astype(jnp.bfloat16)
    return [high, middle, low]


def one_hot(index, count):
    rows = lax.broadcasted_iota(jnp.int32, (count, index.shape[1]), 0)
    return rows == index


def take(table, index):
    rows, lanes = table.shape
    pick = one_hot(index // lanes, rows).astype(jnp.float32).astype(jnp.bfloat16)
    inside = one_hot(index % lanes, lanes)
    got = None
    for part in thirds(table):
        term = lax.dot_general(part, pick, (((0,), (0,)), ((), ())), preferred_element_type=jnp.float32)
        got = term if got is None else got + term
    return jnp.sum(jnp.where(inside, got, 0.0), axis=0, keepdims=True)


def put(values, index, rows, lanes):
    hot = one_hot(index // lanes, rows).astype(jnp.float32)
    inside = one_hot(index % lanes, lanes).astype(jnp.float32).astype(jnp.bfloat16)
    outs = []
    for value in values:
        total = None
        for part in thirds(value):
            left = (hot * part.astype(jnp.float32)).astype(jnp.bfloat16)
            term = lax.dot_general(left, inside, (((1,), (1,)), ((), ())), preferred_element_type=jnp.float32)
            total = term if total is None else total + term
        outs.append(total)
    return outs


def send_kernel(temp, cell, slot, coef, solid, temp_at, outgoing):
    lanes = temp.shape[1]
    got = take(temp[...], cell[...])
    temp_at[...] = got
    rows = outgoing.shape[1]
    filled = put([got, coef[...], solid[...]], slot[...], rows, lanes)
    for which in range(3):
        outgoing[which] = filled[which]


def land_kernel(arrived, source, gain, load):
    rows, lanes = source.shape
    temp, coef = arrived[0:1, :], arrived[1:2, :]
    cell = (arrived[2:3, :] + 0.5).astype(jnp.int32)
    total, inflow = put([coef, coef * temp], cell, rows, lanes)
    gain[...] = total
    load[...] = source[...] + inflow


def wall_kernel(solid, arrived, out):
    out[...] = take(solid[...], (arrived[2:3, :] + 0.5).astype(jnp.int32))


def flux_kernel(returned, slot, cell, coef, temp_at, out):
    rows, lanes = out.shape
    wall = take(returned[...], slot[...])
    out[...] = put([coef[...] * (wall - temp_at[...])], cell[...], rows, lanes)[0]


def local_call(kernel, outs, *args):
    whole = pl.BlockSpec(memory_space=VMEM)
    many = isinstance(outs[0], tuple)
    shaped = [jax.ShapeDtypeStruct(o, jnp.float32) for o in (outs if many else (outs,))]
    return pl.pallas_call(
        kernel,
        out_shape=tuple(shaped) if many else shaped[0],
        in_specs=[whole] * len(args),
        out_specs=(whole,) * len(shaped) if many else whole,
        name=kernel.__name__,
    )(*args)


def total_kernel(sizes, mine, out, held, send_sem, recv_sem):
    devices = sizes[0] * sizes[1] * sizes[2]
    me = (lax.axis_index("gx") * sizes[1] + lax.axis_index("gy")) * sizes[2] + lax.axis_index("gz")

    def place(step):
        other = lax.rem(me + step, devices)
        rest = lax.rem(other, sizes[1] * sizes[2])
        return (other // (sizes[1] * sizes[2]), rest // sizes[2], lax.rem(rest, sizes[2]))

    barrier = pltpu.get_barrier_semaphore()

    def greet(step, carry):
        pl.semaphore_signal(barrier, inc=1, device_id=place(step), device_id_type=pl.DeviceIdType.MESH)
        return carry

    def copy_of(step):
        return pltpu.make_async_remote_copy(
            src_ref=mine,
            dst_ref=held.at[step],
            send_sem=send_sem.at[step],
            recv_sem=recv_sem.at[step],
            device_id=place(step),
            device_id_type=pl.DeviceIdType.MESH,
        )

    def send(step, carry):
        copy_of(step).start()
        return carry

    def finish(step, carry):
        copy_of(step).wait()
        return carry

    lax.fori_loop(1, devices, greet, 0)
    pl.semaphore_wait(barrier, devices - 1)
    lax.fori_loop(1, devices, send, 0)
    lax.fori_loop(1, devices, finish, 0)
    out[...] = lax.fori_loop(1, devices, lambda step, total: total + held[step], mine[...])


def total_over_devices(values):
    sizes = tuple(lax.axis_size(axis) for axis in AXES)
    devices = sizes[0] * sizes[1] * sizes[2]
    whole = pl.BlockSpec(memory_space=VMEM)
    return pl.pallas_call(
        functools.partial(total_kernel, sizes),
        out_shape=jax.ShapeDtypeStruct(values.shape, values.dtype),
        in_specs=[whole],
        out_specs=whole,
        scratch_shapes=[
            VMEM((devices,) + values.shape, values.dtype),
            pltpu.SemaphoreType.DMA((devices,)),
            pltpu.SemaphoreType.DMA((devices,)),
        ],
        compiler_params=pltpu.CompilerParams(collective_id=0, has_side_effects=True),
        name="total",
    )(values)


def neighbours(padded):
    return (
        padded[2:, 1:-1, 1:-1],
        padded[:-2, 1:-1, 1:-1],
        padded[1:-1, 2:, 1:-1],
        padded[1:-1, :-2, 1:-1],
        padded[1:-1, 1:-1, 2:],
        padded[1:-1, 1:-1, :-2],
    )


def apply_operator(field, diagonal, weights):
    padded = with_halo(field, (("gx", 0), ("gy", 1), ("gz", 2)), 1, False)
    total = diagonal * field
    for weight, other in zip(weights, neighbours(padded)):
        total = total + weight * (field - other)
    return total


def per_device(
    density_start,
    velocity_start,
    temp_start,
    block_level,
    solid_source,
    ambient,
    conduct,
    pair_cell,
    pair_dest,
    pair_solid,
    pair_coef,
):
    size_x, size_y, size_z = density_start.shape
    blocks_x, blocks_y, blocks_z = block_level.shape
    fine = jnp.broadcast_to(
        (block_level == 1)[:, None, :, None, :, None], (blocks_x, BLK, blocks_y, BLK, blocks_z, BLK)
    ).reshape(size_x, size_y, size_z)
    fields = jnp.stack(
        [density_start, velocity_start[0], velocity_start[1], velocity_start[2], temp_start, fine.astype(jnp.float32)]
    )
    count = lax.axis_size("gx")
    fields = jnp.concatenate(
        [
            lax.ppermute(fields[:, -HALO:], "gx", [(i, (i + 1) % count) for i in range(count)]),
            fields,
            lax.ppermute(fields[:, :HALO], "gx", [((i + 1) % count, i) for i in range(count)]),
        ],
        axis=1,
    )
    fields = ring_halo(fields, "gy", 2, size_y + 8)
    fields = ring_halo(fields, "gz", 3, size_z + 128)
    fluid_temp, fluid_vel = run_fluid(fields, (size_x, size_y, size_z))

    groups = lax.axis_size(("gy", "gz"))
    pair_count = pair_cell.shape[0]
    capacity = 2 * pair_count // groups
    dest = pair_dest[:, 0]
    onehot = (dest[:, None] == jnp.arange(groups, dtype=jnp.int32)[None, :]).astype(jnp.int32)
    rank = jnp.sum((jnp.cumsum(onehot, axis=0) - onehot) * onehot, axis=1)
    slot = (dest * capacity + rank)[None, :]
    cell = pair_cell[None, :]
    coef = pair_coef[None, :]
    solid = pair_solid.astype(jnp.float32)[None, :]
    slot_rows = groups * capacity // size_z
    temp_at, outgoing = local_call(
        send_kernel,
        ((1, pair_count), (3, slot_rows, size_z)),
        fluid_temp.reshape(size_x * size_y, size_z), cell, slot, coef, solid,
    )
    arrived = lax.all_to_all(
        outgoing.reshape(3, groups, capacity), ("gy", "gz"), split_axis=1, concat_axis=1, tiled=True
    ).reshape(3, groups * capacity)
    solid_shape = solid_source.shape
    flat = (solid_shape[0] * solid_shape[1], solid_shape[2])
    gain, load = local_call(land_kernel, (flat, flat), arrived, solid_source.reshape(flat))
    diagonal = ambient + gain.reshape(solid_shape)
    residual = load.reshape(solid_shape)
    conduct_pad = with_halo(conduct, (("gx", 0), ("gy", 1), ("gz", 2)), 1, False)
    weights = [2.0 * conduct * other / (conduct + other) for other in neighbours(conduct_pad)]
    image = apply_operator(residual, diagonal, weights)
    twice = apply_operator(image, diagonal, weights)
    sums = [jnp.sum(a * b, axis=(0, 1)) for a, b in ((residual, residual), (residual, image), (image, image), (image, twice))]
    sums = total_over_devices(jnp.stack(sums + sums))
    sums = jnp.sum(sums, axis=1)
    norm, product, square, cross = sums[0], sums[1], sums[2], sums[3]
    alpha = norm / product
    norm_next = norm - 2.0 * alpha * product + alpha * alpha * square
    product_next = product - 2.0 * alpha * square + alpha * alpha * cross
    ratio = norm_next / norm
    alpha_next = norm_next / (product_next - ratio * norm_next / alpha)
    solid_temp = (alpha + alpha_next * (1.0 + ratio)) * residual - (alpha_next * alpha) * image

    wall = local_call(wall_kernel, (1, groups * capacity), solid_temp.reshape(flat), arrived)
    returned = lax.all_to_all(wall.reshape(groups, capacity), ("gy", "gz"), split_axis=0, concat_axis=0, tiled=True)
    wall_flux = local_call(
        flux_kernel, (size_x * size_y, size_z), returned.reshape(slot_rows, size_z), slot, cell, coef, temp_at
    )
    return (fluid_temp, fluid_vel, solid_temp, wall_flux.reshape(size_x, size_y, size_z))


def solution(mesh):
    return jax.shard_map(
        per_device,
        mesh=mesh,
        in_specs=(
            P("gx", "gy", "gz"),
            P(None, "gx", "gy", "gz"),
            P("gx", "gy", "gz"),
            P("gx", "gy", "gz"),
            P("gx", "gy", "gz"),
            P("gx", "gy", "gz"),
            P("gx", "gy", "gz"),
            P(("gx", "gy", "gz")),
            P(("gx", "gy", "gz"), None),
            P(("gx", "gy", "gz")),
            P(("gx", "gy", "gz")),
        ),
        out_specs=(
            P("gx", "gy", "gz"),
            P(None, "gx", "gy", "gz"),
            P("gx", "gy", "gz"),
            P("gx", "gy", "gz"),
        ),
        check_vma=False,
    )
```

time: 405 us -> 166 us (0.41)
  local copies, waits for them, and re-layouts: 121 us -> 13.7 us
  blocking collectives: 84.1 us -> 9.15 us
  other arithmetic: 76.8 us -> 15.2 us
  Pallas kernels: 0 us -> 45.9 us
  waiting for transfers between devices: 45.5 us -> 13.9 us
  starting transfers between devices: 68 us -> 58.2 us
    psum x2 -> x0, blocking collectives: 84.1 us -> none  [paired_sums(): lax.psum((jnp.sum(residual * residual), jnp.sum(residual * image)), ('gx'...]
    pallas_call x0 -> x6, Pallas kernels: none -> 45.9 us  [the longest x1 19.2 us: total_over_devices(): pl.pallas_call(functools.partial(total_kernel, sizes), out_shape=jax.Shap...]
    gather x3 -> x0, local copies, waits for them, and re-layouts: 37.2 us -> none  [the longest x1 20.4 us: per_device(): wall_slots = solid_temp.reshape(-1)[got_cell].reshape(groups, capacity)]
    scatter-add x3 -> x0, other arithmetic: 31.7 us -> none  [the longest x1 12.9 us: per_device(): gain = zeros_solid.at[got_cell].add(got_coef).reshape(solid_shape)]
    ppermute x15 -> x9, waiting for transfers between devices: 23.2 us -> 0.02 us  [with_halo(): lax.ppermute(head, axis, [((i + 1) % count, i) for i in range(ends)])]
    slice x9 -> x3, local copies, waits for them, and re-layouts: 23.2 us -> 0.86 us  [with_halo(): lax.slice_in_dim(cells, cells.shape[dim] - width, cells.shape[dim], axis=...]
    ppermute x8 -> x2, local copies, waits for them, and re-layouts: 22.2 us -> 2.44 us  [the longest x1 1.67 us: ring_halo(): lax.ppermute(tail, axis, [(i, (i + 1) % count) for i in range(count)])]
    unnamed x143 -> x36, local copies, waits for them, and re-layouts: 15.1 us -> 1.94 us
  transfers between devices with their start and end apart: 32 -> 25, of which waited for: 11 -> 9; matrix products, arithmetic and copies ran while one was open for 26% -> 9% of each run, Pallas kernels for 0% -> 2%
where the time goes in v1:
time: 166 us; the launch traced here: 165 us
  starting transfers between devices  58.2 us (35%)
  Pallas kernels  45.9 us (28%)
  other arithmetic  15.2 us (9%)
  waiting for transfers between devices  13.9 us (8%)
  local copies, waits for them, and re-layouts  13.7 us (8%)
  blocking collectives  9.15 us (6%)
  between operations  8.63 us (5%)
    ppermute x9, starting transfers between devices, with_halo(): lax.ppermute(tail, axis, [(i, (i + 1) % count) for i in range(ends)])  35.5 us
    pallas_call x1, Pallas kernels, total_over_devices(): pl.pallas_call(functools.partial(total_kernel, sizes), out_shape=jax.Shap...  19.2 us
    pallas_call x1, Pallas kernels, run_fluid(): pl.pallas_call(fluid_kernel, out_shape=(jax.ShapeDtypeStruct(shape, jnp.f...  16.6 us
    ppermute x9, starting transfers between devices, with_halo(): lax.ppermute(head, axis, [((i + 1) % count, i) for i in range(ends)])  11.6 us
    pallas_call x4, Pallas kernels, local_call(): pl.pallas_call(kernel, out_shape=tuple(shaped) if many else shaped[0], in...  10 us
    all_to_all x1, blocking collectives, per_device(): lax.all_to_all(wall.reshape(groups, capacity), ('gy', 'gz'), split_axis=0...  9.15 us
    ppermute x9, waiting for transfers between devices, with_halo(): lax.ppermute(tail, axis, [(i, (i + 1) % count) for i in range(ends)])  5.78 us
    ppermute x2, waiting for transfers between devices, ring_halo(): lax.ppermute(head, axis, [((i + 1) % count, i) for i in range(count)])  4.32 us
  transfers between devices with their start and end apart: 25, of which 9 were waited for; matrix products, arithmetic and copies ran while one was open for 9% of the time, Pallas kernels for 2%

profile of v1, /device:TPU:0, one launch (start us, length us, event | category | flops | bytes accessed | tf_op | source)
XLA Modules:
  0.0 164.7 jit_solution(12450620117718138563)
XLA Ops:
  0.7 0.7 fusion.48
  1.6 0.9 pad_maximum_fusion.14
  2.5 3.1 %collective-permute-start = (f32[6,2,16,128]{3,2,1,0:T(8,128)S(1)}, f32[6,2,16,128]{3,2,1,0:T(8,128)S(1)}, u32[]{:S(2)}, u32[]{:S(2)}) collective-permute-start(f32[6,2,16,128]{3,2,1,0:T(8,128)S(1)} %get-tuple-element.26), channel_id=1, source_target_pairs={{0,8},{8,16},{16,24},{24,0},{1,9},{9,17},{17,25},{25,1},{2,10},{10... | collective-permute-start | bytes 294920 | tf_op jit(solution)/shard_map/ppermute | solution.py:379
  5.6 2.1 %collective-permute-start.1 = (f32[6,2,16,128]{3,2,1,0:T(8,128)S(1)}, f32[6,2,16,128]{3,2,1,0:T(8,128)S(1)}, u32[]{:S(2)}, u32[]{:S(2)}) collective-permute-start(f32[6,2,16,128]{3,2,1,0:T(8,128)S(1)} %get-tuple-element.27), channel_id=1, source_target_pairs={{8,0},{16,8},{24,16},{0,24},{9,1},{17,9},{25,17},{1,25},{10,2},{18... | collective-permute-start | bytes 294920 | tf_op jit(solution)/shard_map/ppermute | solution.py:381
  7.7 1.3 fusion.56
  9.0 1.8 %collective-permute-start.8 = (f32[1,16,128]{2,1,0:T(8,128)S(1)}, f32[1,16,128]{2,1,0:T(8,128)S(1)}, u32[]{:S(2)}, u32[]{:S(2)}) collective-permute-start(f32[1,16,128]{2,1,0:T(8,128)S(1)} %get-tuple-element.43), channel_id=1, source_target_pairs={{0,8},{8,16},{16,24},{1,9},{9,17},{17,25},{2,10},{10,18},{18,26},{... | collective-permute-start | bytes 24584 | tf_op jit(solution)/shard_map/ppermute | solution.py:48
  10.8 1.3 collective-permute-start.6
  12.1 0.7 fusion.47
  12.8 2.3 %reduce-window.6 = s32[8,8,128]{2,1,0:T(8,128)S(1)} reduce-window(s32[8,8,128]{2,1,0:T(8,128)S(1)} %fusion.47, s32[]{:T(128)} %constant.9.clone.1), window={size=1x1x128 pad=0_0x0_0x127_0}, to_apply=%region_0.0 | reduce-window | flops 1040384 | bytes 65540 | tf_op jit(solution)/shard_map/reduce-window
  15.6 0.7 fusion.46
  16.3 1.3 bitcast_add_fusion.slot
  17.6 1.3 convert_element_type.27
  18.8 0.6 pad.93.clone
  19.6 1.6 collective-permute-start.2
  21.7 3.5 %collective-permute-done.2 = f32[6,20,2,128]{3,2,1,0:T(2,128)S(1)} collective-permute-done((f32[6,20,2,128]{3,2,1,0:T(2,128)S(1)}, f32[6,20,2,128]{3,2,1,0:T(2,128)S(1)}, u32[]{:S(2)}, u32[]{:S(2)}) %collective-permute-start.2) | collective-permute-done | bytes 122912 | tf_op jit(solution)/shard_map/ppermute | solution.py:66
  25.2 1.3 collective-permute-done.3
  27.2 0.7 copy-done.2
  28.6 1.4 copy.15
  30.0 0.8 copy.16
  31.3 0.6 constant_dynamic-update-slice_fusion
  31.9 0.8 collective-permute-done.4
  32.8 0.8 copy.17
  33.5 2.5 %collective-permute-done.5 = f32[6,20,24,2]{2,3,1,0:T(2,128)} collective-permute-done((f32[6,20,24,2]{2,3,1,0:T(2,128)S(1)}, f32[6,20,24,2]{2,3,1,0:T(2,128)}, u32[]{:S(2)}, u32[]{:S(2)}) %collective-permute-start.5) | collective-permute-done | bytes 23072 | tf_op jit(solution)/shard_map/ppermute | solution.py:67
  36.0 1.7 %copy.18 = f32[6,20,24,2]{3,2,1,0:T(8,128)S(1)} copy(f32[6,20,24,2]{2,3,1,0:T(2,128)} %collective-permute-done.5) | data formatting | bytes 46080 | tf_op jit(solution)/shard_map/ppermute | solution.py:67
  37.7 3.2 %pad_maximum_fusion.fields = f32[6,20,24,256]{3,2,1,0:T(8,128)} fusion(f32[6,20,24,2]{3,2,1,0:T(8,128)S(1)} %copy.18, f32[6,20,24,2]{3,2,1,0:T(8,128)S(1)} %copy.17, f32[6,20,2,128]{3,2,1,0:T(2,128)} %copy-done.12, f32[6,20,4,128]{3,2,1,0:T(4,128)} %copy-done.2, f32[6,20,2,128]{3,2,1,0:T(2,128)} %copy-done.11, f32[6,2,16,128]{3,2,1,0:T(8,128)} %copy-done.6, ...), kind=kLoop, calls=%fused_computation | loop fusion | flops 8110080 | bytes 4470784 | tf_op jit(solution)/shard_map/concatenate | solution.py:70
  40.9 16.6 %fluid.1 = (f32[16,16,128]{2,1,0:T(8,128)}, f32[3,16,16,128]{3,2,1,0:T(8,128)}) custom-call(f32[6,20,24,256]{3,2,1,0:T(8,128)} %pad_maximum_fusion.fields), custom_call_target="tpu_custom_call" | custom-call | tf_op jit(solution)/shard_map/fluid/pallas_call | solution.py:186
  57.6 3.0 %send_kernel.1 = (f32[1,1024]{1,0:T(1,128)}, f32[3,16,128]{2,1,0:T(8,128)}) custom-call(f32[256,128]{1,0:T(8,128)} %bitcast.69, s32[1,1024]{1,0:T(1,128)} %bitcast.76, s32[1,1024]{1,0:T(1,128)} %bitcast_add_fusion.slot, f32[1,1024]{1,0:T(1,128)} %bitcast.78, f32[1,1024]{1,0:T(1,128)} %bitcast.81), custom_call_target="tpu_custom_call" | custom-call | tf_op jit(solution)/shard_map/send_kernel/pallas_call | solution.py:268
  60.5 0.7 reshape.88
  61.3 0.6 copy.19
  61.9 3.3 %all-to-all-start = ((f32[3,8,256]{2,0,1:T(4,128)}), f32[3,8,256]{2,0,1:T(4,128)S(1)}, u32[]{:S(2)}, u32[]{:S(2)}) async-start(f32[3,8,256]{2,0,1:T(4,128)} %copy.19), calls=%async_computation | async-start | bytes 65536 | tf_op jit(solution)/shard_map/all_to_all | solution.py:405
  65.3 1.3 collective-permute-start.10
  66.6 4.5 %collective-permute-start.12 = (f32[10,1,128]{2,1,0:T(1,128)S(1)}, f32[10,1,128]{2,1,0:T(1,128)S(1)}, u32[]{:S(2)}, u32[]{:S(2)}) collective-permute-start(f32[10,1,128]{2,1,0:T(1,128)S(1)} %get-tuple-element.37), channel_id=1, source_target_pairs={{0,4},{1,5},{2,6},{3,7},{8,12},{9,13},{10,14},{11,15},{16,20},{17,... | collective-permute-start | bytes 15368 | tf_op jit(solution)/shard_map/ppermute | solution.py:48
  71.2 0.6 copy-done.13
  71.8 2.6 %land_kernel.1 = (f32[128,128]{1,0:T(8,128)}, f32[128,128]{1,0:T(8,128)}) custom-call(f32[3,2048]{1,0:T(4,128)} %bitcast.66, f32[128,128]{1,0:T(8,128)} %bitcast.71), custom_call_target="tpu_custom_call" | custom-call | tf_op jit(solution)/shard_map/land_kernel/pallas_call | solution.py:268
  74.3 0.8 slice_bitcast_fusion
  75.1 1.3 collective-permute-start.7
  76.4 4.9 %collective-permute-start.9 = (f32[1,16,128]{2,1,0:T(8,128)S(1)}, f32[1,16,128]{2,1,0:T(8,128)S(1)}, u32[]{:S(2)}, u32[]{:S(2)}) collective-permute-start(f32[1,16,128]{2,1,0:T(8,128)S(1)} %get-tuple-element.44), channel_id=1, source_target_pairs={{0,8},{8,16},{16,24},{1,9},{9,17},{17,25},{2,10},{10,18},{18,26},{... | collective-permute-start | bytes 24584 | tf_op jit(solution)/shard_map/ppermute | solution.py:48
  81.4 1.3 collective-permute-done.9
  82.6 0.8 pad_maximum_fusion.64
  83.4 1.3 collective-permute-start.11
  84.7 4.5 %collective-permute-start.13 = (f32[10,1,128]{2,1,0:T(1,128)S(1)}, f32[10,1,128]{2,1,0:T(1,128)S(1)}, u32[]{:S(2)}, u32[]{:S(2)}) collective-permute-start(f32[10,1,128]{2,1,0:T(1,128)S(1)} %get-tuple-element.38), channel_id=1, source_target_pairs={{0,4},{1,5},{2,6},{3,7},{8,12},{9,13},{10,14},{11,15},{16,20},{17,... | collective-permute-start | bytes 15368 | tf_op jit(solution)/shard_map/ppermute | solution.py:48
  89.4 1.3 collective-permute-start.14
  90.7 3.0 %collective-permute-start.16 = (f32[10,18,1]{2,1,0:T(8,128)S(1)}, f32[10,18,1]{2,1,0:T(8,128)S(1)}, u32[]{:S(2)}, u32[]{:S(2)}) collective-permute-start(f32[10,18,1]{2,1,0:T(8,128)S(1)} %get-tuple-element.30), channel_id=1, source_target_pairs={{0,1},{1,2},{2,3},{4,5},{5,6},{6,7},{8,9},{9,10},{10,11},{12,13},{... | collective-permute-start | bytes 2168 | tf_op jit(solution)/shard_map/ppermute | solution.py:48
  93.7 0.9 pad_maximum_fusion.9
  94.7 1.3 collective-permute-start.15
  96.0 4.1 %collective-permute-start.17 = (f32[10,18,1]{2,1,0:T(8,128)S(1)}, f32[10,18,1]{2,1,0:T(8,128)S(1)}, u32[]{:S(2)}, u32[]{:S(2)}) collective-permute-start(f32[10,18,1]{2,1,0:T(8,128)S(1)} %get-tuple-element.33), channel_id=1, source_target_pairs={{0,1},{1,2},{2,3},{4,5},{5,6},{6,7},{8,9},{9,10},{10,11},{12,13},{... | collective-permute-start | bytes 2168 | tf_op jit(solution)/shard_map/ppermute | solution.py:48
  100.1 0.9 collective-permute-done.17
  101.3 1.3 collective-permute-start.18
  102.6 4.8 %collective-permute-start.19 = (f32[1,16,128]{2,1,0:T(8,128)S(1)}, f32[1,16,128]{2,1,0:T(8,128)S(1)}, u32[]{:S(2)}, u32[]{:S(2)}) collective-permute-start(f32[1,16,128]{2,1,0:T(8,128)S(1)} %get-tuple-element.40), channel_id=1, source_target_pairs={{0,8},{8,16},{16,24},{1,9},{9,17},{17,25},{2,10},{10,18},{18,26},{... | collective-permute-start | bytes 24584 | tf_op jit(solution)/shard_map/ppermute | solution.py:48
  107.4 1.3 collective-permute-done.19
  108.8 1.3 collective-permute-start.20
  110.1 4.5 %collective-permute-start.21 = (f32[10,1,128]{2,1,0:T(1,128)S(1)}, f32[10,1,128]{2,1,0:T(1,128)S(1)}, u32[]{:S(2)}, u32[]{:S(2)}) collective-permute-start(f32[10,1,128]{2,1,0:T(1,128)S(1)} %get-tuple-element.34), channel_id=1, source_target_pairs={{0,4},{1,5},{2,6},{3,7},{8,12},{9,13},{10,14},{11,15},{16,20},{17,... | collective-permute-start | bytes 15368 | tf_op jit(solution)/shard_map/ppermute | solution.py:48
  114.6 1.3 collective-permute-done.21
  116.1 1.3 collective-permute-start.22
  117.4 3.2 %collective-permute-start.23 = (f32[10,18,1]{2,1,0:T(8,128)S(1)}, f32[10,18,1]{2,1,0:T(8,128)S(1)}, u32[]{:S(2)}, u32[]{:S(2)}) collective-permute-start(f32[10,18,1]{2,1,0:T(8,128)S(1)} %get-tuple-element.29), channel_id=1, source_target_pairs={{0,1},{1,2},{2,3},{4,5},{5,6},{6,7},{8,9},{9,10},{10,11},{12,13},{... | collective-permute-start | bytes 2168 | tf_op jit(solution)/shard_map/ppermute | solution.py:48
  120.6 0.9 collective-permute-done.23
  121.7 0.6 stack.37.mine
  122.3 19.2 %total.1 = f32[8,128]{1,0:T(8,128)} custom-call(f32[8,128]{1,0:T(8,128)} %stack.37.mine), custom_call_target="tpu_custom_call" | custom-call | tf_op jit(solution)/shard_map/total/pallas_call | solution.py:321
  141.5 0.8 reduce_sum.62
  142.3 0.7 fusion.57
  150.5 0.6 multiply_subtract_fusion
  151.1 2.1 %wall_kernel.1 = f32[1,2048]{1,0:T(1,128)} custom-call(f32[128,128]{1,0:T(8,128)} %bitcast.68, f32[3,2048]{1,0:T(4,128)} %bitcast.67), custom_call_target="tpu_custom_call" | custom-call | tf_op jit(solution)/shard_map/wall_kernel/pallas_call | solution.py:268
  153.2 9.1 %all_to_all.14 = f32[8,1,256]{2,1,0:T(1,128)} all-to-all(f32[8,1,256]{2,1,0:T(1,128)} %bitcast.75), channel_id=1, replica_groups=mesh['gx'=4,'gy'=2,'gz'=4] {'gy','gz'}, dimensions={0} | all-to-all | bytes 16384 | tf_op jit(solution)/shard_map/all_to_all | solution.py:429
  162.3 2.4 %flux_kernel.1 = f32[256,128]{1,0:T(8,128)} custom-call(f32[16,128]{1,0:T(8,128)} %bitcast.74, s32[1,1024]{1,0:T(1,128)} %bitcast_add_fusion.slot, s32[1,1024]{1,0:T(1,128)} %bitcast.77, f32[1,1024]{1,0:T(1,128)} %bitcast.79, f32[1,1024]{1,0:T(1,128)} %get-tuple-element.15.temp_at), custom_call_target="tpu_custom_call" | custom-call | tf_op jit(solution)/shard_map/flux_kernel/pallas_call | solution.py:268
  (75 shorter events, 4.1 us)
Async XLA Ops:
  0.6 18.8 %copy-start.4 = (f32[16,16,128]{2,1,0:T(8,128)S(1)}, f32[16,16,128]{2,1,0:T(8,128)}, u32[]{:S(2)}) copy-start(f32[16,16,128]{2,1,0:T(8,128)} %param.11) | copy-start | bytes 393220
  0.6 18.8 %copy-start.3 = (f32[16,16,128]{2,1,0:T(8,128)S(1)}, f32[16,16,128]{2,1,0:T(8,128)}, u32[]{:S(2)}) copy-start(f32[16,16,128]{2,1,0:T(8,128)} %param.13) | copy-start | bytes 393220
  0.7 18.8 %copy-start = (f32[3,16,16,128]{3,2,1,0:T(8,128)S(1)}, f32[3,16,16,128]{3,2,1,0:T(8,128)}, u32[]{:S(2)}) copy-start(f32[3,16,16,128]{3,2,1,0:T(8,128)} %param.12) | copy-start | bytes 1179652
  0.7 21.0 %copy-start.9 = (f32[8,16,128]{2,1,0:T(8,128)S(1)}, f32[8,16,128]{2,1,0:T(8,128)}, u32[]{:S(2)}) copy-start(f32[8,16,128]{2,1,0:T(8,128)} %param.17) | copy-start | bytes 196612
  2.5 17.0 %collective-permute-start = (f32[6,2,16,128]{3,2,1,0:T(8,128)S(1)}, f32[6,2,16,128]{3,2,1,0:T(8,128)S(1)}, u32[]{:S(2)}, u32[]{:S(2)}) collective-permute-start(f32[6,2,16,128]{3,2,1,0:T(8,128)S(1)} %get-tuple-element.26), channel_id=1, source_target_pairs={{0,8},{8,16},{16,24},{24,0},{1,9},{9,17},{17,25},{25,1},{2,10},{10... | collective-permute-start | bytes 294920 | tf_op jit(solution)/shard_map/ppermute | solution.py:379
  5.6 13.9 %collective-permute-start.1 = (f32[6,2,16,128]{3,2,1,0:T(8,128)S(1)}, f32[6,2,16,128]{3,2,1,0:T(8,128)S(1)}, u32[]{:S(2)}, u32[]{:S(2)}) collective-permute-start(f32[6,2,16,128]{3,2,1,0:T(8,128)S(1)} %get-tuple-element.27), channel_id=1, source_target_pairs={{8,0},{16,8},{24,16},{0,24},{9,1},{17,9},{25,17},{1,25},{10,2},{18... | collective-permute-start | bytes 294920 | tf_op jit(solution)/shard_map/ppermute | solution.py:381
  9.0 12.7 %collective-permute-start.8 = (f32[1,16,128]{2,1,0:T(8,128)S(1)}, f32[1,16,128]{2,1,0:T(8,128)S(1)}, u32[]{:S(2)}, u32[]{:S(2)}) collective-permute-start(f32[1,16,128]{2,1,0:T(8,128)S(1)} %get-tuple-element.43), channel_id=1, source_target_pairs={{0,8},{8,16},{16,24},{1,9},{9,17},{17,25},{2,10},{10,18},{18,26},{... | collective-permute-start | bytes 24584 | tf_op jit(solution)/shard_map/ppermute | solution.py:48
  10.8 20.5 %collective-permute-start.6 = (f32[1,16,128]{2,1,0:T(8,128)}, f32[1,16,128]{2,1,0:T(8,128)S(1)}, u32[]{:S(2)}, u32[]{:S(2)}) collective-permute-start(f32[1,16,128]{2,1,0:T(8,128)} %get-tuple-element.42), channel_id=1, source_target_pairs={{8,0},{16,8},{24,16},{9,1},{17,9},{25,17},{10,2},{18,10},{26,18},{... | collective-permute-start | bytes 24584 | tf_op jit(solution)/shard_map/ppermute | solution.py:50
  19.5 7.1 %copy-start.5 = (f32[6,2,16,128]{3,2,1,0:T(8,128)}, f32[6,2,16,128]{3,2,1,0:T(8,128)S(1)}, u32[]{:S(2)}) copy-start(f32[6,2,16,128]{3,2,1,0:T(8,128)S(1)} %collective-permute-done) | copy-start | bytes 294916
  19.5 7.1 %copy-start.6 = (f32[6,2,16,128]{3,2,1,0:T(8,128)}, f32[6,2,16,128]{3,2,1,0:T(8,128)S(1)}, u32[]{:S(2)}) copy-start(f32[6,2,16,128]{3,2,1,0:T(8,128)S(1)} %collective-permute-done.1) | copy-start | bytes 294916
  19.6 5.6 %collective-permute-start.2 = (f32[6,20,2,128]{3,2,1,0:T(2,128)S(1)}, f32[6,20,2,128]{3,2,1,0:T(2,128)S(1)}, u32[]{:S(2)}, u32[]{:S(2)}) collective-permute-start(f32[6,20,2,128]{3,2,1,0:T(2,128)S(1)} %get-tuple-element.24), channel_id=1, source_target_pairs={{4,0},{0,4},{5,1},{1,5},{6,2},{2,6},{7,3},{3,7},{12,8},{8,12},{13,... | collective-permute-start | bytes 368648 | tf_op jit(solution)/shard_map/ppermute | solution.py:66
  21.2 5.4 %collective-permute-start.3 = (f32[6,20,2,128]{3,2,1,0:T(2,128)S(1)}, f32[6,20,2,128]{3,2,1,0:T(2,128)S(1)}, u32[]{:S(2)}, u32[]{:S(2)}) collective-permute-start(f32[6,20,2,128]{3,2,1,0:T(2,128)S(1)} %get-tuple-element.25), channel_id=1, source_target_pairs={{0,4},{4,0},{1,5},{5,1},{2,6},{6,2},{3,7},{7,3},{8,12},{12,8},{9,1... | collective-permute-start | bytes 368648 | tf_op jit(solution)/shard_map/ppermute | solution.py:67
  21.7 4.8 %copy-start.7 = (f32[10,16,128]{2,1,0:T(8,128)}, f32[10,16,128]{2,1,0:T(8,128)S(1)}, u32[]{:S(2)}) copy-start(f32[10,16,128]{2,1,0:T(8,128)S(1)} %constant_dynamic-update-slice_fusion.1) | copy-start | bytes 245764
  25.2 1.4 copy-start.11
  26.5 0.6 copy-start.12
  27.2 0.7 copy-start.2
  30.0 2.8 %collective-permute-start.4 = (f32[6,20,24,2]{2,3,1,0:T(2,128)}, f32[6,20,24,2]{2,3,1,0:T(2,128)S(1)}, u32[]{:S(2)}, u32[]{:S(2)}) collective-permute-start(f32[6,20,24,2]{2,3,1,0:T(2,128)} %copy.15), channel_id=1, source_target_pairs={{1,0},{2,1},{3,2},{0,3},{5,4},{6,5},{7,6},{4,7},{9,8},{10,9},{11,1... | collective-permute-start | bytes 69128 | tf_op jit(solution)/shard_map/ppermute | solution.py:66
  30.8 5.2 %collective-permute-start.5 = (f32[6,20,24,2]{2,3,1,0:T(2,128)S(1)}, f32[6,20,24,2]{2,3,1,0:T(2,128)}, u32[]{:S(2)}, u32[]{:S(2)}) collective-permute-start(f32[6,20,24,2]{2,3,1,0:T(2,128)S(1)} %copy.16), channel_id=1, source_target_pairs={{0,1},{1,2},{2,3},{3,0},{4,5},{5,6},{6,7},{7,4},{8,9},{9,10},{10,1... | collective-permute-start | bytes 69128 | tf_op jit(solution)/shard_map/ppermute | solution.py:67
  31.9 5.7 %copy-start.16 = (f32[256]{0:T(256)S(1)}, f32[256]{0:T(256)}, u32[]{:S(2)}) copy-start(f32[256]{0:T(256)} %pad.93.clone) | copy-start | bytes 3076
  40.9 24.3 %copy-start.8 = (f32[10,16,128]{2,1,0:T(8,128)S(1)}, f32[10,16,128]{2,1,0:T(8,128)}, u32[]{:S(2)}) copy-start(f32[10,16,128]{2,1,0:T(8,128)} %constant_dynamic-update-slice_fusion) | copy-start | bytes 245764
  57.5 43.5 %copy-start.10 = (f32[8,16,128]{2,1,0:T(8,128)S(1)}, f32[8,16,128]{2,1,0:T(8,128)}, u32[]{:S(2)}) copy-start(f32[8,16,128]{2,1,0:T(8,128)} %param.17) | copy-start | bytes 196612
  57.5 43.5 %copy-start.14 = (f32[8,16,128]{2,1,0:T(8,128)S(1)}, f32[8,16,128]{2,1,0:T(8,128)}, u32[]{:S(2)}) copy-start(f32[8,16,128]{2,1,0:T(8,128)} %param.16) | copy-start | bytes 196612
  61.9 9.2 %all-to-all-start = ((f32[3,8,256]{2,0,1:T(4,128)}), f32[3,8,256]{2,0,1:T(4,128)S(1)}, u32[]{:S(2)}, u32[]{:S(2)}) async-start(f32[3,8,256]{2,0,1:T(4,128)} %copy.19), calls=%async_computation | async-start | bytes 65536 | tf_op jit(solution)/shard_map/all_to_all | solution.py:405
  65.3 16.0 %collective-permute-start.10 = (f32[10,1,128]{2,1,0:T(1,128)S(1)}, f32[10,1,128]{2,1,0:T(1,128)S(1)}, u32[]{:S(2)}, u32[]{:S(2)}) collective-permute-start(f32[10,1,128]{2,1,0:T(1,128)S(1)} %get-tuple-element.36), channel_id=1, source_target_pairs={{4,0},{5,1},{6,2},{7,3},{12,8},{13,9},{14,10},{15,11},{20,16},{21,... | collective-permute-start | bytes 15368 | tf_op jit(solution)/shard_map/ppermute | solution.py:50
  66.6 14.7 %collective-permute-start.12 = (f32[10,1,128]{2,1,0:T(1,128)S(1)}, f32[10,1,128]{2,1,0:T(1,128)S(1)}, u32[]{:S(2)}, u32[]{:S(2)}) collective-permute-start(f32[10,1,128]{2,1,0:T(1,128)S(1)} %get-tuple-element.37), channel_id=1, source_target_pairs={{0,4},{1,5},{2,6},{3,7},{8,12},{9,13},{10,14},{11,15},{16,20},{17,... | collective-permute-start | bytes 15368 | tf_op jit(solution)/shard_map/ppermute | solution.py:48
  71.1 0.6 copy-start.13
  74.3 26.7 %copy-start.1 = (f32[128,128]{1,0:T(8,128)S(1)}, f32[128,128]{1,0:T(8,128)}, u32[]{:S(2)}) copy-start(f32[128,128]{1,0:T(8,128)} %get-tuple-element.13) | copy-start | bytes 196612
  74.3 26.7 %copy-start.15 = (f32[128,128]{1,0:T(8,128)S(1)}, f32[128,128]{1,0:T(8,128)}, u32[]{:S(2)}) copy-start(f32[128,128]{1,0:T(8,128)} %get-tuple-element.14) | copy-start | bytes 196612
  75.1 6.2 %collective-permute-start.7 = (f32[1,16,128]{2,1,0:T(8,128)S(1)}, f32[1,16,128]{2,1,0:T(8,128)S(1)}, u32[]{:S(2)}, u32[]{:S(2)}) collective-permute-start(f32[1,16,128]{2,1,0:T(8,128)S(1)} %get-tuple-element.45), channel_id=1, source_target_pairs={{8,0},{16,8},{24,16},{9,1},{17,9},{25,17},{10,2},{18,10},{26,18},{... | collective-permute-start | bytes 24584 | tf_op jit(solution)/shard_map/ppermute | solution.py:50
  76.4 6.3 %collective-permute-start.9 = (f32[1,16,128]{2,1,0:T(8,128)S(1)}, f32[1,16,128]{2,1,0:T(8,128)S(1)}, u32[]{:S(2)}, u32[]{:S(2)}) collective-permute-start(f32[1,16,128]{2,1,0:T(8,128)S(1)} %get-tuple-element.44), channel_id=1, source_target_pairs={{0,8},{8,16},{16,24},{1,9},{9,17},{17,25},{2,10},{10,18},{18,26},{... | collective-permute-start | bytes 24584 | tf_op jit(solution)/shard_map/ppermute | solution.py:48
  83.4 10.3 %collective-permute-start.11 = (f32[10,1,128]{2,1,0:T(1,128)S(1)}, f32[10,1,128]{2,1,0:T(1,128)S(1)}, u32[]{:S(2)}, u32[]{:S(2)}) collective-permute-start(f32[10,1,128]{2,1,0:T(1,128)S(1)} %get-tuple-element.39), channel_id=1, source_target_pairs={{4,0},{5,1},{6,2},{7,3},{12,8},{13,9},{14,10},{15,11},{20,16},{21,... | collective-permute-start | bytes 15368 | tf_op jit(solution)/shard_map/ppermute | solution.py:50
  84.7 9.0 %collective-permute-start.13 = (f32[10,1,128]{2,1,0:T(1,128)S(1)}, f32[10,1,128]{2,1,0:T(1,128)S(1)}, u32[]{:S(2)}, u32[]{:S(2)}) collective-permute-start(f32[10,1,128]{2,1,0:T(1,128)S(1)} %get-tuple-element.38), channel_id=1, source_target_pairs={{0,4},{1,5},{2,6},{3,7},{8,12},{9,13},{10,14},{11,15},{16,20},{17,... | collective-permute-start | bytes 15368 | tf_op jit(solution)/shard_map/ppermute | solution.py:48
  89.4 10.7 %collective-permute-start.14 = (f32[10,18,1]{2,1,0:T(8,128)S(1)}, f32[10,18,1]{2,1,0:T(8,128)S(1)}, u32[]{:S(2)}, u32[]{:S(2)}) collective-permute-start(f32[10,18,1]{2,1,0:T(8,128)S(1)} %get-tuple-element.31), channel_id=1, source_target_pairs={{1,0},{2,1},{3,2},{5,4},{6,5},{7,6},{9,8},{10,9},{11,10},{13,12},{... | collective-permute-start | bytes 2168 | tf_op jit(solution)/shard_map/ppermute | solution.py:50
  90.7 9.4 %collective-permute-start.16 = (f32[10,18,1]{2,1,0:T(8,128)S(1)}, f32[10,18,1]{2,1,0:T(8,128)S(1)}, u32[]{:S(2)}, u32[]{:S(2)}) collective-permute-start(f32[10,18,1]{2,1,0:T(8,128)S(1)} %get-tuple-element.30), channel_id=1, source_target_pairs={{0,1},{1,2},{2,3},{4,5},{5,6},{6,7},{8,9},{9,10},{10,11},{12,13},{... | collective-permute-start | bytes 2168 | tf_op jit(solution)/shard_map/ppermute | solution.py:48
  94.7 5.4 %collective-permute-start.15 = (f32[10,18,1]{2,1,0:T(8,128)S(1)}, f32[10,18,1]{2,1,0:T(8,128)S(1)}, u32[]{:S(2)}, u32[]{:S(2)}) collective-permute-start(f32[10,18,1]{2,1,0:T(8,128)S(1)} %get-tuple-element.32), channel_id=1, source_target_pairs={{1,0},{2,1},{3,2},{5,4},{6,5},{7,6},{9,8},{10,9},{11,10},{13,12},{... | collective-permute-start | bytes 2168 | tf_op jit(solution)/shard_map/ppermute | solution.py:50
  96.0 5.0 %collective-permute-start.17 = (f32[10,18,1]{2,1,0:T(8,128)S(1)}, f32[10,18,1]{2,1,0:T(8,128)S(1)}, u32[]{:S(2)}, u32[]{:S(2)}) collective-permute-start(f32[10,18,1]{2,1,0:T(8,128)S(1)} %get-tuple-element.33), channel_id=1, source_target_pairs={{0,1},{1,2},{2,3},{4,5},{5,6},{6,7},{8,9},{9,10},{10,11},{12,13},{... | collective-permute-start | bytes 2168 | tf_op jit(solution)/shard_map/ppermute | solution.py:48
  101.3 6.1 %collective-permute-start.18 = (f32[1,16,128]{2,1,0:T(8,128)S(1)}, f32[1,16,128]{2,1,0:T(8,128)S(1)}, u32[]{:S(2)}, u32[]{:S(2)}) collective-permute-start(f32[1,16,128]{2,1,0:T(8,128)S(1)} %get-tuple-element.41), channel_id=1, source_target_pairs={{8,0},{16,8},{24,16},{9,1},{17,9},{25,17},{10,2},{18,10},{26,18},{... | collective-permute-start | bytes 24584 | tf_op jit(solution)/shard_map/ppermute | solution.py:50
  102.6 6.2 %collective-permute-start.19 = (f32[1,16,128]{2,1,0:T(8,128)S(1)}, f32[1,16,128]{2,1,0:T(8,128)S(1)}, u32[]{:S(2)}, u32[]{:S(2)}) collective-permute-start(f32[1,16,128]{2,1,0:T(8,128)S(1)} %get-tuple-element.40), channel_id=1, source_target_pairs={{0,8},{8,16},{16,24},{1,9},{9,17},{17,25},{2,10},{10,18},{18,26},{... | collective-permute-start | bytes 24584 | tf_op jit(solution)/shard_map/ppermute | solution.py:48
  108.8 5.9 %collective-permute-start.20 = (f32[10,1,128]{2,1,0:T(1,128)S(1)}, f32[10,1,128]{2,1,0:T(1,128)S(1)}, u32[]{:S(2)}, u32[]{:S(2)}) collective-permute-start(f32[10,1,128]{2,1,0:T(1,128)S(1)} %get-tuple-element.35), channel_id=1, source_target_pairs={{4,0},{5,1},{6,2},{7,3},{12,8},{13,9},{14,10},{15,11},{20,16},{21,... | collective-permute-start | bytes 15368 | tf_op jit(solution)/shard_map/ppermute | solution.py:50
  110.1 5.9 %collective-permute-start.21 = (f32[10,1,128]{2,1,0:T(1,128)S(1)}, f32[10,1,128]{2,1,0:T(1,128)S(1)}, u32[]{:S(2)}, u32[]{:S(2)}) collective-permute-start(f32[10,1,128]{2,1,0:T(1,128)S(1)} %get-tuple-element.34), channel_id=1, source_target_pairs={{0,4},{1,5},{2,6},{3,7},{8,12},{9,13},{10,14},{11,15},{16,20},{17,... | collective-permute-start | bytes 15368 | tf_op jit(solution)/shard_map/ppermute | solution.py:48
  116.1 4.5 %collective-permute-start.22 = (f32[10,18,1]{2,1,0:T(8,128)S(1)}, f32[10,18,1]{2,1,0:T(8,128)S(1)}, u32[]{:S(2)}, u32[]{:S(2)}) collective-permute-start(f32[10,18,1]{2,1,0:T(8,128)S(1)} %get-tuple-element.28), channel_id=1, source_target_pairs={{1,0},{2,1},{3,2},{5,4},{6,5},{7,6},{9,8},{10,9},{11,10},{13,12},{... | collective-permute-start | bytes 2168 | tf_op jit(solution)/shard_map/ppermute | solution.py:50
  117.4 4.1 %collective-permute-start.23 = (f32[10,18,1]{2,1,0:T(8,128)S(1)}, f32[10,18,1]{2,1,0:T(8,128)S(1)}, u32[]{:S(2)}, u32[]{:S(2)}) collective-permute-start(f32[10,18,1]{2,1,0:T(8,128)S(1)} %get-tuple-element.29), channel_id=1, source_target_pairs={{0,1},{1,2},{2,3},{4,5},{5,6},{6,7},{8,9},{9,10},{10,11},{12,13},{... | collective-permute-start | bytes 2168 | tf_op jit(solution)/shard_map/ppermute | solution.py:48

commit v2 on v1

--- a/solution.py
+++ b/solution.py
@@ -37,22 +37,6 @@
 stacked_set = velocity_set + velocity_set[:7]
 
 
-def with_halo(cells, sides, width, closed):
-    for axis, dim in sides:
-        count = lax.axis_size(axis)
-        ends = count if closed else count - 1
-        head = lax.slice_in_dim(cells, 0, width, axis=dim)
-        tail = lax.slice_in_dim(cells, cells.shape[dim] - width, cells.shape[dim], axis=dim)
-        cells = jnp.concatenate(
-            [
-                lax.ppermute(tail, axis, [(i, (i + 1) % count) for i in range(ends)]),
-                cells,
-                lax.ppermute(head, axis, [((i + 1) % count, i) for i in range(ends)]),
-            ],
-            axis=dim,
-        )
-    return cells
-
 AXES = ("gx", "gy", "gz")
 HALO = 2
 VMEM = pltpu.VMEM
@@ -233,123 +217,225 @@
 
 
 def send_kernel(temp, cell, slot, coef, solid, temp_at, outgoing):
-    lanes = temp.shape[1]
     got = take(temp[...], cell[...])
     temp_at[...] = got
-    rows = outgoing.shape[1]
-    filled = put([got, coef[...], solid[...]], slot[...], rows, lanes)
-    for which in range(3):
-        outgoing[which] = filled[which]
-
-
-def land_kernel(arrived, source, gain, load):
-    rows, lanes = source.shape
-    temp, coef = arrived[0:1, :], arrived[1:2, :]
-    cell = (arrived[2:3, :] + 0.5).astype(jnp.int32)
-    total, inflow = put([coef, coef * temp], cell, rows, lanes)
-    gain[...] = total
-    load[...] = source[...] + inflow
-
-
-def wall_kernel(solid, arrived, out):
-    out[...] = take(solid[...], (arrived[2:3, :] + 0.5).astype(jnp.int32))
-
-
-def flux_kernel(returned, slot, cell, coef, temp_at, out):
-    rows, lanes = out.shape
-    wall = take(returned[...], slot[...])
-    out[...] = put([coef[...] * (wall - temp_at[...])], cell[...], rows, lanes)[0]
+    groups, kinds, width = outgoing.shape
+    filled = put([got, coef[...], solid[...]], slot[...], groups, width)
+    for which in range(kinds):
+        for group in range(groups):
+            outgoing[group, which : which + 1, :] = filled[which][group : group + 1, :]
 
 
 def local_call(kernel, outs, *args):
     whole = pl.BlockSpec(memory_space=VMEM)
-    many = isinstance(outs[0], tuple)
-    shaped = [jax.ShapeDtypeStruct(o, jnp.float32) for o in (outs if many else (outs,))]
     return pl.pallas_call(
         kernel,
-        out_shape=tuple(shaped) if many else shaped[0],
+        out_shape=tuple(jax.ShapeDtypeStruct(o, jnp.float32) for o in outs),
         in_specs=[whole] * len(args),
-        out_specs=(whole,) * len(shaped) if many else whole,
+        out_specs=(whole,) * len(outs),
         name=kernel.__name__,
     )(*args)
 
 
-def total_kernel(sizes, mine, out, held, send_sem, recv_sem):
-    devices = sizes[0] * sizes[1] * sizes[2]
-    me = (lax.axis_index("gx") * sizes[1] + lax.axis_index("gy")) * sizes[2] + lax.axis_index("gz")
-
-    def place(step):
-        other = lax.rem(me + step, devices)
-        rest = lax.rem(other, sizes[1] * sizes[2])
-        return (other // (sizes[1] * sizes[2]), rest // sizes[2], lax.rem(rest, sizes[2]))
+def wall_kernel(
+    sizes, outgoing, source, ambient, conduct, slot, cell, coef, temp_at, solid_out, flux_out,
+    arrived, back, returned, residual, image, face_y, face_z, got_x, got_y, got_z, part, whole, held_x, held_g,
+    own_sem, pair_send, pair_recv, back_send, back_recv, face_send, face_recv, x_send, x_recv, g_send, g_recv,
+):
+    count_x, count_y, count_z = sizes
+    groups = count_y * count_z
+    my_x, my_y, my_z = (lax.axis_index(axis) for axis in AXES)
+    me = my_y * count_z + my_z
+    mesh = pl.DeviceIdType.MESH
+    size_x, size_y, size_z = source.shape
+
+    def mate(step):
+        other = lax.rem(me + step, groups)
+        return (my_x, other // count_z, lax.rem(other, count_z))
+
+    def row(step):
+        return (lax.rem(my_x + step, count_x), my_y, my_z)
+
+    def remote(src, dst, send, recv, device):
+        return pltpu.make_async_remote_copy(
+            src_ref=src, dst_ref=dst, send_sem=send, recv_sem=recv, device_id=device, device_id_type=mesh
+        )
 
     barrier = pltpu.get_barrier_semaphore()
-
-    def greet(step, carry):
-        pl.semaphore_signal(barrier, inc=1, device_id=place(step), device_id_type=pl.DeviceIdType.MESH)
-        return carry
-
-    def copy_of(step):
-        return pltpu.make_async_remote_copy(
-            src_ref=mine,
-            dst_ref=held.at[step],
-            send_sem=send_sem.at[step],
-            recv_sem=recv_sem.at[step],
-            device_id=place(step),
-            device_id_type=pl.DeviceIdType.MESH,
+    for step in range(1, groups):
+        pl.semaphore_signal(barrier, inc=1, device_id=mate(step), device_id_type=mesh)
+    for step in range(1, count_x):
+        pl.semaphore_signal(barrier, inc=1, device_id=row(step), device_id_type=mesh)
+    pl.semaphore_wait(barrier, groups + count_x - 2)
+
+    pairs = [
+        remote(
+            outgoing.at[lax.rem(me + step, groups)], arrived.at[step], pair_send.at[step], pair_recv.at[step], mate(step)
         )
-
-    def send(step, carry):
-        copy_of(step).start()
-        return carry
-
-    def finish(step, carry):
-        copy_of(step).wait()
-        return carry
-
-    lax.fori_loop(1, devices, greet, 0)
-    pl.semaphore_wait(barrier, devices - 1)
-    lax.fori_loop(1, devices, send, 0)
-    lax.fori_loop(1, devices, finish, 0)
-    out[...] = lax.fori_loop(1, devices, lambda step, total: total + held[step], mine[...])
-
-
-def total_over_devices(values):
+        for step in range(1, groups)
+    ]
+    for copy in pairs:
+        copy.start()
+    own = pltpu.make_async_copy(outgoing.at[me], arrived.at[0], own_sem.at[0])
+    own.start()
+
+    y_next = (my_x, lax.rem(my_y + 1, count_y), my_z)
+    y_last = (my_x, lax.rem(my_y + count_y - 1, count_y), my_z)
+    z_next = (my_x, my_y, lax.rem(my_z + 1, count_z))
+    z_last = (my_x, my_y, lax.rem(my_z + count_z - 1, count_z))
+
+    def send_faces(which, field):
+        value = field[...]
+        face_y[which, 0] = value[:, 0, :]
+        face_y[which, 1] = value[:, size_y - 1, :]
+        turned = jnp.transpose(value.reshape(size_x * size_y, size_z))
+        face_z[which, 0] = turned[0:8]
+        face_z[which, 1] = turned[size_z - 8 : size_z]
+        plan = (
+            (field.at[size_x - 1], got_x.at[which, 0], row(1)),
+            (field.at[0], got_x.at[which, 1], row(count_x - 1)),
+            (face_y.at[which, 1], got_y.at[which, 0], y_next),
+            (face_y.at[which, 0], got_y.at[which, 1], y_last),
+            (face_z.at[which, 1], got_z.at[which, 0], z_next),
+            (face_z.at[which, 0], got_z.at[which, 1], z_last),
+        )
+        copies = [
+            remote(src, dst, face_send.at[which, at], face_recv.at[which, at], device)
+            for at, (src, dst, device) in enumerate(plan)
+        ]
+        for copy in copies:
+            copy.start()
+        return copies
+
+    def around(which, field, copies):
+        for copy in copies:
+            copy.wait()
+        value = field[...]
+        below_x = jnp.concatenate([got_x[which, 0][None], value[:-1]], axis=0)
+        above_x = jnp.concatenate([value[1:], got_x[which, 1][None]], axis=0)
+        at_y = lax.broadcasted_iota(jnp.int32, value.shape, 1)
+        below_y = jnp.where(at_y == 0, got_y[which, 0][:, None, :], pltpu.roll(value, 1, 1))
+        above_y = jnp.where(at_y == size_y - 1, got_y[which, 1][:, None, :], pltpu.roll(value, size_y - 1, 1))
+        at_z = lax.broadcasted_iota(jnp.int32, value.shape, 2)
+
+        def column(line):
+            return jnp.transpose(jnp.broadcast_to(line, (size_z, size_x * size_y))).reshape(value.shape)
+
+        below_z = jnp.where(at_z == 0, column(got_z[which, 0][7:8]), pltpu.roll(value, 1, 2))
+        above_z = jnp.where(at_z == size_z - 1, column(got_z[which, 1][0:1]), pltpu.roll(value, size_z - 1, 2))
+        return (above_x, below_x, above_y, below_y, above_z, below_z)
+
+    conduct_copies = send_faces(0, conduct)
+    conducts = around(0, conduct, conduct_copies)
+    at_x, at_y, at_z = (lax.broadcasted_iota(jnp.int32, source.shape, dim) for dim in range(3))
+    place_x, place_y, place_z = at_x + my_x * size_x, at_y + my_y * size_y, at_z + my_z * size_z
+    inside = (
+        place_x < count_x * size_x - 1, place_x > 0,
+        place_y < count_y * size_y - 1, place_y > 0,
+        place_z < count_z * size_z - 1, place_z > 0,
+    )
+    here = conduct[...]
+    weights = [jnp.where(ok, 2.0 * here * other / (here + other), 0.0) for ok, other in zip(inside, conducts)]
+
+    own.wait()
+    for copy in pairs:
+        copy.wait()
+    landed = jnp.concatenate([arrived[step] for step in range(groups)], axis=1)
+    solid_cell = (landed[2:3, :] + 0.5).astype(jnp.int32)
+    gain, inflow = put([landed[1:2, :], landed[1:2, :] * landed[0:1, :]], solid_cell, size_x * size_y, size_z)
+    residual[...] = source[...] + inflow.reshape(source.shape)
+    diagonal = ambient[...] + gain.reshape(source.shape)
+
+    def operate(which, field, copies):
+        value = field[...]
+        total = diagonal * value
+        for weight, other in zip(weights, around(which, field, copies)):
+            total = total + weight * (value - other)
+        return total
+
+    image[...] = operate(1, residual, send_faces(1, residual))
+    twice = operate(2, image, send_faces(2, image))
+
+    first, second = residual[...], image[...]
+    products = [jnp.sum(jnp.sum(a * b, axis=0), axis=0, keepdims=True)
+                for a, b in ((first, first), (first, second), (second, second), (second, twice))]
+    part[...] = jnp.concatenate(products + products, axis=0)
+    copies = [remote(part, held_x.at[step], x_send.at[step], x_recv.at[step], row(step)) for step in range(1, count_x)]
+    for copy in copies:
+        copy.start()
+    total = part[...]
+    for step, copy in enumerate(copies):
+        copy.wait()
+        total = total + held_x[step + 1]
+    whole[...] = total
+    copies = [remote(whole, held_g.at[step], g_send.at[step], g_recv.at[step], mate(step)) for step in range(1, groups)]
+    for copy in copies:
+        copy.start()
+    for step, copy in enumerate(copies):
+        copy.wait()
+        total = total + held_g[step + 1]
+    total = jnp.broadcast_to(jnp.sum(total, axis=1, keepdims=True), total.shape)
+    norm, product, square, cross = (total[at : at + 1] for at in range(4))
+    alpha = norm / product
+    norm_next = norm - 2.0 * alpha * product + alpha * alpha * square
+    product_next = product - 2.0 * alpha * square + alpha * alpha * cross
+    ratio = norm_next / norm
+    alpha_next = norm_next / (product_next - ratio * norm_next / alpha)
+    on_first = alpha + alpha_next * (1.0 + ratio)
+    on_second = alpha_next * alpha
+    flat = (size_x * size_y, size_z)
+    solid = on_first * first.reshape(flat) - on_second * second.reshape(flat)
+    solid_out[...] = solid.reshape(source.shape)
+
+    wall = take(solid, solid_cell)
+    width = returned.shape[2]
+    for step in range(groups):
+        back[step] = wall[:, step * width : (step + 1) * width]
+    copies = [
+        remote(back.at[step], returned.at[me], back_send.at[step], back_recv.at[step], mate(groups - step))
+        for step in range(1, groups)
+    ]
+    for copy in copies:
+        copy.start()
+    own = pltpu.make_async_copy(back.at[0], returned.at[me], own_sem.at[1])
+    own.start()
+    own.wait()
+    for copy in copies:
+        copy.wait()
+    table = jnp.concatenate([returned[group] for group in range(groups)], axis=0)
+    flux = coef[...] * (take(table, slot[...]) - temp_at[...])
+    rows, lanes = flux_out.shape
+    flux_out[...] = put([flux], cell[...], rows, lanes)[0]
+
+
+def run_wall(fluid_flat, outgoing, source, *rest):
     sizes = tuple(lax.axis_size(axis) for axis in AXES)
-    devices = sizes[0] * sizes[1] * sizes[2]
-    whole = pl.BlockSpec(memory_space=VMEM)
+    groups, kinds, width = outgoing.shape
+    size_x, size_y, size_z = source.shape
+    count_x = sizes[0]
+    block = pl.BlockSpec(memory_space=VMEM)
+    dma = pltpu.SemaphoreType.DMA
+
+    def f32(*shape):
+        return VMEM(shape, jnp.float32)
+
     return pl.pallas_call(
-        functools.partial(total_kernel, sizes),
-        out_shape=jax.ShapeDtypeStruct(values.shape, values.dtype),
-        in_specs=[whole],
-        out_specs=whole,
+        functools.partial(wall_kernel, sizes),
+        out_shape=(jax.ShapeDtypeStruct(source.shape, jnp.float32), jax.ShapeDtypeStruct(fluid_flat, jnp.float32)),
+        in_specs=[block] * (2 + len(rest)),
+        out_specs=(block, block),
         scratch_shapes=[
-            VMEM((devices,) + values.shape, values.dtype),
-            pltpu.SemaphoreType.DMA((devices,)),
-            pltpu.SemaphoreType.DMA((devices,)),
+            f32(groups, kinds, width), f32(groups, 1, width), f32(groups, 1, width),
+            f32(*source.shape), f32(*source.shape),
+            f32(3, 2, size_x, size_z), f32(3, 2, 8, size_x * size_y),
+            f32(3, 2, size_y, size_z), f32(3, 2, size_x, size_z), f32(3, 2, 8, size_x * size_y),
+            f32(8, size_z), f32(8, size_z), f32(count_x, 8, size_z), f32(groups, 8, size_z),
+            dma((2,)), dma((groups,)), dma((groups,)), dma((groups,)), dma((groups,)),
+            dma((3, 6)), dma((3, 6)), dma((count_x,)), dma((count_x,)), dma((groups,)), dma((groups,)),
         ],
         compiler_params=pltpu.CompilerParams(collective_id=0, has_side_effects=True),
-        name="total",
-    )(values)
-
-
-def neighbours(padded):
-    return (
-        padded[2:, 1:-1, 1:-1],
-        padded[:-2, 1:-1, 1:-1],
-        padded[1:-1, 2:, 1:-1],
-        padded[1:-1, :-2, 1:-1],
-        padded[1:-1, 1:-1, 2:],
-        padded[1:-1, 1:-1, :-2],
-    )
-
-
-def apply_operator(field, diagonal, weights):
-    padded = with_halo(field, (("gx", 0), ("gy", 1), ("gz", 2)), 1, False)
-    total = diagonal * field
-    for weight, other in zip(weights, neighbours(padded)):
-        total = total + weight * (field - other)
-    return total
+        name="wall",
+    )(outgoing, source, *rest)
 
 
 def per_device(
@@ -392,43 +478,17 @@
     dest = pair_dest[:, 0]
     onehot = (dest[:, None] == jnp.arange(groups, dtype=jnp.int32)[None, :]).astype(jnp.int32)
     rank = jnp.sum((jnp.cumsum(onehot, axis=0) - onehot) * onehot, axis=1)
-    slot = (dest * capacity + rank)[None, :]
+    width = -(-capacity // size_z) * size_z
+    slot = (dest * width + rank)[None, :]
     cell = pair_cell[None, :]
     coef = pair_coef[None, :]
     solid = pair_solid.astype(jnp.float32)[None, :]
-    slot_rows = groups * capacity // size_z
+    flat = (size_x * size_y, size_z)
     temp_at, outgoing = local_call(
-        send_kernel,
-        ((1, pair_count), (3, slot_rows, size_z)),
-        fluid_temp.reshape(size_x * size_y, size_z), cell, slot, coef, solid,
+        send_kernel, ((1, pair_count), (groups, 3, width)), fluid_temp.reshape(flat), cell, slot, coef, solid
     )
-    arrived = lax.all_to_all(
-        outgoing.reshape(3, groups, capacity), ("gy", "gz"), split_axis=1, concat_axis=1, tiled=True
-    ).reshape(3, groups * capacity)
-    solid_shape = solid_source.shape
-    flat = (solid_shape[0] * solid_shape[1], solid_shape[2])
-    gain, load = local_call(land_kernel, (flat, flat), arrived, solid_source.reshape(flat))
-    diagonal = ambient + gain.reshape(solid_shape)
-    residual = load.reshape(solid_shape)
-    conduct_pad = with_halo(conduct, (("gx", 0), ("gy", 1), ("gz", 2)), 1, False)
-    weights = [2.0 * conduct * other / (conduct + other) for other in neighbours(conduct_pad)]
-    image = apply_operator(residual, diagonal, weights)
-    twice = apply_operator(image, diagonal, weights)
-    sums = [jnp.sum(a * b, axis=(0, 1)) for a, b in ((residual, residual), (residual, image), (image, image), (image, twice))]
-    sums = total_over_devices(jnp.stack(sums + sums))
-    sums = jnp.sum(sums, axis=1)
-    norm, product, square, cross = sums[0], sums[1], sums[2], sums[3]
-    alpha = norm / product
-    norm_next = norm - 2.0 * alpha * product + alpha * alpha * square
-    product_next = product - 2.0 * alpha * square + alpha * alpha * cross
-    ratio = norm_next / norm
-    alpha_next = norm_next / (product_next - ratio * norm_next / alpha)
-    solid_temp = (alpha + alpha_next * (1.0 + ratio)) * residual - (alpha_next * alpha) * image
-
-    wall = local_call(wall_kernel, (1, groups * capacity), solid_temp.reshape(flat), arrived)
-    returned = lax.all_to_all(wall.reshape(groups, capacity), ("gy", "gz"), split_axis=0, concat_axis=0, tiled=True)
-    wall_flux = local_call(
-        flux_kernel, (size_x * size_y, size_z), returned.reshape(slot_rows, size_z), slot, cell, coef, temp_at
+    solid_temp, wall_flux = run_wall(
+        flat, outgoing, solid_source, ambient, conduct, slot, cell, coef, temp_at
     )
     return (fluid_temp, fluid_vel, solid_temp, wall_flux.reshape(size_x, size_y, size_z))
 

time: 166 us -> 87.5 us (0.53)
  starting transfers between devices: 58.2 us -> 7.84 us
  blocking collectives: 9.15 us -> 0 us
  between operations: 8.63 us -> 0.76 us
  waiting for transfers between devices: 13.9 us -> 8.68 us
  other arithmetic: 15.2 us -> 10.5 us
  local copies, waits for them, and re-layouts: 13.7 us -> 10 us
  Pallas kernels: 45.9 us -> 49.2 us
    ppermute x18 -> x0, starting transfers between devices: 47.1 us -> none  [the longest x9 35.5 us: with_halo(): lax.ppermute(tail, axis, [(i, (i + 1) % count) for i in range(ends)])]
    all_to_all x1 -> x0, blocking collectives: 9.15 us -> none  [per_device(): lax.all_to_all(wall.reshape(groups, capacity), ('gy', 'gz'), split_axis=0...]
    ppermute x18 -> x0, waiting for transfers between devices: 5.8 us -> none  [the longest x9 5.78 us: with_halo(): lax.ppermute(tail, axis, [(i, (i + 1) % count) for i in range(ends)])]
    pallas_call x5 -> x2, Pallas kernels: 29.2 us -> 32.6 us  [the longest x1 29.3 us: run_wall(): pl.pallas_call(functools.partial(wall_kernel, sizes), out_shape=(jax.Shap...]
    all_to_all x1 -> x0, starting transfers between devices: 3.34 us -> none  [per_device(): lax.all_to_all(outgoing.reshape(3, groups, capacity), ('gy', 'gz'), split...]
    slice x9 -> x1, local copies, waits for them, and re-layouts: 3.29 us -> 0.28 us  [the longest x4 1.5 us: with_halo(): head = lax.slice_in_dim(cells, 0, width, axis=dim)]
    unnamed x36 -> x22, local copies, waits for them, and re-layouts: 1.94 us -> 4.36 us
    concatenate x5 -> x0, other arithmetic: 1.71 us -> none  [with_halo(): jnp.concatenate([lax.ppermute(tail, axis, [(i, (i + 1) % count) for i in...]
  transfers between devices with their start and end apart: 25 -> 6, of which waited for: 9 -> 5; matrix products, arithmetic and copies ran while one was open for 9% -> 7% of each run, Pallas kernels for 2% -> 0%
where the time goes in v2:
time: 87.5 us; the launch traced here: 87 us
  Pallas kernels  49.2 us (56%)
  other arithmetic  10.5 us (12%)
  local copies, waits for them, and re-layouts  10 us (11%)
  waiting for transfers between devices  8.68 us (10%)
  starting transfers between devices  7.84 us (9%)
    pallas_call x1, Pallas kernels, run_wall(): pl.pallas_call(functools.partial(wall_kernel, sizes), out_shape=(jax.Shap...  29.3 us
    pallas_call x1, Pallas kernels, run_fluid(): pl.pallas_call(fluid_kernel, out_shape=(jax.ShapeDtypeStruct(shape, jnp.f...  16.6 us
    unnamed x22, local copies, waits for them, and re-layouts  4.36 us
    ppermute x2, waiting for transfers between devices, ring_halo(): lax.ppermute(head, axis, [((i + 1) % count, i) for i in range(count)])  4.02 us
    ppermute x2, waiting for transfers between devices, ring_halo(): lax.ppermute(tail, axis, [(i, (i + 1) % count) for i in range(count)])  3.78 us
    concatenate x2, other arithmetic, ring_halo(): jnp.concatenate([cells, after, jnp.ones(gap, cells.dtype), before], axis=...  3.43 us
    pallas_call x1, Pallas kernels, local_call(): pl.pallas_call(kernel, out_shape=tuple((jax.ShapeDtypeStruct(o, jnp.float...  3.29 us
    ppermute x1, starting transfers between devices, per_device(): lax.ppermute(fields[:, -HALO:], 'gx', [(i, (i + 1) % count) for i in rang...  3.1 us
  transfers between devices with their start and end apart: 6, of which 5 were waited for; matrix products, arithmetic and copies ran while one was open for 7% of the time, Pallas kernels for 0%

profile of v2, /device:TPU:0, one launch (start us, length us, event | category | flops | bytes accessed | tf_op | source)
XLA Modules:
  0.0 87.0 jit_solution(7402205656518158747)
XLA Ops:
  0.6 0.0 copy-start.3
  0.6 0.0 copy-start.2
  0.7 0.0 copy-start
  0.7 0.0 copy-start.8
  0.7 0.7 fusion.4
  1.4 0.1 broadcast_in_dim.25
  1.5 0.1 convert_element_type.24
  1.6 0.9 %pad_maximum_fusion.11 = (f32[6,2,16,128]{3,2,1,0:T(8,128)S(1)}, f32[6,2,16,128]{3,2,1,0:T(8,128)S(1)}) fusion(f32[1,16,16,128]{3,2,1,0:T(8,128)S(1)} %broadcast_in_dim.26, f32[1,16,16,128]{3,2,1,0:T(8,128)} %bitcast.33, f32[3,16,16,128]{3,2,1,0:T(8,128)} %param.12, f32[1,16,16,128]{3,2,1,0:T(8,128)} %bitcast.37), kind=kLoop, calls=%fused_computation.11 | loop fusion | flops 147456 | bytes 983040 | tf_op jit(solution)/shard_map/slice | solution.py:465
  2.5 3.1 %collective-permute-start = (f32[6,2,16,128]{3,2,1,0:T(8,128)S(1)}, f32[6,2,16,128]{3,2,1,0:T(8,128)S(1)}, u32[]{:S(2)}, u32[]{:S(2)}) collective-permute-start(f32[6,2,16,128]{3,2,1,0:T(8,128)S(1)} %get-tuple-element.20), channel_id=1, source_target_pairs={{0,8},{8,16},{16,24},{24,0},{1,9},{9,17},{17,25},{25,1},{2,10},{10... | collective-permute-start | bytes 294920 | tf_op jit(solution)/shard_map/ppermute | solution.py:465
  5.6 2.1 %collective-permute-start.1 = (f32[6,2,16,128]{3,2,1,0:T(8,128)S(1)}, f32[6,2,16,128]{3,2,1,0:T(8,128)S(1)}, u32[]{:S(2)}, u32[]{:S(2)}) collective-permute-start(f32[6,2,16,128]{3,2,1,0:T(8,128)S(1)} %get-tuple-element.21), channel_id=1, source_target_pairs={{8,0},{16,8},{24,16},{0,24},{9,1},{17,9},{25,17},{1,25},{10,2},{18... | collective-permute-start | bytes 294920 | tf_op jit(solution)/shard_map/ppermute | solution.py:467
  7.6 0.7 fusion.3
  8.3 2.3 %reduce-window.6 = s32[8,8,128]{2,1,0:T(8,128)S(1)} reduce-window(s32[8,8,128]{2,1,0:T(8,128)S(1)} %fusion.3, s32[]{:T(128)} %constant.12.clone.1), window={size=1x1x128 pad=0_0x0_0x127_0}, to_apply=%region_0.0 | reduce-window | flops 1040384 | bytes 65540 | tf_op jit(solution)/shard_map/reduce-window
  10.6 0.3 slice_reduce_fusion
  10.9 0.2 reduce-window.9
  11.0 0.0 collective-permute-done
  11.0 0.0 copy-start.4
  11.0 0.9 %collective-permute-done.1 = f32[6,2,16,128]{3,2,1,0:T(8,128)S(1)} collective-permute-done((f32[6,2,16,128]{3,2,1,0:T(8,128)S(1)}, f32[6,2,16,128]{3,2,1,0:T(8,128)S(1)}, u32[]{:S(2)}, u32[]{:S(2)}) %collective-permute-start.1) | collective-permute-done | bytes 98336 | tf_op jit(solution)/shard_map/ppermute | solution.py:467
  11.9 0.0 copy-done
  11.9 0.0 copy-start.5
  11.9 1.1 %pad_maximum_fusion.7 = (f32[6,20,2,128]{3,2,1,0:T(2,128)S(1)}, f32[6,20,2,128]{3,2,1,0:T(2,128)S(1)}) fusion(f32[6,2,16,128]{3,2,1,0:T(8,128)S(1)} %collective-permute-done.1, f32[6,2,16,128]{3,2,1,0:T(8,128)S(1)} %collective-permute-done, f32[1,16,16,128]{3,2,1,0:T(8,128)S(1)} %broadcast_in_dim.26, f32[1,16,16,128]{3,2,1,0:T(8,128)} %bitcast.34, ...), kind=kLoop, calls=%fused_computation.7 | loop fusion | flops 307200 | bytes 1228800 | tf_op jit(solution)/shard_map/slice | solution.py:48
  13.0 1.6 %collective-permute-start.2 = (f32[6,20,2,128]{3,2,1,0:T(2,128)S(1)}, f32[6,20,2,128]{3,2,1,0:T(2,128)S(1)}, u32[]{:S(2)}, u32[]{:S(2)}) collective-permute-start(f32[6,20,2,128]{3,2,1,0:T(2,128)S(1)} %get-tuple-element.18), channel_id=1, source_target_pairs={{4,0},{0,4},{5,1},{1,5},{6,2},{2,6},{7,3},{3,7},{12,8},{8,12},{13,... | collective-permute-start | bytes 368648 | tf_op jit(solution)/shard_map/ppermute | solution.py:50
  14.5 0.5 collective-permute-start.3
  15.1 0.1 add_bitcast_fusion
  15.1 0.0 copy-done.8
  15.2 3.9 %collective-permute-done.2 = f32[6,20,2,128]{3,2,1,0:T(2,128)S(1)} collective-permute-done((f32[6,20,2,128]{3,2,1,0:T(2,128)S(1)}, f32[6,20,2,128]{3,2,1,0:T(2,128)S(1)}, u32[]{:S(2)}, u32[]{:S(2)}) %collective-permute-start.2) | collective-permute-done | bytes 122912 | tf_op jit(solution)/shard_map/ppermute | solution.py:50
  19.0 0.0 copy-start.6
  19.0 1.3 %collective-permute-done.3 = f32[6,20,2,128]{3,2,1,0:T(2,128)S(1)} collective-permute-done((f32[6,20,2,128]{3,2,1,0:T(2,128)S(1)}, f32[6,20,2,128]{3,2,1,0:T(2,128)S(1)}, u32[]{:S(2)}, u32[]{:S(2)}) %collective-permute-start.3) | collective-permute-done | bytes 122912 | tf_op jit(solution)/shard_map/ppermute | solution.py:51
  20.4 0.0 copy-start.7
  20.4 0.0 copy-done.4
  20.4 0.0 copy-done.5
  20.4 0.0 copy-done.6
  20.4 0.6 copy-done.7
  21.0 0.0 copy-start.1
  21.0 0.7 copy-done.1
  21.7 0.0 copy-done.3
  21.7 0.0 copy-done.2
  21.7 0.2 pad_maximum_fusion.1
  21.9 0.5 fusion.5
  22.4 0.0 copy-start.9
  22.4 1.4 %copy.15 = f32[6,20,24,2]{2,3,1,0:T(2,128)} copy(f32[6,20,24,2]{3,2,1,0:T(8,128)S(1)} %get-tuple-element.16) | data formatting | bytes 46080 | tf_op jit(solution)/shard_map/slice | solution.py:48
  23.8 0.0 collective-permute-start.4
  23.8 0.8 copy.16
  24.6 0.5 collective-permute-start.5
  25.2 0.6 bitcast_add_fusion.slot
  25.8 0.0 copy-done.9
  25.8 0.6 convert_element_type.27
  26.4 0.1 pad.10.clone
  26.5 0.2 collective-permute-done.4
  26.6 0.8 copy.17
  27.4 2.5 %collective-permute-done.5 = f32[6,20,24,2]{2,3,1,0:T(2,128)} collective-permute-done((f32[6,20,24,2]{2,3,1,0:T(2,128)S(1)}, f32[6,20,24,2]{2,3,1,0:T(2,128)}, u32[]{:S(2)}, u32[]{:S(2)}) %collective-permute-start.5) | collective-permute-done | bytes 23072 | tf_op jit(solution)/shard_map/ppermute | solution.py:51
  29.9 1.7 %copy.18 = f32[6,20,24,2]{3,2,1,0:T(8,128)S(1)} copy(f32[6,20,24,2]{2,3,1,0:T(2,128)} %collective-permute-done.5) | data formatting | bytes 46080 | tf_op jit(solution)/shard_map/ppermute | solution.py:51
  31.5 3.2 %pad_maximum_fusion.fields = f32[6,20,24,256]{3,2,1,0:T(8,128)} fusion(f32[6,20,24,2]{3,2,1,0:T(8,128)S(1)} %copy.18, f32[6,20,24,2]{3,2,1,0:T(8,128)S(1)} %copy.17, f32[6,20,2,128]{3,2,1,0:T(2,128)} %copy-done.7, f32[6,20,4,128]{3,2,1,0:T(4,128)} %copy-done.1, f32[6,20,2,128]{3,2,1,0:T(2,128)} %copy-done.6, f32[6,2,16,128]{3,2,1,0:T(8,128)} %copy-done.5, ...), kind=kLoop, calls=%fused_computation | loop fusion | flops 8110080 | bytes 4470784 | tf_op jit(solution)/shard_map/concatenate | solution.py:54
  34.7 16.6 %fluid.1 = (f32[16,16,128]{2,1,0:T(8,128)}, f32[3,16,16,128]{3,2,1,0:T(8,128)}) custom-call(f32[6,20,24,256]{3,2,1,0:T(8,128)} %pad_maximum_fusion.fields), custom_call_target="tpu_custom_call" | custom-call | tf_op jit(solution)/shard_map/fluid/pallas_call | solution.py:170
  51.3 3.3 %send_kernel.1 = (f32[1,1024]{1,0:T(1,128)}, f32[8,3,256]{2,1,0:T(4,128)}) custom-call(f32[256,128]{1,0:T(8,128)} %bitcast.41, s32[1,1024]{1,0:T(1,128)} %bitcast.45, s32[1,1024]{1,0:T(1,128)} %bitcast_add_fusion.slot, f32[1,1024]{1,0:T(1,128)} %bitcast.47, f32[1,1024]{1,0:T(1,128)} %bitcast.50), custom_call_target="tpu_custom_call" | custom-call | tf_op jit(solution)/shard_map/send_kernel/pallas_call | solution.py:231
  54.6 29.3 %wall.1 = (f32[8,16,128]{2,1,0:T(8,128)}, f32[256,128]{1,0:T(8,128)}) custom-call(f32[8,3,256]{2,1,0:T(4,128)} %get-tuple-element.12.outgoing, f32[8,16,128]{2,1,0:T(8,128)} %source.1, f32[8,16,128]{2,1,0:T(8,128)} %ambient.1, f32[8,16,128]{2,1,0:T(8,128)} %conduct.1, s32[1,1024]{1,0:T(1,128)} %bitcast_add_fusion.slot, s32[1,1024]{1,0:T(1,128)} %bitcast.46, ...), custom_call_target="tpu_custom_call" | custom-call | tf_op jit(solution)/shard_map/wall/pallas_call | solution.py:422
  83.9 1.5 %copy.23 = f32[8,16,128]{2,1,0:T(8,128)} copy(f32[8,16,128]{2,1,0:T(8,128)} %get-tuple-element.28) | data formatting | bytes 131072
  85.4 1.6 %copy.24 = f32[16,16,128]{2,1,0:T(8,128)} copy(f32[16,16,128]{2,1,0:T(8,128)} %bitcast.42) | data formatting | bytes 262144
  (4 shorter events, 0.1 us)
Async XLA Ops:
  0.6 21.1 %copy-start.3 = (f32[16,16,128]{2,1,0:T(8,128)S(1)}, f32[16,16,128]{2,1,0:T(8,128)}, u32[]{:S(2)}) copy-start(f32[16,16,128]{2,1,0:T(8,128)} %param.11) | copy-start | bytes 393220
  0.6 21.1 %copy-start.2 = (f32[16,16,128]{2,1,0:T(8,128)S(1)}, f32[16,16,128]{2,1,0:T(8,128)}, u32[]{:S(2)}) copy-start(f32[16,16,128]{2,1,0:T(8,128)} %param.13) | copy-start | bytes 393220
  0.7 11.3 %copy-start = (f32[3,16,16,128]{3,2,1,0:T(8,128)S(1)}, f32[3,16,16,128]{3,2,1,0:T(8,128)}, u32[]{:S(2)}) copy-start(f32[3,16,16,128]{3,2,1,0:T(8,128)} %param.12) | copy-start | bytes 1179652
  0.7 14.5 %copy-start.8 = (s32[1024,1]{0,1:T(1,128)S(1)}, s32[1024,1]{0,1:T(1,128)}, u32[]{:S(2)}) copy-start(s32[1024,1]{0,1:T(1,128)} %param.19) | copy-start | bytes 12292
  2.5 8.6 %collective-permute-start = (f32[6,2,16,128]{3,2,1,0:T(8,128)S(1)}, f32[6,2,16,128]{3,2,1,0:T(8,128)S(1)}, u32[]{:S(2)}, u32[]{:S(2)}) collective-permute-start(f32[6,2,16,128]{3,2,1,0:T(8,128)S(1)} %get-tuple-element.20), channel_id=1, source_target_pairs={{0,8},{8,16},{16,24},{24,0},{1,9},{9,17},{17,25},{25,1},{2,10},{10... | collective-permute-start | bytes 294920 | tf_op jit(solution)/shard_map/ppermute | solution.py:465
  5.6 6.4 %collective-permute-start.1 = (f32[6,2,16,128]{3,2,1,0:T(8,128)S(1)}, f32[6,2,16,128]{3,2,1,0:T(8,128)S(1)}, u32[]{:S(2)}, u32[]{:S(2)}) collective-permute-start(f32[6,2,16,128]{3,2,1,0:T(8,128)S(1)} %get-tuple-element.21), channel_id=1, source_target_pairs={{8,0},{16,8},{24,16},{0,24},{9,1},{17,9},{25,17},{1,25},{10,2},{18... | collective-permute-start | bytes 294920 | tf_op jit(solution)/shard_map/ppermute | solution.py:467
  11.0 9.4 %copy-start.4 = (f32[6,2,16,128]{3,2,1,0:T(8,128)}, f32[6,2,16,128]{3,2,1,0:T(8,128)S(1)}, u32[]{:S(2)}) copy-start(f32[6,2,16,128]{3,2,1,0:T(8,128)S(1)} %collective-permute-done) | copy-start | bytes 294916
  11.9 8.5 %copy-start.5 = (f32[6,2,16,128]{3,2,1,0:T(8,128)}, f32[6,2,16,128]{3,2,1,0:T(8,128)S(1)}, u32[]{:S(2)}) copy-start(f32[6,2,16,128]{3,2,1,0:T(8,128)S(1)} %collective-permute-done.1) | copy-start | bytes 294916
  13.0 6.1 %collective-permute-start.2 = (f32[6,20,2,128]{3,2,1,0:T(2,128)S(1)}, f32[6,20,2,128]{3,2,1,0:T(2,128)S(1)}, u32[]{:S(2)}, u32[]{:S(2)}) collective-permute-start(f32[6,20,2,128]{3,2,1,0:T(2,128)S(1)} %get-tuple-element.18), channel_id=1, source_target_pairs={{4,0},{0,4},{5,1},{1,5},{6,2},{2,6},{7,3},{3,7},{12,8},{8,12},{13,... | collective-permute-start | bytes 368648 | tf_op jit(solution)/shard_map/ppermute | solution.py:50
  14.5 5.8 %collective-permute-start.3 = (f32[6,20,2,128]{3,2,1,0:T(2,128)S(1)}, f32[6,20,2,128]{3,2,1,0:T(2,128)S(1)}, u32[]{:S(2)}, u32[]{:S(2)}) collective-permute-start(f32[6,20,2,128]{3,2,1,0:T(2,128)S(1)} %get-tuple-element.19), channel_id=1, source_target_pairs={{0,4},{4,0},{1,5},{5,1},{2,6},{6,2},{3,7},{7,3},{8,12},{12,8},{9,1... | collective-permute-start | bytes 368648 | tf_op jit(solution)/shard_map/ppermute | solution.py:51
  19.0 1.4 %copy-start.6 = (f32[6,20,2,128]{3,2,1,0:T(2,128)}, f32[6,20,2,128]{3,2,1,0:T(2,128)S(1)}, u32[]{:S(2)}) copy-start(f32[6,20,2,128]{3,2,1,0:T(2,128)S(1)} %collective-permute-done.2) | copy-start | bytes 368644
  20.4 0.6 copy-start.7
  21.0 0.7 copy-start.1
  22.4 3.4 %copy-start.9 = (s32[1024]{0:T(1024)S(1)}, s32[1024]{0:T(1024)}, u32[]{:S(2)}) copy-start(s32[1024]{0:T(1024)} %param.20) | copy-start | bytes 12292
  23.8 2.8 %collective-permute-start.4 = (f32[6,20,24,2]{2,3,1,0:T(2,128)}, f32[6,20,24,2]{2,3,1,0:T(2,128)S(1)}, u32[]{:S(2)}, u32[]{:S(2)}) collective-permute-start(f32[6,20,24,2]{2,3,1,0:T(2,128)} %copy.15), channel_id=1, source_target_pairs={{1,0},{2,1},{3,2},{0,3},{5,4},{6,5},{7,6},{4,7},{9,8},{10,9},{11,1... | collective-permute-start | bytes 69128 | tf_op jit(solution)/shard_map/ppermute | solution.py:50
  24.6 5.2 %collective-permute-start.5 = (f32[6,20,24,2]{2,3,1,0:T(2,128)S(1)}, f32[6,20,24,2]{2,3,1,0:T(2,128)}, u32[]{:S(2)}, u32[]{:S(2)}) collective-permute-start(f32[6,20,24,2]{2,3,1,0:T(2,128)S(1)} %copy.16), channel_id=1, source_target_pairs={{0,1},{1,2},{2,3},{3,0},{4,5},{5,6},{6,7},{7,4},{8,9},{9,10},{10,1... | collective-permute-start | bytes 69128 | tf_op jit(solution)/shard_map/ppermute | solution.py:51

commit v3 on v2

--- a/solution.py
+++ b/solution.py
@@ -42,16 +42,120 @@
 VMEM = pltpu.VMEM
 
 
-def ring_halo(cells, axis, dim, total):
-    count = lax.axis_size(axis)
-    size = cells.shape[dim]
-    head = lax.slice_in_dim(cells, 0, HALO, axis=dim)
-    tail = lax.slice_in_dim(cells, size - HALO, size, axis=dim)
-    after = lax.ppermute(head, axis, [((i + 1) % count, i) for i in range(count)])
-    before = lax.ppermute(tail, axis, [(i, (i + 1) % count) for i in range(count)])
-    gap = list(cells.shape)
-    gap[dim] = total - size - 2 * HALO
-    return jnp.concatenate([cells, after, jnp.ones(gap, cells.dtype), before], axis=dim)
+def halo_kernel(sizes, cells, fields, got_x, pack_y, got_y, pack_z, got_z, send_sem, recv_sem):
+    kinds, size_x, size_y, size_z = cells.shape
+    planes = fields.shape[1]
+    spots = [lax.axis_index(axis) for axis in AXES]
+    mesh = pl.DeviceIdType.MESH
+
+    def beside(axis, step):
+        moved = list(spots)
+        moved[axis] = lax.rem(spots[axis] + (sizes[axis] + step), sizes[axis])
+        return tuple(moved)
+
+    barrier = pltpu.get_barrier_semaphore()
+    for axis in range(3):
+        for step in (1, -1):
+            pl.semaphore_signal(barrier, inc=1, device_id=beside(axis, step), device_id_type=mesh)
+    pl.semaphore_wait(barrier, 6)
+
+    def both(axis, up, down, got):
+        copies = [
+            pltpu.make_async_remote_copy(
+                src_ref=src, dst_ref=got.at[side], send_sem=send_sem.at[axis, side], recv_sem=recv_sem.at[axis, side],
+                device_id=beside(axis, step), device_id_type=mesh,
+            )
+            for side, (src, step) in enumerate(((up, 1), (down, -1)))
+        ]
+        if sizes[axis] == 2 and up is down:
+            copies = copies[:1]
+        for copy in copies:
+            copy.start()
+        return copies
+
+    def finish(copies):
+        for copy in copies:
+            copy.wait()
+
+    copies = both(0, cells.at[:, pl.ds(size_x - HALO, HALO)], cells.at[:, pl.ds(0, HALO)], got_x)
+    for kind in range(kinds):
+        fields[kind, HALO : HALO + size_x, :size_y, :size_z] = cells[kind]
+    finish(copies)
+    for kind in range(kinds):
+        fields[kind, :HALO, :size_y, :size_z] = got_x[0, kind]
+        fields[kind, HALO + size_x :, :size_y, :size_z] = got_x[1, kind]
+
+    row = lax.broadcasted_iota(jnp.int32, (8, size_z), 0)
+
+    def ends(kind, plane):
+        return jnp.where(row < 4, fields[kind, plane, 0:8, :size_z], fields[kind, plane, size_y - 8 : size_y, :size_z])
+
+    for kind in range(kinds):
+
+        def pack(pair, carry):
+            even = pltpu.roll(ends(kind, 2 * pair), 2, 0)
+            odd = pltpu.roll(ends(kind, 2 * pair + 1), 6, 0)
+            pack_y[kind, pair] = jnp.where(row < 4, even, odd)
+            return carry
+
+        lax.fori_loop(0, planes // 2, pack, 0, unroll=True)
+    copies = both(1, pack_y, pack_y, got_y)
+    finish(copies)
+    next_y = 1 if len(copies) == 2 else 0
+    for kind in range(kinds):
+
+        def unpack(pair, carry):
+            mixed = jnp.where(row % 4 < 2, got_y[0, kind, pair], got_y[next_y, kind, pair])
+            fields[kind, 2 * pair, size_y:, :size_z] = pltpu.roll(mixed, 6, 0)
+            fields[kind, 2 * pair + 1, size_y:, :size_z] = pltpu.roll(mixed, 2, 0)
+            return carry
+
+        lax.fori_loop(0, planes // 2, unpack, 0, unroll=True)
+
+    per = size_z // 4
+    lane = lax.broadcasted_iota(jnp.int32, (size_y + 8, size_z), 1)
+    for group in range(pack_z.shape[0]):
+        total = jnp.zeros((size_y + 8, size_z), jnp.float32)
+        for spot in range(min(per, kinds * planes - group * per)):
+            kind, plane = divmod(group * per + spot, planes)
+            moved = pltpu.roll(fields[kind, plane, :, :size_z], (4 * spot + 2) % size_z, 1)
+            total = jnp.where(lane // 4 == spot, moved, total)
+        pack_z[group] = total
+    copies = both(2, pack_z, pack_z, got_z)
+    finish(copies)
+    next_z = 1 if len(copies) == 2 else 0
+    for group in range(pack_z.shape[0]):
+        mixed = jnp.where(lane % 4 < 2, got_z[0, group], got_z[next_z, group])
+        for spot in range(min(per, kinds * planes - group * per)):
+            kind, plane = divmod(group * per + spot, planes)
+            fields[kind, plane, :, size_z:] = pltpu.roll(mixed, (size_z - 4 * spot - 2) % size_z, 1)
+
+
+def run_halo(cells):
+    sizes = tuple(lax.axis_size(axis) for axis in AXES)
+    kinds, size_x, size_y, size_z = cells.shape
+    planes = size_x + 2 * HALO
+    groups = -(-kinds * planes // (size_z // 4))
+    block = pl.BlockSpec(memory_space=VMEM)
+    dma = pltpu.SemaphoreType.DMA
+
+    def f32(*shape):
+        return VMEM(shape, jnp.float32)
+
+    return pl.pallas_call(
+        functools.partial(halo_kernel, sizes),
+        out_shape=jax.ShapeDtypeStruct((kinds, planes, size_y + 8, 2 * size_z), jnp.float32),
+        in_specs=[block],
+        out_specs=block,
+        scratch_shapes=[
+            f32(2, kinds, HALO, size_y, size_z),
+            f32(kinds, planes // 2, 8, size_z), f32(2, kinds, planes // 2, 8, size_z),
+            f32(groups, size_y + 8, size_z), f32(2, groups, size_y + 8, size_z),
+            dma((3, 2)), dma((3, 2)),
+        ],
+        compiler_params=pltpu.CompilerParams(collective_id=1, has_side_effects=True),
+        name="halo",
+    )(cells)
 
 
 def along_of(which, speed):
@@ -459,17 +563,7 @@
     fields = jnp.stack(
         [density_start, velocity_start[0], velocity_start[1], velocity_start[2], temp_start, fine.astype(jnp.float32)]
     )
-    count = lax.axis_size("gx")
-    fields = jnp.concatenate(
-        [
-            lax.ppermute(fields[:, -HALO:], "gx", [(i, (i + 1) % count) for i in range(count)]),
-            fields,
-            lax.ppermute(fields[:, :HALO], "gx", [((i + 1) % count, i) for i in range(count)]),
-        ],
-        axis=1,
-    )
-    fields = ring_halo(fields, "gy", 2, size_y + 8)
-    fields = ring_halo(fields, "gz", 3, size_z + 128)
+    fields = run_halo(fields)
     fluid_temp, fluid_vel = run_fluid(fields, (size_x, size_y, size_z))
 
     groups = lax.axis_size(("gy", "gz"))

time: 87.5 us -> 84.1 us (0.961)
  Pallas kernels: 49.2 us -> 73.2 us
  waiting for transfers between devices: 8.68 us -> 0 us
  starting transfers between devices: 7.84 us -> 0 us
  local copies, waits for them, and re-layouts: 10 us -> 3.5 us
  other arithmetic: 10.5 us -> 6.46 us
    pallas_call x0 -> x1, Pallas kernels: none -> 23 us  [run_halo(): pl.pallas_call(functools.partial(halo_kernel, sizes), out_shape=jax.Shape...]
    ppermute x6 -> x0, waiting for transfers between devices: 8.68 us -> none  [the longest x2 4.02 us: ring_halo(): lax.ppermute(head, axis, [((i + 1) % count, i) for i in range(count)])]
    ppermute x6 -> x0, starting transfers between devices: 7.84 us -> none  [the longest x1 3.1 us: per_device(): lax.ppermute(fields[:, -HALO:], 'gx', [(i, (i + 1) % count) for i in rang...]
    concatenate x2 -> x0, other arithmetic: 3.43 us -> none  [ring_halo(): jnp.concatenate([cells, after, jnp.ones(gap, cells.dtype), before], axis=...]
    slice x4 -> x1, local copies, waits for them, and re-layouts: 2.96 us -> 0.28 us  [the longest x2 1.89 us: ring_halo(): head = lax.slice_in_dim(cells, 0, HALO, axis=dim)]
    ppermute x2 -> x0, local copies, waits for them, and re-layouts: 2.44 us -> none  [the longest x1 1.67 us: ring_halo(): lax.ppermute(tail, axis, [(i, (i + 1) % count) for i in range(count)])]
    another operation x2 -> x3, other arithmetic: 2.41 us -> 4.49 us
    slice x2 -> x0, other arithmetic: 1.94 us -> none  [the longest x1 1.06 us: ring_halo(): head = lax.slice_in_dim(cells, 0, HALO, axis=dim)]
  transfers between devices with their start and end apart: 6 -> 0, of which waited for: 5 -> 0; matrix products, arithmetic and copies ran while one was open for 7% -> 0% of each run, Pallas kernels for 0% -> 0%
where the time goes in v3:
time: 84.1 us; the launch traced here: 83.8 us
  Pallas kernels  73.2 us (87%)
  other arithmetic  6.46 us (8%)
  local copies, waits for them, and re-layouts  3.5 us (4%)
    pallas_call x1, Pallas kernels, run_wall(): pl.pallas_call(functools.partial(wall_kernel, sizes), out_shape=(jax.Shap...  30.3 us
    pallas_call x1, Pallas kernels, run_halo(): pl.pallas_call(functools.partial(halo_kernel, sizes), out_shape=jax.Shape...  23 us
    pallas_call x1, Pallas kernels, run_fluid(): pl.pallas_call(fluid_kernel, out_shape=(jax.ShapeDtypeStruct(shape, jnp.f...  16.6 us
    pallas_call x1, Pallas kernels, local_call(): pl.pallas_call(kernel, out_shape=tuple((jax.ShapeDtypeStruct(o, jnp.float...  3.29 us
    unnamed x6, local copies, waits for them, and re-layouts  3.05 us
    another operation x2, other arithmetic  2.43 us
    another operation x1, other arithmetic, per_device(): jnp.stack([density_start, velocity_start[0], velocity_start[1], velocity_...  2.06 us

profile of v3, /device:TPU:0, one launch (start us, length us, event | category | flops | bytes accessed | tf_op | source)
XLA Modules:
  0.0 83.8 jit_solution(17332852094792785426)
XLA Ops:
  0.6 0.7 fusion.4
  1.3 0.1 broadcast_in_dim.19
  1.4 0.1 convert_element_type.24
  1.5 2.1 %pad_maximum_fusion.cells = f32[6,16,16,128]{3,2,1,0:T(8,128)} fusion(f32[1,16,16,128]{3,2,1,0:T(8,128)S(1)} %broadcast_in_dim.20, f32[1,16,16,128]{3,2,1,0:T(8,128)} %bitcast.33, f32[3,16,16,128]{3,2,1,0:T(8,128)} %param.12, f32[1,16,16,128]{3,2,1,0:T(8,128)} %bitcast.34), kind=kLoop, calls=%fused_computation | loop fusion | flops 589824 | bytes 1572864 | tf_op jit(solution)/shard_map/stack | solution.py:563
  3.5 0.0 copy-start
  3.5 0.0 copy-start.1
  3.5 23.0 %halo.1.fields = f32[6,20,24,256]{3,2,1,0:T(8,128)} custom-call(f32[6,16,16,128]{3,2,1,0:T(8,128)} %pad_maximum_fusion.cells), custom_call_target="tpu_custom_call" | custom-call | tf_op jit(solution)/shard_map/halo/pallas_call | solution.py:145
  26.5 16.6 %fluid.1 = (f32[16,16,128]{2,1,0:T(8,128)}, f32[3,16,16,128]{3,2,1,0:T(8,128)}) custom-call(f32[6,20,24,256]{3,2,1,0:T(8,128)} %halo.1.fields), custom_call_target="tpu_custom_call" | custom-call | tf_op jit(solution)/shard_map/fluid/pallas_call | solution.py:274
  43.1 0.0 copy-done
  43.1 2.3 %reduce-window.6 = s32[8,8,128]{2,1,0:T(8,128)S(1)} reduce-window(s32[8,8,128]{2,1,0:T(8,128)S(1)} %fusion.3, s32[]{:T(128)} %constant.9.clone.1), window={size=1x1x128 pad=0_0x0_0x127_0}, to_apply=%region_0.0 | reduce-window | flops 1040384 | bytes 65540 | tf_op jit(solution)/shard_map/reduce-window
  45.4 0.3 slice_reduce_fusion
  45.7 0.2 reduce-window.9
  45.9 0.1 add_bitcast_fusion
  46.0 0.6 bitcast_add_fusion.slot
  46.6 0.0 copy-done.1
  46.6 0.6 convert_element_type.27
  47.2 3.3 %send_kernel.1 = (f32[1,1024]{1,0:T(1,128)}, f32[8,3,256]{2,1,0:T(4,128)}) custom-call(f32[256,128]{1,0:T(8,128)} %bitcast.35, s32[1,1024]{1,0:T(1,128)} %bitcast.39, s32[1,1024]{1,0:T(1,128)} %bitcast_add_fusion.slot, f32[1,1024]{1,0:T(1,128)} %bitcast.41, f32[1,1024]{1,0:T(1,128)} %bitcast.45), custom_call_target="tpu_custom_call" | custom-call | tf_op jit(solution)/shard_map/send_kernel/pallas_call | solution.py:335
  50.5 30.3 %wall.1 = (f32[8,16,128]{2,1,0:T(8,128)}, f32[256,128]{1,0:T(8,128)}) custom-call(f32[8,3,256]{2,1,0:T(4,128)} %get-tuple-element.12.outgoing, f32[8,16,128]{2,1,0:T(8,128)} %source.1, f32[8,16,128]{2,1,0:T(8,128)} %ambient.1, f32[8,16,128]{2,1,0:T(8,128)} %conduct.1, s32[1,1024]{1,0:T(1,128)} %bitcast_add_fusion.slot, s32[1,1024]{1,0:T(1,128)} %bitcast.40, ...), custom_call_target="tpu_custom_call" | custom-call | tf_op jit(solution)/shard_map/wall/pallas_call | solution.py:526
  80.8 1.5 %copy.19 = f32[8,16,128]{2,1,0:T(8,128)} copy(f32[8,16,128]{2,1,0:T(8,128)} %get-tuple-element.22) | data formatting | bytes 131072
  82.2 1.6 %copy.20 = f32[16,16,128]{2,1,0:T(8,128)} copy(f32[16,16,128]{2,1,0:T(8,128)} %bitcast.36) | data formatting | bytes 262144
  (3 shorter events, 0.0 us)
Async XLA Ops:
  3.5 39.6 %copy-start = (s32[1024,1]{0,1:T(1,128)S(1)}, s32[1024,1]{0,1:T(1,128)}, u32[]{:S(2)}) copy-start(s32[1024,1]{0,1:T(1,128)} %param.19) | copy-start | bytes 12292
  3.5 43.1 %copy-start.1 = (s32[1024]{0:T(1024)S(1)}, s32[1024]{0:T(1024)}, u32[]{:S(2)}) copy-start(s32[1024]{0:T(1024)} %param.20) | copy-start | bytes 12292

commit v4 on v3

--- a/solution.py
+++ b/solution.py
@@ -42,9 +42,12 @@
 VMEM = pltpu.VMEM
 
 
-def halo_kernel(sizes, cells, fields, got_x, pack_y, got_y, pack_z, got_z, send_sem, recv_sem):
-    kinds, size_x, size_y, size_z = cells.shape
-    planes = fields.shape[1]
+def halo_kernel(
+    sizes, density, velocity, temper, fine, fields,
+    got_x, pack_y, got_y, pack_c, got_c, pack_z, got_z, send_sem, recv_sem,
+):
+    size_x, size_y, size_z = density.shape
+    kinds, planes = fields.shape[:2]
     spots = [lax.axis_index(axis) for axis in AXES]
     mesh = pl.DeviceIdType.MESH
 
@@ -59,16 +62,15 @@
             pl.semaphore_signal(barrier, inc=1, device_id=beside(axis, step), device_id_type=mesh)
     pl.semaphore_wait(barrier, 6)
 
-    def both(axis, up, down, got):
+    def both(number, axis, up, down, got):
         copies = [
             pltpu.make_async_remote_copy(
-                src_ref=src, dst_ref=got.at[side], send_sem=send_sem.at[axis, side], recv_sem=recv_sem.at[axis, side],
+                src_ref=src, dst_ref=dst, send_sem=send_sem.at[number, side], recv_sem=recv_sem.at[number, side],
                 device_id=beside(axis, step), device_id_type=mesh,
             )
-            for side, (src, step) in enumerate(((up, 1), (down, -1)))
+            for side, (src, dst, step) in enumerate(((up, got[0], 1), (down, got[1], -1)))
+            if side == 0 or sizes[axis] > 2 or up is not down
         ]
-        if sizes[axis] == 2 and up is down:
-            copies = copies[:1]
         for copy in copies:
             copy.start()
         return copies
@@ -77,40 +79,54 @@
         for copy in copies:
             copy.wait()
 
-    copies = both(0, cells.at[:, pl.ds(size_x - HALO, HALO)], cells.at[:, pl.ds(0, HALO)], got_x)
+    low, high = pl.ds(0, HALO), pl.ds(size_x - HALO, HALO)
+    copies_x = []
+    for number, (field, kind) in enumerate(((density, 0), (temper, 4), (fine, 5))):
+        copies_x += both(number, 0, field.at[high], field.at[low], [got_x.at[side, kind] for side in range(2)])
+    copies_x += both(
+        3, 0, velocity.at[:, high], velocity.at[:, low], [got_x.at[side, pl.ds(1, 3)] for side in range(2)]
+    )
+    for kind, field in ((0, density), (4, temper), (5, fine)):
+        fields[kind, HALO : HALO + size_x, :size_y, :size_z] = field[...]
+    for kind in range(3):
+        fields[kind + 1, HALO : HALO + size_x, :size_y, :size_z] = velocity[kind]
+
+    row = lax.broadcasted_iota(jnp.int32, (8, size_z), 0)
+
+    def packed(kind, plane):
+        ends = [
+            jnp.where(row < 4, fields[kind, at, 0:8, :size_z], fields[kind, at, size_y - 8 : size_y, :size_z])
+            for at in (plane, plane + 1)
+        ]
+        return jnp.where(row < 4, pltpu.roll(ends[0], 2, 0), pltpu.roll(ends[1], 6, 0))
+
+    def unpacked(kind, plane, below, above):
+        mixed = jnp.where(row % 4 < 2, below, above)
+        fields[kind, plane, size_y:, :size_z] = pltpu.roll(mixed, 6, 0)
+        fields[kind, plane + 1, size_y:, :size_z] = pltpu.roll(mixed, 2, 0)
+
     for kind in range(kinds):
-        fields[kind, HALO : HALO + size_x, :size_y, :size_z] = cells[kind]
-    finish(copies)
+        for pair in range(size_x // 2):
+            pack_y[kind, pair] = packed(kind, HALO + 2 * pair)
+    copies_y = both(4, 1, pack_y, pack_y, [got_y.at[side] for side in range(2)])
+    finish(copies_x)
     for kind in range(kinds):
         fields[kind, :HALO, :size_y, :size_z] = got_x[0, kind]
         fields[kind, HALO + size_x :, :size_y, :size_z] = got_x[1, kind]
-
-    row = lax.broadcasted_iota(jnp.int32, (8, size_z), 0)
-
-    def ends(kind, plane):
-        return jnp.where(row < 4, fields[kind, plane, 0:8, :size_z], fields[kind, plane, size_y - 8 : size_y, :size_z])
-
+    corners = (0, HALO + size_x)
     for kind in range(kinds):
-
-        def pack(pair, carry):
-            even = pltpu.roll(ends(kind, 2 * pair), 2, 0)
-            odd = pltpu.roll(ends(kind, 2 * pair + 1), 6, 0)
-            pack_y[kind, pair] = jnp.where(row < 4, even, odd)
-            return carry
-
-        lax.fori_loop(0, planes // 2, pack, 0, unroll=True)
-    copies = both(1, pack_y, pack_y, got_y)
-    finish(copies)
-    next_y = 1 if len(copies) == 2 else 0
+        for corner, plane in enumerate(corners):
+            pack_c[kind, corner] = packed(kind, plane)
+    copies_c = both(5, 1, pack_c, pack_c, [got_c.at[side] for side in range(2)])
+    next_y = len(copies_y) - 1
+    finish(copies_y)
     for kind in range(kinds):
-
-        def unpack(pair, carry):
-            mixed = jnp.where(row % 4 < 2, got_y[0, kind, pair], got_y[next_y, kind, pair])
-            fields[kind, 2 * pair, size_y:, :size_z] = pltpu.roll(mixed, 6, 0)
-            fields[kind, 2 * pair + 1, size_y:, :size_z] = pltpu.roll(mixed, 2, 0)
-            return carry
-
-        lax.fori_loop(0, planes // 2, unpack, 0, unroll=True)
+        for pair in range(size_x // 2):
+            unpacked(kind, HALO + 2 * pair, got_y[0, kind, pair], got_y[next_y, kind, pair])
+    finish(copies_c)
+    for kind in range(kinds):
+        for corner, plane in enumerate(corners):
+            unpacked(kind, plane, got_c[0, kind, corner], got_c[next_y, kind, corner])
 
     per = size_z // 4
     lane = lax.broadcasted_iota(jnp.int32, (size_y + 8, size_z), 1)
@@ -121,9 +137,9 @@
             moved = pltpu.roll(fields[kind, plane, :, :size_z], (4 * spot + 2) % size_z, 1)
             total = jnp.where(lane // 4 == spot, moved, total)
         pack_z[group] = total
-    copies = both(2, pack_z, pack_z, got_z)
+    copies = both(6, 2, pack_z, pack_z, [got_z.at[side] for side in range(2)])
     finish(copies)
-    next_z = 1 if len(copies) == 2 else 0
+    next_z = len(copies) - 1
     for group in range(pack_z.shape[0]):
         mixed = jnp.where(lane % 4 < 2, got_z[0, group], got_z[next_z, group])
         for spot in range(min(per, kinds * planes - group * per)):
@@ -131,9 +147,10 @@
             fields[kind, plane, :, size_z:] = pltpu.roll(mixed, (size_z - 4 * spot - 2) % size_z, 1)
 
 
-def run_halo(cells):
+def run_halo(density, velocity, temper, fine):
     sizes = tuple(lax.axis_size(axis) for axis in AXES)
-    kinds, size_x, size_y, size_z = cells.shape
+    size_x, size_y, size_z = density.shape
+    kinds = 6
     planes = size_x + 2 * HALO
     groups = -(-kinds * planes // (size_z // 4))
     block = pl.BlockSpec(memory_space=VMEM)
@@ -145,17 +162,18 @@
     return pl.pallas_call(
         functools.partial(halo_kernel, sizes),
         out_shape=jax.ShapeDtypeStruct((kinds, planes, size_y + 8, 2 * size_z), jnp.float32),
-        in_specs=[block],
+        in_specs=[block] * 4,
         out_specs=block,
         scratch_shapes=[
             f32(2, kinds, HALO, size_y, size_z),
-            f32(kinds, planes // 2, 8, size_z), f32(2, kinds, planes // 2, 8, size_z),
+            f32(kinds, size_x // 2, 8, size_z), f32(2, kinds, size_x // 2, 8, size_z),
+            f32(kinds, 2, 8, size_z), f32(2, kinds, 2, 8, size_z),
             f32(groups, size_y + 8, size_z), f32(2, groups, size_y + 8, size_z),
-            dma((3, 2)), dma((3, 2)),
+            dma((7, 2)), dma((7, 2)),
         ],
         compiler_params=pltpu.CompilerParams(collective_id=1, has_side_effects=True),
         name="halo",
-    )(cells)
+    )(density, velocity, temper, fine)
 
 
 def along_of(which, speed):
@@ -320,10 +338,22 @@
     return outs
 
 
-def send_kernel(temp, cell, slot, coef, solid, temp_at, outgoing):
+def send_kernel(temp, cell, dest, coef, solid, temp_at, outgoing, slot):
     got = take(temp[...], cell[...])
     temp_at[...] = got
     groups, kinds, width = outgoing.shape
+    span = temp.shape[1]
+    named = one_hot(dest[...], groups).astype(jnp.float32)
+    earlier = lax.broadcasted_iota(jnp.int32, (span, span), 0) < lax.broadcasted_iota(jnp.int32, (span, span), 1)
+    earlier = earlier.astype(jnp.float32).astype(jnp.bfloat16)
+    before = jnp.zeros((groups, 1), jnp.float32)
+    ranks = []
+    for start in range(0, named.shape[1], span):
+        here = named[:, start : start + span]
+        ahead = jnp.dot(here.astype(jnp.bfloat16), earlier, preferred_element_type=jnp.float32) + before
+        ranks.append(jnp.sum(ahead * here, axis=0, keepdims=True))
+        before = before + jnp.sum(here, axis=1, keepdims=True)
+    slot[...] = dest[...] * width + jnp.concatenate(ranks, axis=1).astype(jnp.int32)
     filled = put([got, coef[...], solid[...]], slot[...], groups, width)
     for which in range(kinds):
         for group in range(groups):
@@ -334,7 +364,7 @@
     whole = pl.BlockSpec(memory_space=VMEM)
     return pl.pallas_call(
         kernel,
-        out_shape=tuple(jax.ShapeDtypeStruct(o, jnp.float32) for o in outs),
+        out_shape=tuple(jax.ShapeDtypeStruct(*o) for o in outs),
         in_specs=[whole] * len(args),
         out_specs=(whole,) * len(outs),
         name=kernel.__name__,
@@ -560,26 +590,22 @@
     fine = jnp.broadcast_to(
         (block_level == 1)[:, None, :, None, :, None], (blocks_x, BLK, blocks_y, BLK, blocks_z, BLK)
     ).reshape(size_x, size_y, size_z)
-    fields = jnp.stack(
-        [density_start, velocity_start[0], velocity_start[1], velocity_start[2], temp_start, fine.astype(jnp.float32)]
-    )
-    fields = run_halo(fields)
+    fields = run_halo(density_start, velocity_start, temp_start, fine.astype(jnp.float32))
     fluid_temp, fluid_vel = run_fluid(fields, (size_x, size_y, size_z))
 
     groups = lax.axis_size(("gy", "gz"))
     pair_count = pair_cell.shape[0]
     capacity = 2 * pair_count // groups
-    dest = pair_dest[:, 0]
-    onehot = (dest[:, None] == jnp.arange(groups, dtype=jnp.int32)[None, :]).astype(jnp.int32)
-    rank = jnp.sum((jnp.cumsum(onehot, axis=0) - onehot) * onehot, axis=1)
     width = -(-capacity // size_z) * size_z
-    slot = (dest * width + rank)[None, :]
+    dest = pair_dest.reshape(1, pair_count)
     cell = pair_cell[None, :]
     coef = pair_coef[None, :]
     solid = pair_solid.astype(jnp.float32)[None, :]
     flat = (size_x * size_y, size_z)
-    temp_at, outgoing = local_call(
-        send_kernel, ((1, pair_count), (groups, 3, width)), fluid_temp.reshape(flat), cell, slot, coef, solid
+    temp_at, outgoing, slot = local_call(
+        send_kernel,
+        (((1, pair_count), jnp.float32), ((groups, 3, width), jnp.float32), ((1, pair_count), jnp.int32)),
+        fluid_temp.reshape(flat), cell, dest, coef, solid,
     )
     solid_temp, wall_flux = run_wall(
         flat, outgoing, solid_source, ambient, conduct, slot, cell, coef, temp_at

time: 84.1 us -> 76.5 us (0.910)
  other arithmetic: 6.46 us -> 1.25 us
  Pallas kernels: 73.2 us -> 70.4 us
    another operation x3 -> x0, other arithmetic: 4.49 us -> none
    pallas_call x1, Pallas kernels: 23 us -> 19.9 us  [run_halo(): pl.pallas_call(functools.partial(halo_kernel, sizes), out_shape=jax.Shape...]
    unnamed x6 -> x4, local copies, waits for them, and re-layouts: 3.05 us -> 3.04 us
where the time goes in v4:
time: 76.5 us; the launch traced here: 76.2 us
  Pallas kernels  70.4 us (92%)
  local copies, waits for them, and re-layouts  3.87 us (5%)
  other arithmetic  1.25 us (2%)
    pallas_call x1, Pallas kernels, run_wall(): pl.pallas_call(functools.partial(wall_kernel, sizes), out_shape=(jax.Shap...  30.5 us
    pallas_call x1, Pallas kernels, run_halo(): pl.pallas_call(functools.partial(halo_kernel, sizes), out_shape=jax.Shape...  19.9 us
    pallas_call x1, Pallas kernels, run_fluid(): pl.pallas_call(fluid_kernel, out_shape=(jax.ShapeDtypeStruct(shape, jnp.f...  16.6 us
    pallas_call x1, Pallas kernels, local_call(): pl.pallas_call(kernel, out_shape=tuple((jax.ShapeDtypeStruct(*o) for o in...  3.4 us
    unnamed x4, local copies, waits for them, and re-layouts  3.04 us

profile of v4, /device:TPU:0, one launch (start us, length us, event | category | flops | bytes accessed | tf_op | source)
XLA Modules:
  0.0 76.2 jit_solution(844641105973551415)
XLA Ops:
  0.6 0.7 fusion
  1.3 0.1 broadcast_in_dim.17
  1.4 0.1 convert_element_type.12
  1.4 0.7 broadcast_in_dim.18.fine
  2.1 0.0 copy-start
  2.1 19.9 %halo.1.fields = f32[6,20,24,256]{3,2,1,0:T(8,128)} custom-call(f32[16,16,128]{2,1,0:T(8,128)} %density.1, f32[3,16,16,128]{3,2,1,0:T(8,128)} %velocity.1, f32[16,16,128]{2,1,0:T(8,128)} %temper.1, f32[16,16,128]{2,1,0:T(8,128)} %broadcast_in_dim.18.fine), custom_call_target="tpu_custom_call" | custom-call | tf_op jit(solution)/shard_map/halo/pallas_call | solution.py:162
  22.1 16.6 %fluid.1 = (f32[16,16,128]{2,1,0:T(8,128)}, f32[3,16,16,128]{3,2,1,0:T(8,128)}) custom-call(f32[6,20,24,256]{3,2,1,0:T(8,128)} %halo.1.fields), custom_call_target="tpu_custom_call" | custom-call | tf_op jit(solution)/shard_map/fluid/pallas_call | solution.py:292
  38.7 0.0 copy-done
  38.7 0.6 convert_element_type.13
  39.3 3.4 %send_kernel.1 = (f32[1,1024]{1,0:T(1,128)}, f32[8,3,256]{2,1,0:T(4,128)}, s32[1,1024]{1,0:T(1,128)}) custom-call(f32[256,128]{1,0:T(8,128)} %bitcast.8, s32[1,1024]{1,0:T(1,128)} %bitcast.10, s32[1,1024]{1,0:T(1,128)} %bitcast.15, f32[1,1024]{1,0:T(1,128)} %bitcast.12, f32[1,1024]{1,0:T(1,128)} %bitcast.14), custom_call_target="tpu_custom_call" | custom-call | tf_op jit(solution)/shard_map/send_kernel/pallas_call | solution.py:365
  42.7 30.5 %wall.1 = (f32[8,16,128]{2,1,0:T(8,128)}, f32[256,128]{1,0:T(8,128)}) custom-call(f32[8,3,256]{2,1,0:T(4,128)} %get-tuple-element.13.outgoing, f32[8,16,128]{2,1,0:T(8,128)} %source.1, f32[8,16,128]{2,1,0:T(8,128)} %ambient.1, f32[8,16,128]{2,1,0:T(8,128)} %conduct.1, s32[1,1024]{1,0:T(1,128)} %get-tuple-element.14.slot, s32[1,1024]{1,0:T(1,128)} %bitcast.11, ...), custom_call_target="tpu_custom_call" | custom-call | tf_op jit(solution)/shard_map/wall/pallas_call | solution.py:556
  73.1 1.5 %copy.17 = f32[8,16,128]{2,1,0:T(8,128)} copy(f32[8,16,128]{2,1,0:T(8,128)} %get-tuple-element.24) | data formatting | bytes 131072
  74.6 1.6 %copy.18 = f32[16,16,128]{2,1,0:T(8,128)} copy(f32[16,16,128]{2,1,0:T(8,128)} %bitcast.9) | data formatting | bytes 262144
Async XLA Ops:
  2.1 36.6 %copy-start = (s32[1024]{0:T(1024)S(1)}, s32[1024]{0:T(1024)}, u32[]{:S(2)}) copy-start(s32[1024]{0:T(1024)} %param.20) | copy-start | bytes 12292

commit v5 on v4

--- a/solution.py
+++ b/solution.py
@@ -354,7 +354,7 @@
         ranks.append(jnp.sum(ahead * here, axis=0, keepdims=True))
         before = before + jnp.sum(here, axis=1, keepdims=True)
     slot[...] = dest[...] * width + jnp.concatenate(ranks, axis=1).astype(jnp.int32)
-    filled = put([got, coef[...], solid[...]], slot[...], groups, width)
+    filled = put([got, coef[...], solid[...].astype(jnp.float32)], slot[...], groups, width)
     for which in range(kinds):
         for group in range(groups):
             outgoing[group, which : which + 1, :] = filled[which][group : group + 1, :]
@@ -372,7 +372,7 @@
 
 
 def wall_kernel(
-    sizes, outgoing, source, ambient, conduct, slot, cell, coef, temp_at, solid_out, flux_out,
+    sizes, outgoing, source, ambient, conduct, solid_out, returned_out,
     arrived, back, returned, residual, image, face_y, face_z, got_x, got_y, got_z, part, whole, held_x, held_g,
     own_sem, pair_send, pair_recv, back_send, back_recv, face_send, face_recv, x_send, x_recv, g_send, g_recv,
 ):
@@ -419,12 +419,6 @@
     z_last = (my_x, my_y, lax.rem(my_z + count_z - 1, count_z))
 
     def send_faces(which, field):
-        value = field[...]
-        face_y[which, 0] = value[:, 0, :]
-        face_y[which, 1] = value[:, size_y - 1, :]
-        turned = jnp.transpose(value.reshape(size_x * size_y, size_z))
-        face_z[which, 0] = turned[0:8]
-        face_z[which, 1] = turned[size_z - 8 : size_z]
         plan = (
             (field.at[size_x - 1], got_x.at[which, 0], row(1)),
             (field.at[0], got_x.at[which, 1], row(count_x - 1)),
@@ -437,7 +431,15 @@
             remote(src, dst, face_send.at[which, at], face_recv.at[which, at], device)
             for at, (src, dst, device) in enumerate(plan)
         ]
-        for copy in copies:
+        copies[0].start()
+        copies[1].start()
+        value = field[...]
+        face_y[which, 0] = value[:, 0, :]
+        face_y[which, 1] = value[:, size_y - 1, :]
+        turned = jnp.transpose(value.reshape(size_x * size_y, size_z))
+        face_z[which, 0] = turned[0:8]
+        face_z[which, 1] = turned[size_z - 8 : size_z]
+        for copy in copies[2:]:
             copy.start()
         return copies
 
@@ -460,6 +462,15 @@
         return (above_x, below_x, above_y, below_y, above_z, below_z)
 
     conduct_copies = send_faces(0, conduct)
+    own.wait()
+    for copy in pairs:
+        copy.wait()
+    landed = jnp.concatenate([arrived[step] for step in range(groups)], axis=1)
+    solid_cell = (landed[2:3, :] + 0.5).astype(jnp.int32)
+    gain, inflow = put([landed[1:2, :], landed[1:2, :] * landed[0:1, :]], solid_cell, size_x * size_y, size_z)
+    residual[...] = source[...] + inflow.reshape(source.shape)
+    residual_copies = send_faces(1, residual)
+    diagonal = ambient[...] + gain.reshape(source.shape)
     conducts = around(0, conduct, conduct_copies)
     at_x, at_y, at_z = (lax.broadcasted_iota(jnp.int32, source.shape, dim) for dim in range(3))
     place_x, place_y, place_z = at_x + my_x * size_x, at_y + my_y * size_y, at_z + my_z * size_z
@@ -471,15 +482,6 @@
     here = conduct[...]
     weights = [jnp.where(ok, 2.0 * here * other / (here + other), 0.0) for ok, other in zip(inside, conducts)]
 
-    own.wait()
-    for copy in pairs:
-        copy.wait()
-    landed = jnp.concatenate([arrived[step] for step in range(groups)], axis=1)
-    solid_cell = (landed[2:3, :] + 0.5).astype(jnp.int32)
-    gain, inflow = put([landed[1:2, :], landed[1:2, :] * landed[0:1, :]], solid_cell, size_x * size_y, size_z)
-    residual[...] = source[...] + inflow.reshape(source.shape)
-    diagonal = ambient[...] + gain.reshape(source.shape)
-
     def operate(which, field, copies):
         value = field[...]
         total = diagonal * value
@@ -487,7 +489,7 @@
             total = total + weight * (value - other)
         return total
 
-    image[...] = operate(1, residual, send_faces(1, residual))
+    image[...] = operate(1, residual, residual_copies)
     twice = operate(2, image, send_faces(2, image))
 
     first, second = residual[...], image[...]
@@ -536,13 +538,18 @@
     own.wait()
     for copy in copies:
         copy.wait()
-    table = jnp.concatenate([returned[group] for group in range(groups)], axis=0)
+    returned_out[...] = returned[...]
+
+
+def flux_kernel(solid, returned, slot, cell, coef, temp_at, solid_out, flux_out):
+    solid_out[...] = solid[...]
+    table = jnp.concatenate([returned[group] for group in range(returned.shape[0])], axis=0)
     flux = coef[...] * (take(table, slot[...]) - temp_at[...])
     rows, lanes = flux_out.shape
     flux_out[...] = put([flux], cell[...], rows, lanes)[0]
 
 
-def run_wall(fluid_flat, outgoing, source, *rest):
+def run_wall(outgoing, source, *rest):
     sizes = tuple(lax.axis_size(axis) for axis in AXES)
     groups, kinds, width = outgoing.shape
     size_x, size_y, size_z = source.shape
@@ -555,7 +562,7 @@
 
     return pl.pallas_call(
         functools.partial(wall_kernel, sizes),
-        out_shape=(jax.ShapeDtypeStruct(source.shape, jnp.float32), jax.ShapeDtypeStruct(fluid_flat, jnp.float32)),
+        out_shape=(jax.ShapeDtypeStruct(source.shape, jnp.float32), jax.ShapeDtypeStruct((groups, 1, width), jnp.float32)),
         in_specs=[block] * (2 + len(rest)),
         out_specs=(block, block),
         scratch_shapes=[
@@ -600,15 +607,18 @@
     dest = pair_dest.reshape(1, pair_count)
     cell = pair_cell[None, :]
     coef = pair_coef[None, :]
-    solid = pair_solid.astype(jnp.float32)[None, :]
+    solid = pair_solid[None, :]
     flat = (size_x * size_y, size_z)
     temp_at, outgoing, slot = local_call(
         send_kernel,
         (((1, pair_count), jnp.float32), ((groups, 3, width), jnp.float32), ((1, pair_count), jnp.int32)),
         fluid_temp.reshape(flat), cell, dest, coef, solid,
     )
-    solid_temp, wall_flux = run_wall(
-        flat, outgoing, solid_source, ambient, conduct, slot, cell, coef, temp_at
+    solid_temp, returned = run_wall(outgoing, solid_source, ambient, conduct)
+    solid_temp, wall_flux = local_call(
+        flux_kernel,
+        ((solid_source.shape, jnp.float32), (flat, jnp.float32)),
+        solid_temp, returned, slot, cell, coef, temp_at,
     )
     return (fluid_temp, fluid_vel, solid_temp, wall_flux.reshape(size_x, size_y, size_z))
 

time: 76.5 us -> 74 us (0.967)
  local copies, waits for them, and re-layouts: 3.87 us -> 0.82 us
  Pallas kernels: 70.4 us -> 71.5 us
    pallas_call x1 -> x2, Pallas kernels: 3.4 us -> 6.81 us  [local_call(): pl.pallas_call(kernel, out_shape=tuple((jax.ShapeDtypeStruct(*o) for o in...]
    unnamed x4 -> x0, local copies, waits for them, and re-layouts: 3.04 us -> none
    pallas_call x1, Pallas kernels: 30.5 us -> 28.2 us  [run_wall(): pl.pallas_call(functools.partial(wall_kernel, sizes), out_shape=(jax.Shap...]
where the time goes in v5:
time: 74 us; the launch traced here: 73.7 us
  Pallas kernels  71.5 us (97%)
  local copies, waits for them, and re-layouts  0.82 us (1%)
    pallas_call x1, Pallas kernels, run_wall(): pl.pallas_call(functools.partial(wall_kernel, sizes), out_shape=(jax.Shap...  28.2 us
    pallas_call x1, Pallas kernels, run_halo(): pl.pallas_call(functools.partial(halo_kernel, sizes), out_shape=jax.Shape...  19.9 us
    pallas_call x1, Pallas kernels, run_fluid(): pl.pallas_call(fluid_kernel, out_shape=(jax.ShapeDtypeStruct(shape, jnp.f...  16.6 us
    pallas_call x2, Pallas kernels, local_call(): pl.pallas_call(kernel, out_shape=tuple((jax.ShapeDtypeStruct(*o) for o in...  6.81 us

profile of v5, /device:TPU:0, one launch (start us, length us, event | category | flops | bytes accessed | tf_op | source)
XLA Modules:
  0.0 73.7 jit_solution(10006804432981874301)
XLA Ops:
  0.6 0.7 fusion
  1.3 0.1 broadcast_in_dim.17
  1.4 0.1 convert_element_type.9
  1.4 0.7 broadcast_in_dim.18.fine
  2.1 19.9 %halo.1.fields = f32[6,20,24,256]{3,2,1,0:T(8,128)} custom-call(f32[16,16,128]{2,1,0:T(8,128)} %density.1, f32[3,16,16,128]{3,2,1,0:T(8,128)} %velocity.1, f32[16,16,128]{2,1,0:T(8,128)} %temper.1, f32[16,16,128]{2,1,0:T(8,128)} %broadcast_in_dim.18.fine), custom_call_target="tpu_custom_call" | custom-call | tf_op jit(solution)/shard_map/halo/pallas_call | solution.py:162
  22.0 16.6 %fluid.1 = (f32[16,16,128]{2,1,0:T(8,128)}, f32[3,16,16,128]{3,2,1,0:T(8,128)}) custom-call(f32[6,20,24,256]{3,2,1,0:T(8,128)} %halo.1.fields), custom_call_target="tpu_custom_call" | custom-call | tf_op jit(solution)/shard_map/fluid/pallas_call | solution.py:292
  38.7 3.4 %send_kernel.1 = (f32[1,1024]{1,0:T(1,128)}, f32[8,3,256]{2,1,0:T(4,128)}, s32[1,1024]{1,0:T(1,128)}) custom-call(f32[256,128]{1,0:T(8,128)} %bitcast.8, s32[1,1024]{1,0:T(1,128)} %bitcast.9, s32[1,1024]{1,0:T(1,128)} %bitcast.13, f32[1,1024]{1,0:T(1,128)} %bitcast.11, s32[1,1024]{1,0:T(1,128)} %bitcast.14), custom_call_target="tpu_custom_call" | custom-call | tf_op jit(solution)/shard_map/send_kernel/pallas_call | solution.py:365
  42.1 28.2 %wall.1 = (f32[8,16,128]{2,1,0:T(8,128)}, f32[8,1,256]{2,1,0:T(1,128)}) custom-call(f32[8,3,256]{2,1,0:T(4,128)} %get-tuple-element.15.outgoing, f32[8,16,128]{2,1,0:T(8,128)} %source.1, f32[8,16,128]{2,1,0:T(8,128)} %ambient.1, f32[8,16,128]{2,1,0:T(8,128)} %conduct.1), custom_call_target="tpu_custom_call" | custom-call | tf_op jit(solution)/shard_map/wall/pallas_call | solution.py:563
  70.3 3.4 %flux_kernel.1 = (f32[8,16,128]{2,1,0:T(8,128)}, f32[256,128]{1,0:T(8,128)}) custom-call(f32[8,16,128]{2,1,0:T(8,128)} %get-tuple-element.16.solid, f32[8,1,256]{2,1,0:T(1,128)} %get-tuple-element.17.returned, s32[1,1024]{1,0:T(1,128)} %get-tuple-element.18.slot, s32[1,1024]{1,0:T(1,128)} %bitcast.10, f32[1,1024]{1,0:T(1,128)} %bitcast.12, ...), custom_call_target="tpu_custom_call" | custom-call | tf_op jit(solution)/shard_map/flux_kernel/pallas_call | solution.py:365

commit v6 on v5

--- a/solution.py
+++ b/solution.py
@@ -325,13 +325,13 @@
 
 
 def put(values, index, rows, lanes):
-    hot = one_hot(index // lanes, rows).astype(jnp.float32)
+    hot = one_hot(index // lanes, rows).astype(jnp.float32).astype(jnp.bfloat16)
     inside = one_hot(index % lanes, lanes).astype(jnp.float32).astype(jnp.bfloat16)
     outs = []
     for value in values:
         total = None
         for part in thirds(value):
-            left = (hot * part.astype(jnp.float32)).astype(jnp.bfloat16)
+            left = hot * part
             term = lax.dot_general(left, inside, (((1,), (1,)), ((), ())), preferred_element_type=jnp.float32)
             total = term if total is None else total + term
         outs.append(total)

time: 74 us -> 73.9 us (level)
  no operation moved by 1% of the time
where the time goes in v6:
time: 73.9 us; the launch traced here: 73.6 us
  Pallas kernels  71.5 us (97%)
  local copies, waits for them, and re-layouts  0.82 us (1%)
    pallas_call x1, Pallas kernels, run_wall(): pl.pallas_call(functools.partial(wall_kernel, sizes), out_shape=(jax.Shap...  28.2 us
    pallas_call x1, Pallas kernels, run_halo(): pl.pallas_call(functools.partial(halo_kernel, sizes), out_shape=jax.Shape...  19.9 us
    pallas_call x1, Pallas kernels, run_fluid(): pl.pallas_call(fluid_kernel, out_shape=(jax.ShapeDtypeStruct(shape, jnp.f...  16.6 us
    pallas_call x2, Pallas kernels, local_call(): pl.pallas_call(kernel, out_shape=tuple((jax.ShapeDtypeStruct(*o) for o in...  6.8 us

profile of v6, /device:TPU:0, one launch (start us, length us, event | category | flops | bytes accessed | tf_op | source)
XLA Modules:
  0.0 73.6 jit_solution(10122824325263287840)
XLA Ops:
  0.6 0.7 fusion
  1.3 0.1 broadcast_in_dim.17
  1.4 0.1 convert_element_type.9
  1.4 0.7 broadcast_in_dim.18.fine
  2.1 19.9 %halo.1.fields = f32[6,20,24,256]{3,2,1,0:T(8,128)} custom-call(f32[16,16,128]{2,1,0:T(8,128)} %density.1, f32[3,16,16,128]{3,2,1,0:T(8,128)} %velocity.1, f32[16,16,128]{2,1,0:T(8,128)} %temper.1, f32[16,16,128]{2,1,0:T(8,128)} %broadcast_in_dim.18.fine), custom_call_target="tpu_custom_call" | custom-call | tf_op jit(solution)/shard_map/halo/pallas_call | solution.py:162
  22.0 16.6 %fluid.1 = (f32[16,16,128]{2,1,0:T(8,128)}, f32[3,16,16,128]{3,2,1,0:T(8,128)}) custom-call(f32[6,20,24,256]{3,2,1,0:T(8,128)} %halo.1.fields), custom_call_target="tpu_custom_call" | custom-call | tf_op jit(solution)/shard_map/fluid/pallas_call | solution.py:292
  38.7 3.4 %send_kernel.1 = (f32[1,1024]{1,0:T(1,128)}, f32[8,3,256]{2,1,0:T(4,128)}, s32[1,1024]{1,0:T(1,128)}) custom-call(f32[256,128]{1,0:T(8,128)} %bitcast.8, s32[1,1024]{1,0:T(1,128)} %bitcast.9, s32[1,1024]{1,0:T(1,128)} %bitcast.13, f32[1,1024]{1,0:T(1,128)} %bitcast.11, s32[1,1024]{1,0:T(1,128)} %bitcast.14), custom_call_target="tpu_custom_call" | custom-call | tf_op jit(solution)/shard_map/send_kernel/pallas_call | solution.py:365
  42.1 28.2 %wall.1 = (f32[8,16,128]{2,1,0:T(8,128)}, f32[8,1,256]{2,1,0:T(1,128)}) custom-call(f32[8,3,256]{2,1,0:T(4,128)} %get-tuple-element.15.outgoing, f32[8,16,128]{2,1,0:T(8,128)} %source.1, f32[8,16,128]{2,1,0:T(8,128)} %ambient.1, f32[8,16,128]{2,1,0:T(8,128)} %conduct.1), custom_call_target="tpu_custom_call" | custom-call | tf_op jit(solution)/shard_map/wall/pallas_call | solution.py:563
  70.3 3.4 %flux_kernel.1 = (f32[8,16,128]{2,1,0:T(8,128)}, f32[256,128]{1,0:T(8,128)}) custom-call(f32[8,16,128]{2,1,0:T(8,128)} %get-tuple-element.16.solid, f32[8,1,256]{2,1,0:T(1,128)} %get-tuple-element.17.returned, s32[1,1024]{1,0:T(1,128)} %get-tuple-element.18.slot, s32[1,1024]{1,0:T(1,128)} %bitcast.10, f32[1,1024]{1,0:T(1,128)} %bitcast.12, ...), custom_call_target="tpu_custom_call" | custom-call | tf_op jit(solution)/shard_map/flux_kernel/pallas_call | solution.py:365
